TPU v7x, 128 devices: a whole 4x4x4 slice. The times are simulated.
128 devices in a mesh: shot: 16 (over z, x), sub: 8 (over y, core).
Axes of the slice: x: 4, y: 4, z: 4, core: 2. Of those that a mesh axis runs over, the one named last changes fastest.
Arguments:
- stiffness: float32 [128, 32, 384], P('sub'), may hold values from 0.04 to 0.15
- buoyancy_first: float32 [128, 32, 384], P('sub'), may hold values from 0.6 to 1.3
- buoyancy_second: float32 [128, 32, 384], P('sub'), may hold values from 0.6 to 1.3
- buoyancy_third: float32 [128, 32, 384], P('sub'), may hold values from 0.6 to 1.3
- adjoint_before: float32 [16, 128, 32, 384], P('shot', 'sub'), may hold values from -6 to 6
- adjoint_current: float32 [16, 128, 32, 384], P('shot', 'sub'), may hold values from -6 to 6
- forward_field: bfloat16 [16, 8, 128, 32, 384], P('shot', None, 'sub'), may hold values from -6 to 6
- traces: float32 [65536, 256], P(('shot', 'sub')), may hold values from -6 to 6
- receiver_target: int32 [65536, 1], P(('shot', 'sub')), may hold values from 0 to 127; in each aligned block of 512 rows (0 to 511, 512 to 1023, ...) at most 6 rows name the same one
- receiver_cell: int32 [65536], P(('shot', 'sub')), may hold values from 0 to 196607
- source_cell: int32 [16, 3], P('shot'), may hold values from 0 to 31
Outputs:
- gradient: float32 [128, 12288], P('sub', 'shot')
- adjoint_earlier: float32 [16, 128, 32, 384], P('shot', 'sub')
- adjoint_latest: float32 [16, 128, 32, 384], P('shot', 'sub')
Inputs may be any that keep to these rules, and one draw needn't show every extreme that they name: `receiver_target`: at most 6 of the receivers stored on one device share a value, and 6 is reached. `receiver_cell`: flattened with the first dimension slowest.
All inputs are finite; a program needn't handle non-finite values.
Results may differ from a plain program's by a relative error of at most 0.0003.
Values sent between devices are 32-bit elements; how exact they have to be, the bound alone decides.
No kernel may reach another device: no remote copies, remote signals or barrier semaphores. Data moves between devices by JAX's collectives and lax.ppermute only.
A program may use at most 128 MiB of HBM per device.

v0:
```python
import jax
import jax.numpy as jnp
from jax import lax
from jax.sharding import PartitionSpec as P

MUTE = 6


COEFFS = (1225.0 / 1024.0, -245.0 / 3072.0, 49.0 / 5120.0, -5.0 / 7168.0)
DAMP = 0.1


def padded(cells, sides, width):
    for axis, dim in sides:
        count = lax.axis_size(axis)
        ends = count - 1
        head = lax.slice_in_dim(cells, 0, width, axis=dim)
        tail = lax.slice_in_dim(cells, cells.shape[dim] - width, cells.shape[dim], axis=dim)
        cells = jnp.concatenate(
            [
                lax.ppermute(tail, axis, [(i, (i + 1) % count) for i in range(ends)]),
                cells,
                lax.ppermute(head, axis, [((i + 1) % count, i) for i in range(ends)]),
            ],
            axis=dim,
        )
    return cells


def take_slice(extended, dimension, offset, length):
    return lax.slice_in_dim(extended, offset, offset + length, axis=dimension)


def forward_difference(extended, dimension, offset, length):
    summed = COEFFS[0] * (
        take_slice(extended, dimension, offset + 1, length)
        - take_slice(extended, dimension, offset, length)
    )
    for order in range(2, 5):
        summed = summed + COEFFS[order - 1] * (
            take_slice(extended, dimension, offset + order, length)
            - take_slice(extended, dimension, offset + 1 - order, length)
        )
    return summed


def backward_difference(extended, dimension, offset, length):
    summed = COEFFS[0] * (
        take_slice(extended, dimension, offset, length)
        - take_slice(extended, dimension, offset - 1, length)
    )
    for order in range(2, 5):
        summed = summed + COEFFS[order - 1] * (
            take_slice(extended, dimension, offset + order - 1, length)
            - take_slice(extended, dimension, offset - order, length)
        )
    return summed


def pad_along(wave_field, dimension, amount):
    widths = [(0, 0)] * wave_field.ndim
    widths[dimension] = (amount, amount)
    return jnp.pad(wave_field, widths)


def local_divergence(wave_field, buoyancy, dimension):
    length = wave_field.shape[dimension]
    flux_field = buoyancy * forward_difference(
        pad_along(wave_field, dimension, 4), dimension, 4, length
    )
    return backward_difference(pad_along(flux_field, dimension, 4), dimension, 4, length)


def trace_kernel(sample_count, step_count):
    sample_pos = jnp.arange(sample_count, dtype=jnp.float32)[:, None]
    centers = (jnp.arange(step_count, dtype=jnp.float32)[None, :] + 0.5) * (
        sample_count / step_count
    )
    return 0.25 * jnp.exp(-jnp.abs(sample_pos - centers) / (sample_count / 8.0))


def first_divergence(current, buoyancy_first):
    slab_depth = current.shape[0]
    extended = padded(current, (("sub", 0),), 4)
    flux_field = buoyancy_first * forward_difference(extended, 0, 4, slab_depth)
    flux_wide = padded(flux_field, (("sub", 0),), 4)
    return backward_difference(flux_wide, 0, 4, slab_depth)


def local(
    stiffness,
    buoyancy_first,
    buoyancy_second,
    buoyancy_third,
    adjoint_before,
    adjoint_current,
    forward_field,
    traces,
    receiver_target,
    receiver_cell,
    source_cell,
):
    device_count = lax.axis_size(("shot", "sub"))
    sample_count = traces.shape[1]
    step_count = forward_field.shape[1]
    slab_depth = stiffness.shape[0]
    row_count = traces.shape[0]
    capacity = max(2, (3 * row_count + 2 * device_count - 1) // (2 * device_count))
    kernel = trace_kernel(sample_count, step_count)
    target = receiver_target[:, 0]
    onehot = target[:, None] == jnp.arange(device_count, dtype=jnp.int32)[None, :]
    row_ids = jnp.arange(row_count, dtype=jnp.int32)
    lower = (row_ids[:, None] >= row_ids[None, :]).astype(jnp.bfloat16)
    running = jnp.dot(lower, onehot.astype(jnp.bfloat16), preferred_element_type=jnp.float32)
    slot_index = (jnp.sum(jnp.where(onehot, running, jnp.float32(0.0)), axis=1) - 1.0).astype(
        jnp.int32
    )
    place_buffer = (
        jnp.zeros((device_count, capacity), jnp.float32)
        .at[target, slot_index]
        .set(receiver_cell.astype(jnp.float32))
    )
    row_buffer = (
        jnp.zeros((device_count, capacity, sample_count), jnp.float32)
        .at[target, slot_index]
        .set(traces)
    )
    got_rows, got_places = (
        lax.all_to_all(row_buffer, ("shot", "sub"), split_axis=0, concat_axis=0, tiled=True),
        lax.all_to_all(place_buffer, ("shot", "sub"), split_axis=0, concat_axis=0, tiled=True),
    )
    received = jnp.dot(
        got_rows.reshape(-1, sample_count),
        kernel,
        precision=lax.Precision.HIGHEST,
        preferred_element_type=jnp.float32,
    )
    place_index = got_places.reshape(-1).astype(jnp.int32)
    step_values = received.T
    earlier = adjoint_before[0]
    current = adjoint_current[0]
    forward_now = forward_field[0]
    image_sum = jnp.zeros(current.shape, jnp.float32)
    illumination = jnp.zeros(current.shape, jnp.float32)
    for moment in range(step_count):
        divergence = first_divergence(current, buoyancy_first)
        divergence = divergence + local_divergence(current, buoyancy_second, 1)
        divergence = divergence + local_divergence(current, buoyancy_third, 2)
        change = (
            (stiffness * divergence)
            .reshape(-1)
            .at[place_index]
            .add(step_values[moment])
            .reshape(current.shape)
        )
        following = 2.0 * current - earlier + change
        frame = forward_now[moment].astype(jnp.float32)
        image_sum = image_sum + frame * change
        illumination = illumination + frame * frame
        earlier, current = (current, following)
    source_pos = source_cell[0].astype(jnp.float32)
    coord_first = (
        lax.axis_index("sub") * slab_depth + jnp.arange(slab_depth, dtype=jnp.int32)
    ).astype(jnp.float32)[:, None, None]
    coord_second = jnp.arange(current.shape[1], dtype=jnp.float32)[None, :, None]
    coord_third = jnp.arange(current.shape[2], dtype=jnp.float32)[None, None, :]
    distance = (
        (coord_first - source_pos[0]) ** 2
        + (coord_second - source_pos[1]) ** 2
        + (coord_third - source_pos[2]) ** 2
    )
    mute_weight = 1.0 - jnp.exp(-distance / (2.0 * MUTE * MUTE))
    muted_image = (mute_weight * image_sum).reshape(slab_depth, -1)
    flat_light = illumination.reshape(slab_depth, -1)
    summed_image, summed_light = (
        lax.psum_scatter(muted_image, "shot", scatter_dimension=1, tiled=True),
        lax.psum_scatter(flat_light, "shot", scatter_dimension=1, tiled=True),
    )
    gradient = summed_image / (summed_light / (step_count * lax.axis_size("shot")) + DAMP)
    return (gradient, earlier[None], current[None])


def solution(mesh):
    placed = (
        P("sub", None, None),
        P("sub", None, None),
        P("sub", None, None),
        P("sub", None, None),
        P("shot", "sub", None, None),
        P("shot", "sub", None, None),
        P("shot", None, "sub", None, None),
        P(("shot", "sub"), None),
        P(("shot", "sub"), None),
        P(("shot", "sub")),
        P("shot", None),
    )
    return jax.shard_map(
        local,
        mesh=mesh,
        in_specs=placed,
        out_specs=(P("sub", "shot"), P("shot", "sub", None, None), P("shot", "sub", None, None)),
        check_vma=False,
    )
```

profile of v0, /device:TPU:0, one launch (start us, length us, event | category | flops | bytes accessed | tf_op | source)
XLA Modules:
  0.0 626.8 jit_solution(1363181937884609092)
XLA Ops:
  15.9 22.0 %scatter_fusion = f32[128,6]{0,1:T(8,128)S(1)} fusion(f32[128,6]{0,1:T(8,128)S(1)} %broadcast_in_dim.7, s32[512]{0:T(512)S(1)} %bitcast.46, f32[512]{0:T(512)S(1)} %convert_element_type.146), kind=kCustom, calls=%fused_computation | custom fusion | bytes 10240 | tf_op jit(solution)/shard_map/scatter | solution.py:121
  38.6 11.8 %all-to-all-start = ((f32[128,1,6]{2,1,0:T(1,128)}), f32[128,1,6]{2,1,0:T(1,128)S(1)}, u32[]{:S(2)}, u32[]{:S(2)}) async-start(f32[128,1,6]{2,1,0:T(1,128)} %copy.18), calls=%async_computation | async-start | bytes 131072 | tf_op jit(solution)/shard_map/all_to_all | solution.py:130
  51.4 56.6 %scatter_fusion.1 = f32[128,6,256]{2,0,1:T(8,128)} fusion(f32[128,6,256]{2,0,1:T(8,128)} %broadcast_in_dim.10, s32[512]{0:T(512)S(1)} %bitcast.47, f32[512,256]{1,0:T(8,128)S(1)} %copy-done.49), kind=kCustom, calls=%fused_computation.1 | custom fusion | bytes 1576960 | tf_op jit(solution)/shard_map/scatter | solution.py:126
  111.4 12.5 %fusion.446 = (f32[16,32,384]{2,1,0:T(8,128)}, f32[16,32,384]{2,1,0:T(8,128)S(1)}, f32[16,32,384]{2,1,0:T(8,128)}) fusion(f32[16,32,384]{2,1,0:T(8,128)S(1)} %copy-done.4, f32[16,32,384]{2,1,0:T(8,128)} %bitcast.48, f32[16,32,384]{2,1,0:T(8,128)S(1)} %copy-done.9, f32[4,32,384]{2,1,0:T(8,128)} %copy-done.50, f32[4,32,384]{2,1,0:T(8,128)S(1)} %collective-permute-done, ...), kind=kLoop, calls=%fused_computation.842 | loop fusion | flops 8454144 | bytes 5898240 | tf_op jit(solution)/shard_map/mul | solution.py:68
  128.2 13.2 %all-to-all-start.1 = ((f32[128,6,256]{2,1,0:T(8,128)}), f32[128,6,256]{2,1,0:T(8,128)}, u32[]{:S(2)}, u32[]{:S(2)}) async-start(f32[128,6,256]{2,1,0:T(8,128)} %copy.19), calls=%async_computation.1 | async-start | bytes 2097152 | tf_op jit(solution)/shard_map/all_to_all | solution.py:129
  141.9 11.1 %fusion.162 = f32[16,32,384]{2,1,0:T(8,128)} fusion(f32[16,32,384]{2,1,0:T(8,128)S(1)} %copy-done.22, f32[16,32,384]{2,1,0:T(8,128)} %copy-done.37, f32[16,32,384]{2,1,0:T(8,128)} %get-tuple-element.78, f32[4,32,384]{2,1,0:T(8,128)} %collective-permute-done.3, f32[16,32,384]{2,1,0:T(8,128)} %get-tuple-element.76, f32[4,32,384]{2,1,0:T(8,128)S(1)} %collective-permute-done.2), kind=kLoop, calls=%fused_computation.558 | loop fusion | flops 8454144 | bytes 4325376 | tf_op jit(solution)/shard_map/mul | solution.py:150
  154.2 6.0 all-to-all-done.1
  203.5 6.8 %collective-permute-start.9 = (f32[4,32,384]{2,1,0:T(8,128)S(1)}, f32[4,32,384]{2,1,0:T(8,128)S(1)}, u32[]{:S(2)}, u32[]{:S(2)}) collective-permute-start(f32[4,32,384]{2,1,0:T(8,128)S(1)} %get-tuple-element.66), channel_id=1, source_target_pairs={{0,1},{1,2},{2,3},{3,4},{4,5},{5,6},{6,7},{8,9},{9,10},{10,11},{11... | collective-permute-start | bytes 589832 | tf_op jit(solution)/shard_map/ppermute | solution.py:21
  238.2 6.8 %collective-permute-start.13 = (f32[4,32,384]{2,1,0:T(8,128)S(1)}, f32[4,32,384]{2,1,0:T(8,128)S(1)}, u32[]{:S(2)}, u32[]{:S(2)}) collective-permute-start(f32[4,32,384]{2,1,0:T(8,128)S(1)} %get-tuple-element.59), channel_id=1, source_target_pairs={{0,1},{1,2},{2,3},{3,4},{4,5},{5,6},{6,7},{8,9},{9,10},{10,11},{11... | collective-permute-start | bytes 589832 | tf_op jit(solution)/shard_map/ppermute | solution.py:21
  263.7 5.2 scatter_fusion.5
  273.3 6.8 %collective-permute-start.17 = (f32[4,32,384]{2,1,0:T(8,128)S(1)}, f32[4,32,384]{2,1,0:T(8,128)S(1)}, u32[]{:S(2)}, u32[]{:S(2)}) collective-permute-start(f32[4,32,384]{2,1,0:T(8,128)S(1)} %get-tuple-element.52), channel_id=1, source_target_pairs={{0,1},{1,2},{2,3},{3,4},{4,5},{5,6},{6,7},{8,9},{9,10},{10,11},{11... | collective-permute-start | bytes 589832 | tf_op jit(solution)/shard_map/ppermute | solution.py:21
  299.6 6.3 scatter_fusion.6
  311.4 6.8 %collective-permute-start.21 = (f32[4,32,384]{2,1,0:T(8,128)S(1)}, f32[4,32,384]{2,1,0:T(8,128)S(1)}, u32[]{:S(2)}, u32[]{:S(2)}) collective-permute-start(f32[4,32,384]{2,1,0:T(8,128)S(1)} %get-tuple-element.45), channel_id=1, source_target_pairs={{0,1},{1,2},{2,3},{3,4},{4,5},{5,6},{6,7},{8,9},{9,10},{10,11},{11... | collective-permute-start | bytes 589832 | tf_op jit(solution)/shard_map/ppermute | solution.py:21
  321.9 5.2 collective-permute-start.22
  337.8 6.2 scatter_fusion.7
  349.5 7.4 %collective-permute-start.25 = (f32[4,32,384]{2,1,0:T(8,128)S(1)}, f32[4,32,384]{2,1,0:T(8,128)S(1)}, u32[]{:S(2)}, u32[]{:S(2)}) collective-permute-start(f32[4,32,384]{2,1,0:T(8,128)S(1)} %get-tuple-element.38), channel_id=1, source_target_pairs={{0,1},{1,2},{2,3},{3,4},{4,5},{5,6},{6,7},{8,9},{9,10},{10,11},{11... | collective-permute-start | bytes 589832 | tf_op jit(solution)/shard_map/ppermute | solution.py:21
  372.5 10.8 %fusion.30 = f32[16,32,384]{2,1,0:T(8,128)} fusion(f32[16,32,384]{2,1,0:T(8,128)} %param.11, f32[16,32,384]{2,1,0:T(8,128)} %copy-done.36, f32[16,32,384]{2,1,0:T(8,128)} %get-tuple-element.35, f32[4,32,384]{2,1,0:T(8,128)S(1)} %collective-permute-done.27, f32[16,32,384]{2,1,0:T(8,128)} %get-tuple-element.34, f32[4,32,384]{2,1,0:T(8,128)S(1)} %collective-permute-done.26), kind=kLoop, calls=%fused_computation.426 | loop fusion | flops 8454144 | bytes 4325376 | tf_op jit(solution)/shard_map/mul | solution.py:150
  385.4 6.2 scatter_fusion.8
  397.1 6.7 %collective-permute-start.29 = (f32[4,32,384]{2,1,0:T(8,128)S(1)}, f32[4,32,384]{2,1,0:T(8,128)S(1)}, u32[]{:S(2)}, u32[]{:S(2)}) collective-permute-start(f32[4,32,384]{2,1,0:T(8,128)S(1)} %get-tuple-element.31), channel_id=1, source_target_pairs={{0,1},{1,2},{2,3},{3,4},{4,5},{5,6},{6,7},{8,9},{9,10},{10,11},{11... | collective-permute-start | bytes 589832 | tf_op jit(solution)/shard_map/ppermute | solution.py:21
  442.0 10.9 %fusion.8 = f32[16,32,384]{2,1,0:T(8,128)} fusion(f32[16,32,384]{2,1,0:T(8,128)} %param.11, f32[16,32,384]{2,1,0:T(8,128)} %copy-done.35, f32[16,32,384]{2,1,0:T(8,128)} %get-tuple-element.29, f32[4,32,384]{2,1,0:T(8,128)S(1)} %collective-permute-done.31, f32[16,32,384]{2,1,0:T(8,128)} %get-tuple-element.27, f32[4,32,384]{2,1,0:T(8,128)S(1)} %collective-permute-done.30), kind=kLoop, calls=%fused_computation.404 | loop fusion | flops 8454144 | bytes 4325376 | tf_op jit(solution)/shard_map/mul | solution.py:150
  455.0 6.2 scatter_fusion.9
  463.4 6.9 %multiply_add_fusion = (f32[16,12288]{1,0:T(8,128)}, f32[16,12288]{1,0:T(8,128)}) fusion(f32[16,12288]{1,0:T(8,128)} %bitcast.56, f32[16,12288]{1,0:T(8,128)} %bitcast.55, f32[16,12288]{1,0:T(8,128)} %bitcast.54, f32[16,12288]{1,0:T(8,128)} %bitcast.53, f32[16,12288]{1,0:T(8,128)} %bitcast.52, f32[16,12288]{1,0:T(8,128)} %bitcast.51, ...), kind=kLoop, calls=%fused_computation.1095 | loop fusion | flops 6881280 | bytes 14991360 | tf_op jit(solution)/shard_map/add | solution.py:159
  486.0 57.1 %reduce-scatter.3.cloned.1.call-done = f32[16,768]{1,0:T(8,128)} async-done(((f32[16,12288]{1,0:T(8,128)}), f32[16,768]{1,0:T(8,128)}) %reduce-scatter.3.cloned.1.call-update) | async-done | bytes 49168 | tf_op jit(solution)/shard_map/reduce_scatter | solution.py:176
  543.1 75.2 %reduce-scatter.5.cloned.1.call-done = f32[16,768]{1,0:T(8,128)} async-done(((f32[16,12288]{1,0:T(8,128)}), f32[16,768]{1,0:T(8,128)}) %reduce-scatter.5.cloned.1.call-update) | async-done | bytes 49168 | tf_op jit(solution)/shard_map/reduce_scatter | solution.py:177
  (274 shorter events, 240.8 us)
Async XLA Ops:
  9.0 101.7 %collective-permute-start = (f32[4,32,384]{2,1,0:T(8,128)}, f32[4,32,384]{2,1,0:T(8,128)S(1)}, u32[]{:S(2)}, u32[]{:S(2)}) collective-permute-start(f32[4,32,384]{2,1,0:T(8,128)} %get-tuple-element.79), channel_id=1, source_target_pairs={{1,0},{2,1},{3,2},{4,3},{5,4},{6,5},{7,6},{9,8},{10,9},{11,10},{12... | collective-permute-start | bytes 589832 | tf_op jit(solution)/shard_map/ppermute | solution.py:23
  10.4 100.3 %collective-permute-start.1 = (f32[4,32,384]{2,1,0:T(8,128)}, f32[4,32,384]{2,1,0:T(8,128)S(1)}, u32[]{:S(2)}, u32[]{:S(2)}) collective-permute-start(f32[4,32,384]{2,1,0:T(8,128)} %get-tuple-element.80), channel_id=1, source_target_pairs={{0,1},{1,2},{2,3},{3,4},{4,5},{5,6},{6,7},{8,9},{9,10},{10,11},{11... | collective-permute-start | bytes 589832 | tf_op jit(solution)/shard_map/ppermute | solution.py:21
  38.6 89.6 %all-to-all-start = ((f32[128,1,6]{2,1,0:T(1,128)}), f32[128,1,6]{2,1,0:T(1,128)S(1)}, u32[]{:S(2)}, u32[]{:S(2)}) async-start(f32[128,1,6]{2,1,0:T(1,128)} %copy.18), calls=%async_computation | async-start | bytes 131072 | tf_op jit(solution)/shard_map/all_to_all | solution.py:130
  125.6 16.3 %collective-permute-start.2 = (f32[4,32,384]{2,1,0:T(8,128)}, f32[4,32,384]{2,1,0:T(8,128)S(1)}, u32[]{:S(2)}, u32[]{:S(2)}) collective-permute-start(f32[4,32,384]{2,1,0:T(8,128)} %get-tuple-element.74), channel_id=1, source_target_pairs={{0,1},{1,2},{2,3},{3,4},{4,5},{5,6},{6,7},{8,9},{9,10},{10,11},{11... | collective-permute-start | bytes 589832 | tf_op jit(solution)/shard_map/ppermute | solution.py:21
  126.9 15.0 %collective-permute-start.3 = (f32[4,32,384]{2,1,0:T(8,128)}, f32[4,32,384]{2,1,0:T(8,128)}, u32[]{:S(2)}, u32[]{:S(2)}) collective-permute-start(f32[4,32,384]{2,1,0:T(8,128)} %get-tuple-element.75), channel_id=1, source_target_pairs={{1,0},{2,1},{3,2},{4,3},{5,4},{6,5},{7,6},{9,8},{10,9},{11,10},{12... | collective-permute-start | bytes 589832 | tf_op jit(solution)/shard_map/ppermute | solution.py:23
  128.2 31.9 %all-to-all-start.1 = ((f32[128,6,256]{2,1,0:T(8,128)}), f32[128,6,256]{2,1,0:T(8,128)}, u32[]{:S(2)}, u32[]{:S(2)}) async-start(f32[128,6,256]{2,1,0:T(8,128)} %copy.19), calls=%async_computation.1 | async-start | bytes 2097152 | tf_op jit(solution)/shard_map/all_to_all | solution.py:129
  141.5 401.6 %reduce-scatter.3.cloned.1.call-start = ((), (), s32[]{:S(2)}) async-start(), calls=%async_computation.4 | async-start | bytes 835584 | tf_op jit(solution)/shard_map/reduce_scatter | solution.py:176
  202.2 8.1 %collective-permute-start.8 = (f32[4,32,384]{2,1,0:T(8,128)S(1)}, f32[4,32,384]{2,1,0:T(8,128)S(1)}, u32[]{:S(2)}, u32[]{:S(2)}) collective-permute-start(f32[4,32,384]{2,1,0:T(8,128)S(1)} %get-tuple-element.65), channel_id=1, source_target_pairs={{1,0},{2,1},{3,2},{4,3},{5,4},{6,5},{7,6},{9,8},{10,9},{11,10},{12... | collective-permute-start | bytes 589832 | tf_op jit(solution)/shard_map/ppermute | solution.py:23
  203.5 7.9 %collective-permute-start.9 = (f32[4,32,384]{2,1,0:T(8,128)S(1)}, f32[4,32,384]{2,1,0:T(8,128)S(1)}, u32[]{:S(2)}, u32[]{:S(2)}) collective-permute-start(f32[4,32,384]{2,1,0:T(8,128)S(1)} %get-tuple-element.66), channel_id=1, source_target_pairs={{0,1},{1,2},{2,3},{3,4},{4,5},{5,6},{6,7},{8,9},{9,10},{10,11},{11... | collective-permute-start | bytes 589832 | tf_op jit(solution)/shard_map/ppermute | solution.py:21
  214.0 6.5 %collective-permute-start.10 = (f32[4,32,384]{2,1,0:T(8,128)S(1)}, f32[4,32,384]{2,1,0:T(8,128)S(1)}, u32[]{:S(2)}, u32[]{:S(2)}) collective-permute-start(f32[4,32,384]{2,1,0:T(8,128)S(1)} %get-tuple-element.60), channel_id=1, source_target_pairs={{0,1},{1,2},{2,3},{3,4},{4,5},{5,6},{6,7},{8,9},{9,10},{10,11},{11... | collective-permute-start | bytes 589832 | tf_op jit(solution)/shard_map/ppermute | solution.py:21
  236.9 8.1 %collective-permute-start.12 = (f32[4,32,384]{2,1,0:T(8,128)S(1)}, f32[4,32,384]{2,1,0:T(8,128)S(1)}, u32[]{:S(2)}, u32[]{:S(2)}) collective-permute-start(f32[4,32,384]{2,1,0:T(8,128)S(1)} %get-tuple-element.58), channel_id=1, source_target_pairs={{1,0},{2,1},{3,2},{4,3},{5,4},{6,5},{7,6},{9,8},{10,9},{11,10},{12... | collective-permute-start | bytes 589832 | tf_op jit(solution)/shard_map/ppermute | solution.py:23
  238.2 7.9 %collective-permute-start.13 = (f32[4,32,384]{2,1,0:T(8,128)S(1)}, f32[4,32,384]{2,1,0:T(8,128)S(1)}, u32[]{:S(2)}, u32[]{:S(2)}) collective-permute-start(f32[4,32,384]{2,1,0:T(8,128)S(1)} %get-tuple-element.59), channel_id=1, source_target_pairs={{0,1},{1,2},{2,3},{3,4},{4,5},{5,6},{6,7},{8,9},{9,10},{10,11},{11... | collective-permute-start | bytes 589832 | tf_op jit(solution)/shard_map/ppermute | solution.py:21
  271.9 8.1 %collective-permute-start.16 = (f32[4,32,384]{2,1,0:T(8,128)S(1)}, f32[4,32,384]{2,1,0:T(8,128)S(1)}, u32[]{:S(2)}, u32[]{:S(2)}) collective-permute-start(f32[4,32,384]{2,1,0:T(8,128)S(1)} %get-tuple-element.51), channel_id=1, source_target_pairs={{1,0},{2,1},{3,2},{4,3},{5,4},{6,5},{7,6},{9,8},{10,9},{11,10},{12... | collective-permute-start | bytes 589832 | tf_op jit(solution)/shard_map/ppermute | solution.py:23
  273.3 7.9 %collective-permute-start.17 = (f32[4,32,384]{2,1,0:T(8,128)S(1)}, f32[4,32,384]{2,1,0:T(8,128)S(1)}, u32[]{:S(2)}, u32[]{:S(2)}) collective-permute-start(f32[4,32,384]{2,1,0:T(8,128)S(1)} %get-tuple-element.52), channel_id=1, source_target_pairs={{0,1},{1,2},{2,3},{3,4},{4,5},{5,6},{6,7},{8,9},{9,10},{10,11},{11... | collective-permute-start | bytes 589832 | tf_op jit(solution)/shard_map/ppermute | solution.py:21
  310.1 8.1 %collective-permute-start.20 = (f32[4,32,384]{2,1,0:T(8,128)S(1)}, f32[4,32,384]{2,1,0:T(8,128)S(1)}, u32[]{:S(2)}, u32[]{:S(2)}) collective-permute-start(f32[4,32,384]{2,1,0:T(8,128)S(1)} %get-tuple-element.44), channel_id=1, source_target_pairs={{1,0},{2,1},{3,2},{4,3},{5,4},{6,5},{7,6},{9,8},{10,9},{11,10},{12... | collective-permute-start | bytes 589832 | tf_op jit(solution)/shard_map/ppermute | solution.py:23
  311.4 7.9 %collective-permute-start.21 = (f32[4,32,384]{2,1,0:T(8,128)S(1)}, f32[4,32,384]{2,1,0:T(8,128)S(1)}, u32[]{:S(2)}, u32[]{:S(2)}) collective-permute-start(f32[4,32,384]{2,1,0:T(8,128)S(1)} %get-tuple-element.45), channel_id=1, source_target_pairs={{0,1},{1,2},{2,3},{3,4},{4,5},{5,6},{6,7},{8,9},{9,10},{10,11},{11... | collective-permute-start | bytes 589832 | tf_op jit(solution)/shard_map/ppermute | solution.py:21
  348.1 8.7 %collective-permute-start.24 = (f32[4,32,384]{2,1,0:T(8,128)S(1)}, f32[4,32,384]{2,1,0:T(8,128)S(1)}, u32[]{:S(2)}, u32[]{:S(2)}) collective-permute-start(f32[4,32,384]{2,1,0:T(8,128)S(1)} %get-tuple-element.37), channel_id=1, source_target_pairs={{1,0},{2,1},{3,2},{4,3},{5,4},{6,5},{7,6},{9,8},{10,9},{11,10},{12... | collective-permute-start | bytes 589832 | tf_op jit(solution)/shard_map/ppermute | solution.py:23
  349.5 8.0 %collective-permute-start.25 = (f32[4,32,384]{2,1,0:T(8,128)S(1)}, f32[4,32,384]{2,1,0:T(8,128)S(1)}, u32[]{:S(2)}, u32[]{:S(2)}) collective-permute-start(f32[4,32,384]{2,1,0:T(8,128)S(1)} %get-tuple-element.38), channel_id=1, source_target_pairs={{0,1},{1,2},{2,3},{3,4},{4,5},{5,6},{6,7},{8,9},{9,10},{10,11},{11... | collective-permute-start | bytes 589832 | tf_op jit(solution)/shard_map/ppermute | solution.py:21
  361.8 9.9 %collective-permute-start.26 = (f32[4,32,384]{2,1,0:T(8,128)}, f32[4,32,384]{2,1,0:T(8,128)S(1)}, u32[]{:S(2)}, u32[]{:S(2)}) collective-permute-start(f32[4,32,384]{2,1,0:T(8,128)} %get-tuple-element.32), channel_id=1, source_target_pairs={{0,1},{1,2},{2,3},{3,4},{4,5},{5,6},{6,7},{8,9},{9,10},{10,11},{11... | collective-permute-start | bytes 589832 | tf_op jit(solution)/shard_map/ppermute | solution.py:21
  395.8 9.2 %collective-permute-start.28 = (f32[4,32,384]{2,1,0:T(8,128)S(1)}, f32[4,32,384]{2,1,0:T(8,128)S(1)}, u32[]{:S(2)}, u32[]{:S(2)}) collective-permute-start(f32[4,32,384]{2,1,0:T(8,128)S(1)} %get-tuple-element.30), channel_id=1, source_target_pairs={{1,0},{2,1},{3,2},{4,3},{5,4},{6,5},{7,6},{9,8},{10,9},{11,10},{12... | collective-permute-start | bytes 589832 | tf_op jit(solution)/shard_map/ppermute | solution.py:23
  397.1 7.9 %collective-permute-start.29 = (f32[4,32,384]{2,1,0:T(8,128)S(1)}, f32[4,32,384]{2,1,0:T(8,128)S(1)}, u32[]{:S(2)}, u32[]{:S(2)}) collective-permute-start(f32[4,32,384]{2,1,0:T(8,128)S(1)} %get-tuple-element.31), channel_id=1, source_target_pairs={{0,1},{1,2},{2,3},{3,4},{4,5},{5,6},{6,7},{8,9},{9,10},{10,11},{11... | collective-permute-start | bytes 589832 | tf_op jit(solution)/shard_map/ppermute | solution.py:21
  409.4 32.6 %collective-permute-start.30 = (f32[4,32,384]{2,1,0:T(8,128)}, f32[4,32,384]{2,1,0:T(8,128)S(1)}, u32[]{:S(2)}, u32[]{:S(2)}) collective-permute-start(f32[4,32,384]{2,1,0:T(8,128)} %get-tuple-element.25), channel_id=1, source_target_pairs={{0,1},{1,2},{2,3},{3,4},{4,5},{5,6},{6,7},{8,9},{9,10},{10,11},{11... | collective-permute-start | bytes 589832 | tf_op jit(solution)/shard_map/ppermute | solution.py:21
  414.5 27.5 %collective-permute-start.31 = (f32[4,32,384]{2,1,0:T(8,128)}, f32[4,32,384]{2,1,0:T(8,128)S(1)}, u32[]{:S(2)}, u32[]{:S(2)}) collective-permute-start(f32[4,32,384]{2,1,0:T(8,128)} %get-tuple-element.26), channel_id=1, source_target_pairs={{1,0},{2,1},{3,2},{4,3},{5,4},{6,5},{7,6},{9,8},{10,9},{11,10},{12... | collective-permute-start | bytes 589832 | tf_op jit(solution)/shard_map/ppermute | solution.py:23
  470.3 147.9 %reduce-scatter.5.cloned.1.call-start = ((), (), s32[]{:S(2)}) async-start(), calls=%async_computation.5 | async-start | bytes 835584 | tf_op jit(solution)/shard_map/reduce_scatter | solution.py:177
  (65 other events, 798.3 us)
Sparse Core Ops, SparseCore 0:
  470.4 72.5 reduce-scatter.2
  546.3 71.9 reduce-scatter.4
where the time goes:
time: 639 us; the launch traced here: 627 us
  waiting for transfers between devices  165 us (26%)
  other arithmetic  161 us (25%)
  local copies, waits for them, and re-layouts  151 us (24%)
  starting transfers between devices  130 us (20%)
  between operations  15.3 us (2%)
    ppermute x16, starting transfers between devices, padded(): lax.ppermute(tail, axis, [(i, (i + 1) % count) for i in range(ends)])  84.1 us
    reduce_scatter x1, waiting for transfers between devices, local(): lax.psum_scatter(flat_light, 'shot', scatter_dimension=1, tiled=True)  75.2 us
    scatter x2, local copies, waits for them, and re-layouts, local(): row_buffer = jnp.zeros((device_count, capacity, sample_count), jnp.float3...  59.3 us
    reduce_scatter x1, waiting for transfers between devices, local(): lax.psum_scatter(muted_image, 'shot', scatter_dimension=1, tiled=True)  57.1 us
    mul x8, other arithmetic, local(): stiffness * divergence  48.9 us
    scatter-add x8, other arithmetic, local(): change = (stiffness * divergence).reshape(-1).at[place_index].add(step_va...  45.2 us
    reshape x31, local copies, waits for them, and re-layouts, local(): change = (stiffness * divergence).reshape(-1).at[place_index].add(step_va...  44.7 us
    mul x8, other arithmetic, local_divergence(): buoyancy * forward_difference(pad_along(wave_field, dimension, 4), dimens...  32.4 us
  transfers between devices with their start and end apart: 36, of which 15 were waited for; matrix products, arithmetic and copies ran while one was open for 25% of the time, Pallas kernels for 0%

commit v1 on v0

v1 whole, which is shorter than its diff:
```python
import jax
import jax.numpy as jnp
import numpy as np
from jax import lax
from jax.experimental import pallas as pl
from jax.experimental.pallas import tpu as pltpu
from jax.sharding import PartitionSpec as P

MUTE = 6
COEFFS = (1225.0 / 1024.0, -245.0 / 3072.0, 49.0 / 5120.0, -5.0 / 7168.0)
DAMP = 0.1
HALO = 7
SLOTS = 6
FIELDS = 16
F32 = jnp.float32
BF16 = jnp.bfloat16
PARAMS = pltpu.CompilerParams(vmem_limit_bytes=48 * 1024 * 1024)


def shape_of(*dims, dtype=F32):
    return jax.ShapeDtypeStruct(dims, dtype)


def split2(x):
    high = x.astype(BF16)
    return high, (x - high.astype(F32)).astype(BF16)


def split3(x):
    high = x.astype(BF16)
    rest = x - high.astype(F32)
    mid = rest.astype(BF16)
    return high, mid, (rest - mid.astype(F32)).astype(BF16)


def pack_kernel(traces_ref, kernel_ref, target_ref, cell_ref, send_ref):
    rows = traces_ref.shape[0]
    values = jnp.dot(
        traces_ref[...],
        kernel_ref[...],
        precision=lax.Precision.HIGHEST,
        preferred_element_type=F32,
    )
    lane = lax.broadcasted_iota(jnp.int32, (rows, 128), 1)
    hit = target_ref[...] == lane
    onehot = jnp.where(hit, 1.0, 0.0)
    lower = (
        lax.broadcasted_iota(jnp.int32, (rows, rows), 0)
        >= lax.broadcasted_iota(jnp.int32, (rows, rows), 1)
    )
    running = jnp.dot(
        jnp.where(lower, 1.0, 0.0).astype(BF16),
        onehot.astype(BF16),
        preferred_element_type=F32,
    )
    slot = jnp.sum(jnp.where(hit, running, 0.0), axis=1, keepdims=True) - 1.0
    slot = slot.astype(jnp.int32)
    entries = jnp.where(lane % FIELDS == 8, cell_ref[...].astype(F32), values)
    entries = jnp.where(lane // FIELDS == slot, entries, 0.0)
    turned = onehot.T.astype(BF16)
    packed = jnp.zeros((128, 128), F32)
    for piece in split3(entries):
        packed = packed + jnp.dot(turned, piece, preferred_element_type=F32)
    send_ref[...] = packed


def pack(traces, target, cell):
    samples = traces.shape[1]
    position = np.arange(samples, dtype=np.float32)[:, None]
    centers = (np.arange(8, dtype=np.float32)[None, :] + np.float32(0.5)) * np.float32(samples / 8)
    kernel = (0.25 * np.exp(-np.abs(position - centers) / np.float32(samples / 8.0))).astype(np.float32)
    tiled = np.zeros((samples, 128), np.float32)
    for slot in range(SLOTS):
        tiled[:, slot * FIELDS : slot * FIELDS + 8] = kernel
    return pl.pallas_call(
        pack_kernel,
        out_shape=shape_of(128, 128),
        compiler_params=PARAMS,
        name="pack",
    )(traces, jnp.asarray(tiled), target, cell)


def fill_columns(got_ref, spread_ref, moment, nz):
    zlane = lax.broadcasted_iota(jnp.int32, (128, nz), 1)
    for slot in range(SLOTS):
        base = slot * FIELDS
        cell = got_ref[:, base + 8 : base + 9].astype(jnp.int32)
        value = got_ref[:, base + moment : base + moment + 1]
        spread = jnp.where(cell % nz == zlane, value, 0.0)
        high, low = split2(spread)
        spread_ref[0, slot * 128 : (slot + 1) * 128, :] = high
        spread_ref[1, slot * 128 : (slot + 1) * 128, :] = low


def inject_rows(turned_ref, spread_ref, first_row, count, nz):
    row = first_row + lax.broadcasted_iota(jnp.int32, (count, 128), 0)
    picks = []
    for slot in range(SLOTS):
        base = slot * FIELDS
        cell = turned_ref[base + 8 : base + 9, :].astype(jnp.int32)
        picks.append(jnp.where(cell // nz == row, 1.0, 0.0).astype(BF16))
    pick = jnp.concatenate(picks, axis=1)
    return jnp.dot(pick, spread_ref[0], preferred_element_type=F32) + jnp.dot(
        pick, spread_ref[1], preferred_element_type=F32
    )


def first_inject_kernel(got_ref, turned_ref, local_ref, out_ref, spread_ref):
    planes, ny, nz = local_ref.shape
    block = pl.program_id(0)

    @pl.when(block == 0)
    def _():
        fill_columns(got_ref, spread_ref, 0, nz)

    added = inject_rows(turned_ref, spread_ref, block * (planes * ny), planes * ny, nz)
    for x in range(planes):
        out_ref[x] = local_ref[x] + added[x * ny : (x + 1) * ny]


def first_inject(got, turned, local):
    nx, ny, nz = local.shape
    planes = 4
    whole = pl.BlockSpec((128, 128), lambda i: (0, 0))
    field = pl.BlockSpec((planes, ny, nz), lambda i: (i, 0, 0))
    return pl.pallas_call(
        first_inject_kernel,
        grid=(nx // planes,),
        in_specs=[whole, whole, field],
        out_specs=field,
        out_shape=shape_of(nx, ny, nz),
        scratch_shapes=[pltpu.VMEM((2, SLOTS * 128, nz), BF16)],
        compiler_params=PARAMS,
        name="first_inject",
    )(got, turned, local)


def divergence_yz(plane, flux_second, flux_third, ps_ref, qs_ref, index):
    ny, nz = plane.shape
    tiles = nz // 128
    pieces = []
    for tile in range(tiles):
        where = index * tiles + tile
        lanes = slice(tile * 128, (tile + 1) * 128)
        ps_ref[where, 8 : 8 + ny, :] = plane[:, lanes]
        total = None
        for k in range(1, 5):
            term = COEFFS[k - 1] * (
                ps_ref[where, 8 + k : 8 + k + ny, :] - ps_ref[where, 9 - k : 9 - k + ny, :]
            )
            total = term if total is None else total + term
        qs_ref[where, 8 : 8 + ny, :] = flux_second[:, lanes] * total
        total = None
        for k in range(1, 5):
            term = COEFFS[k - 1] * (
                qs_ref[where, 7 + k : 7 + k + ny, :] - qs_ref[where, 8 - k : 8 - k + ny, :]
            )
            total = term if total is None else total + term
        pieces.append(total)
    along_second = jnp.concatenate(pieces, axis=1)

    lane = lax.broadcasted_iota(jnp.int32, (ny, nz), 1)

    def shifted(value, amount):
        if amount == 0:
            return value
        moved = pltpu.roll(value, (-amount) % nz, 1)
        inside = lane < nz - amount if amount > 0 else lane >= -amount
        return jnp.where(inside, moved, 0.0)

    total = None
    for k in range(1, 5):
        term = COEFFS[k - 1] * (shifted(plane, k) - shifted(plane, 1 - k))
        total = term if total is None else total + term
    flux = flux_third * total
    total = None
    for k in range(1, 5):
        term = COEFFS[k - 1] * (shifted(flux, k - 1) - shifted(flux, -k))
        total = term if total is None else total + term
    return along_second + total


def clear_edges(ps_ref, qs_ref, ny):
    zero = jnp.zeros((ps_ref.shape[0], 8, 128), F32)
    for ref in (ps_ref, qs_ref):
        ref[:, 0:8, :] = zero
        ref[:, 8 + ny : 16 + ny, :] = zero


def first_local_kernel(p_ref, k_ref, b2_ref, b3_ref, out_ref, ps_ref, qs_ref):
    planes, ny, nz = p_ref.shape

    @pl.when(pl.program_id(0) == 0)
    def _():
        clear_edges(ps_ref, qs_ref, ny)

    for x in range(planes):
        out_ref[x] = k_ref[x] * divergence_yz(p_ref[x], b2_ref[x], b3_ref[x], ps_ref, qs_ref, x)


def first_local(current, stiffness, b2, b3):
    nx, ny, nz = current.shape
    planes = 4
    field = pl.BlockSpec((planes, ny, nz), lambda i: (i, 0, 0))
    shift = pltpu.VMEM((planes * (nz // 128), ny + 16, 128), F32)
    return pl.pallas_call(
        first_local_kernel,
        grid=(nx // planes,),
        in_specs=[field] * 4,
        out_specs=field,
        out_shape=shape_of(nx, ny, nz),
        scratch_shapes=[shift, shift],
        compiler_params=PARAMS,
        name="first_local",
    )(current, stiffness, b2, b3)


def make_local_kernel(moment):
    def local_kernel(*refs):
        p_ref, k_ref, b2_ref, b3_ref, f_ref, change_ref = refs[:6]
        refs = refs[6:]
        if moment > 1:
            image_ref, refs = refs[0], refs[1:]
        got_ref, turned_ref, out_ref, image_out_ref, ps_ref, qs_ref, spread_ref = refs
        planes, ny, nz = p_ref.shape
        block = pl.program_id(0)

        @pl.when(block == 0)
        def _():
            clear_edges(ps_ref, qs_ref, ny)
            fill_columns(got_ref, spread_ref, moment, nz)

        added = inject_rows(turned_ref, spread_ref, block * (planes * ny), planes * ny, nz)
        for x in range(planes):
            out_ref[x] = (
                k_ref[x] * divergence_yz(p_ref[x], b2_ref[x], b3_ref[x], ps_ref, qs_ref, x)
                + added[x * ny : (x + 1) * ny]
            )
            image = f_ref[0, x].astype(F32) * change_ref[x]
            if moment > 1:
                image = image + image_ref[x]
            image_out_ref[x] = image

    return local_kernel


def local_step(moment, current, stiffness, b2, b3, forward, change, image, got, turned):
    nx, ny, nz = current.shape
    planes = 4
    field = pl.BlockSpec((planes, ny, nz), lambda i: (i, 0, 0))
    frame = pl.BlockSpec((1, planes, ny, nz), lambda i: (moment - 1, i, 0, 0))
    whole = pl.BlockSpec((128, 128), lambda i: (0, 0))
    shift = pltpu.VMEM((planes * (nz // 128), ny + 16, 128), F32)
    images = [image] if moment > 1 else []
    return pl.pallas_call(
        make_local_kernel(moment),
        grid=(nx // planes,),
        in_specs=[field] * 4 + [frame, field] + [field] * len(images) + [whole, whole],
        out_specs=[field, field],
        out_shape=[shape_of(nx, ny, nz)] * 2,
        scratch_shapes=[shift, shift, pltpu.VMEM((2, SLOTS * 128, nz), BF16)],
        compiler_params=PARAMS,
        name="local_step",
    )(current, stiffness, b2, b3, forward, change, *images, got, turned)


def change_column(p_refs, b_refs, k_ref, local_ref, rows):
    pl_ref, pm_ref, pr_ref = p_refs
    bl_ref, bm_ref, br_ref = b_refs
    nx = pm_ref.shape[0]

    def cell(i):
        if i < 0:
            return pl_ref[HALO + i, rows, :]
        if i >= nx:
            return pr_ref[i - nx, rows, :]
        return pm_ref[i, rows, :]

    def face(i):
        if i < 0:
            return bl_ref[4 + i, rows, :]
        if i >= nx:
            return br_ref[i - nx, rows, :]
        return bm_ref[i, rows, :]

    cells = {i: cell(i) for i in range(-HALO, 0)}
    fluxes = {}
    for ahead in range(0, nx + HALO):
        cells[ahead] = cell(ahead)
        j = ahead - 4
        if j >= -4:
            total = None
            for k in range(1, 5):
                term = COEFFS[k - 1] * (cells[j + k] - cells[j + 1 - k])
                total = term if total is None else total + term
            fluxes[j] = face(j) * total
        i = j - 3
        if i >= 0:
            total = None
            for k in range(1, 5):
                term = COEFFS[k - 1] * (fluxes[i + k - 1] - fluxes[i - k])
                total = term if total is None else total + term
            yield i, cells[i], local_ref[i, rows, :] + k_ref[i, rows, :] * total


def update_kernel(
    pl_ref, pm_ref, pr_ref, bl_ref, bm_ref, br_ref, k_ref, local_ref, before_ref,
    next_ref, change_ref, head_ref, tail_ref,
):
    nx, ny = pm_ref.shape[:2]
    for band in range(ny // 8):
        rows = slice(band * 8, band * 8 + 8)
        for i, now, change in change_column(
            (pl_ref, pm_ref, pr_ref), (bl_ref, bm_ref, br_ref), k_ref, local_ref, rows
        ):
            following = 2.0 * now - before_ref[i, rows, :] + change
            next_ref[i, rows, :] = following
            change_ref[i, rows, :] = change
            if i < HALO:
                head_ref[i, rows, :] = following
            if i >= nx - HALO:
                tail_ref[i - (nx - HALO), rows, :] = following


def last_kernel(
    place_ref, pl_ref, pm_ref, pr_ref, bl_ref, bm_ref, br_ref, k_ref, local_ref, before_ref,
    image_ref, f_ref, next_ref, muted_ref, kept_ref,
):
    nx, ny, lanes = pm_ref.shape
    second = lax.broadcasted_iota(jnp.int32, (8, lanes), 0).astype(F32)
    third = (pl.program_id(0) * lanes + lax.broadcasted_iota(jnp.int32, (8, lanes), 1)).astype(F32)
    first_at = (place_ref[3] - place_ref[0]).astype(F32)
    second_at = place_ref[1].astype(F32)
    third_at = place_ref[2].astype(F32)
    for band in range(ny // 8):
        rows = slice(band * 8, band * 8 + 8)
        flat = (second + float(band * 8) - second_at) ** 2 + (third - third_at) ** 2
        for i, now, change in change_column(
            (pl_ref, pm_ref, pr_ref), (bl_ref, bm_ref, br_ref), k_ref, local_ref, rows
        ):
            next_ref[i, rows, :] = 2.0 * now - before_ref[i, rows, :] + change
            image = image_ref[i, rows, :] + f_ref[0, i, rows, :].astype(F32) * change
            distance = (first_at + float(i)) ** 2 + flat
            kept_ref[i, rows, :] = (1.0 - jnp.exp(distance * (-1.0 / (2.0 * MUTE * MUTE)))) * image
    for y in range(ny):
        muted_ref[y // 2, y % 2, :, :] = kept_ref[:, y, :]


def update_step(halos, current, b1_halos, b1, stiffness, local, before):
    nx, ny, nz = current.shape

    def tall(depth):
        return pl.BlockSpec((depth, ny, 128), lambda i: (0, 0, i))

    return pl.pallas_call(
        update_kernel,
        grid=(nz // 128,),
        in_specs=[tall(HALO), tall(nx), tall(HALO), tall(4), tall(nx), tall(3)] + [tall(nx)] * 3,
        out_specs=[tall(nx), tall(nx), tall(HALO), tall(HALO)],
        out_shape=[shape_of(nx, ny, nz)] * 2 + [shape_of(HALO, ny, nz)] * 2,
        compiler_params=PARAMS,
        name="update_step",
    )(halos[0], current, halos[1], b1_halos[0], b1, b1_halos[1], stiffness, local, before)


def last_step(place, halos, current, b1_halos, b1, stiffness, local, before, image, forward):
    nx, ny, nz = current.shape
    steps = forward.shape[0]

    def tall(depth):
        return pl.BlockSpec((depth, ny, 128), lambda i, s: (0, 0, i))

    return pl.pallas_call(
        last_kernel,
        grid_spec=pltpu.PrefetchScalarGridSpec(
            num_scalar_prefetch=1,
            grid=(nz // 128,),
            in_specs=[tall(HALO), tall(nx), tall(HALO), tall(4), tall(nx), tall(3)]
            + [tall(nx)] * 4
            + [pl.BlockSpec((1, nx, ny, 128), lambda i, s: (steps - 1, 0, 0, i))],
            out_specs=[
                tall(nx),
                pl.BlockSpec((ny // 2, 2, nx, 128), lambda i, s: (0, 0, 0, i)),
            ],
            scratch_shapes=[pltpu.VMEM((nx, ny, 128), F32)],
        ),
        out_shape=[shape_of(nx, ny, nz), shape_of(ny // 2, 2, nx, nz)],
        compiler_params=PARAMS,
        name="last_step",
    )(
        place, halos[0], current, halos[1], b1_halos[0], b1, b1_halos[1], stiffness, local, before,
        image, forward,
    )


def light_kernel(f_ref, out_ref, kept_ref):
    steps, nx, ny, lanes = f_ref.shape
    for i in range(nx):
        total = jnp.zeros((ny, lanes), F32)
        for t in range(steps):
            frame = f_ref[t, i].astype(F32)
            total = total + frame * frame
        kept_ref[i] = total
    for y in range(ny):
        out_ref[y // 2, y % 2, :, :] = kept_ref[:, y, :]


def light_sum(forward):
    steps, nx, ny, nz = forward.shape
    return pl.pallas_call(
        light_kernel,
        grid=(nz // 128,),
        in_specs=[pl.BlockSpec((steps, nx, ny, 128), lambda i: (0, 0, 0, i))],
        out_specs=pl.BlockSpec((ny // 2, 2, nx, 128), lambda i: (0, 0, 0, i)),
        out_shape=shape_of(ny // 2, 2, nx, nz),
        scratch_shapes=[pltpu.VMEM((nx, ny, 128), F32)],
        compiler_params=PARAMS,
        name="light_sum",
    )(forward)


def quotient_kernel(image_ref, light_ref, out_ref, *, scale):
    nz = image_ref.shape[-1]
    for side in range(2):
        image = image_ref[0, side]
        light = light_ref[0, side]
        for shot in range(1, image_ref.shape[0]):
            image = image + image_ref[shot, side]
            light = light + light_ref[shot, side]
        out_ref[:, side * nz : (side + 1) * nz] = image / (light * scale + DAMP)


def quotient(images, lights, scale):
    _, _, nx, nz = images.shape
    return pl.pallas_call(
        lambda *refs: quotient_kernel(*refs, scale=scale),
        out_shape=shape_of(nx, 2 * nz),
        compiler_params=PARAMS,
        name="quotient",
    )(images, lights)


def exchange(head, tail):
    count = lax.axis_size("sub")
    from_left = lax.ppermute(tail, "sub", [(i, i + 1) for i in range(count - 1)])
    from_right = lax.ppermute(head, "sub", [(i + 1, i) for i in range(count - 1)])
    return from_left, from_right


def local(
    stiffness, b1, b2, b3, adjoint_before, adjoint_current, forward_field,
    traces, receiver_target, receiver_cell, source_cell,
):
    both = ("shot", "sub")
    steps = forward_field.shape[1]
    nx = stiffness.shape[0]
    forward = forward_field[0]
    before = adjoint_before[0]
    current = adjoint_current[0]

    halos = exchange(current[:HALO], current[nx - HALO :])
    b1_halos = exchange(b1[:3], b1[nx - 4 :])
    send = pack(traces, receiver_target, receiver_cell[:, None])
    got = lax.all_to_all(send, both, split_axis=0, concat_axis=0, tiled=True)
    lights = lax.all_to_all(light_sum(forward), "shot", split_axis=0, concat_axis=0, tiled=True)
    nearby = first_local(current, stiffness, b2, b3)
    turned = got.T
    nearby = first_inject(got, turned, nearby)

    image = None
    for moment in range(steps - 1):
        following, change, head, tail = update_step(
            halos, current, b1_halos, b1, stiffness, nearby, before
        )
        halos = exchange(head, tail)
        before, current = current, following
        nearby, image = local_step(
            moment + 1, current, stiffness, b2, b3, forward, change, image, got, turned
        )
    place = jnp.concatenate(
        [source_cell[0], (lax.axis_index("sub") * nx).astype(jnp.int32)[None]]
    )
    following, muted = last_step(
        place, halos, current, b1_halos, b1, stiffness, nearby, before, image, forward
    )
    images = lax.all_to_all(muted, "shot", split_axis=0, concat_axis=0, tiled=True)
    gradient = quotient(images, lights, 1.0 / (steps * lax.axis_size("shot")))
    return gradient, current[None], following[None]


def solution(mesh):
    placed = (
        P("sub", None, None),
        P("sub", None, None),
        P("sub", None, None),
        P("sub", None, None),
        P("shot", "sub", None, None),
        P("shot", "sub", None, None),
        P("shot", None, "sub", None, None),
        P(("shot", "sub"), None),
        P(("shot", "sub"), None),
        P(("shot", "sub")),
        P("shot", None),
    )
    return jax.shard_map(
        local,
        mesh=mesh,
        in_specs=placed,
        out_specs=(P("sub", "shot"), P("shot", "sub", None, None), P("shot", "sub", None, None)),
        check_vma=False,
    )
```

time: 639 us -> 212 us (0.33); the launches traced: 627 us -> 209 us
  waiting for transfers between devices: 165 us -> 2.99 us
  other arithmetic: 161 us -> 0.73 us
  local copies, waits for them, and re-layouts: 151 us -> 37.1 us
  Pallas kernels: 0 us -> 81.2 us
  starting transfers between devices: 130 us -> 63.4 us
  blocking collectives: 0 us -> 22.4 us
  between operations: 15.3 us -> 1.3 us
    reduce_scatter x2 -> x0, waiting for transfers between devices: 132 us -> none  [the longest x1 75.2 us: local(): lax.psum_scatter(flat_light, 'shot', scatter_dimension=1, tiled=True)]
    mul x17 -> x0, other arithmetic: 81.4 us -> none  [the longest x8 48.9 us: local(): stiffness * divergence]
    scatter x3 -> x0, local copies, waits for them, and re-layouts: 81.2 us -> none  [the longest x2 59.3 us: local(): row_buffer = jnp.zeros((device_count, capacity, sample_count), jnp.float3...]
    pallas_call x0 -> x20, Pallas kernels: none -> 81.2 us  [the longest x7 42.4 us: local_step(): pl.pallas_call(make_local_kernel(moment), grid=(nx // planes,), in_specs=...]
    ppermute x32 -> x18, starting transfers between devices: 105 us -> 45.1 us  [the longest x9 33.4 us: exchange(): lax.ppermute(tail, 'sub', [(i, i + 1) for i in range(count - 1)])]
    reshape x32 -> x0, local copies, waits for them, and re-layouts: 46.9 us -> none  [the longest x31 44.7 us: local(): change = (stiffness * divergence).reshape(-1).at[place_index].add(step_va...]
    scatter-add x8 -> x0, other arithmetic: 45.2 us -> none  [local(): change = (stiffness * divergence).reshape(-1).at[place_index].add(step_va...]
    add x11 -> x0, other arithmetic: 27.3 us -> none  [the longest x9 20.3 us: local(): following = 2.0 * current - earlier + change]
  transfers between devices with their start and end apart: 36 -> 20, of which waited for: 15 -> 1; matrix products, arithmetic and copies ran while one was open for 25% -> 3% of each run, Pallas kernels for 0% -> 30%
where the time goes in v1:
time: 212 us; the launch traced here: 209 us
  Pallas kernels  81.2 us (38%)
  starting transfers between devices  63.4 us (30%)
  local copies, waits for them, and re-layouts  37.1 us (18%)
  blocking collectives  22.4 us (11%)
  waiting for transfers between devices  2.99 us (1%)
    pallas_call x7, Pallas kernels, local_step(): pl.pallas_call(make_local_kernel(moment), grid=(nx // planes,), in_specs=...  42.4 us
    ppermute x9, starting transfers between devices, exchange(): lax.ppermute(tail, 'sub', [(i, i + 1) for i in range(count - 1)])  33.4 us
    unnamed x103, local copies, waits for them, and re-layouts  30.2 us
    pallas_call x7, Pallas kernels, update_step(): pl.pallas_call(update_kernel, grid=(nz // 128,), in_specs=[tall(HALO), ta...  22.9 us
    all_to_all x1, blocking collectives, local(): lax.all_to_all(muted, 'shot', split_axis=0, concat_axis=0, tiled=True)  22.4 us
    all_to_all x1, starting transfers between devices, local(): got = lax.all_to_all(send, both, split_axis=0, concat_axis=0, tiled=True)  13.5 us
    ppermute x9, starting transfers between devices, exchange(): lax.ppermute(head, 'sub', [(i + 1, i) for i in range(count - 1)])  11.8 us
    all_to_all x1, starting transfers between devices, local(): lax.all_to_all(light_sum(forward), 'shot', split_axis=0, concat_axis=0, t...  4.78 us
  transfers between devices with their start and end apart: 20, of which 1 were waited for; matrix products, arithmetic and copies ran while one was open for 3% of the time, Pallas kernels for 30%

profile of v1, /device:TPU:0, one launch (start us, length us, event | category | flops | bytes accessed | tf_op | source)
XLA Modules:
  0.0 209.1 jit_solution(13499223057325682376)
XLA Ops:
  7.7 4.2 %collective-permute-start.2 = (f32[4,32,384]{2,1,0:T(8,128)}, f32[4,32,384]{2,1,0:T(8,128)S(1)}, u32[]{:S(2)}, u32[]{:S(2)}) collective-permute-start(f32[4,32,384]{2,1,0:T(8,128)} %slice.22), channel_id=1, source_target_pairs={{0,1},{1,2},{2,3},{3,4},{4,5},{5,6},{6,7},{8,9},{9,10},{10,11},{11... | collective-permute-start | bytes 589832 | tf_op jit(solution)/shard_map/ppermute | solution.py:445
  20.2 13.5 %all-to-all-start = ((f32[128,1,128]{2,1,0:T(1,128)}), f32[128,1,128]{2,1,0:T(1,128)S(1)}, u32[]{:S(2)}, u32[]{:S(2)}) async-start(f32[128,1,128]{2,1,0:T(1,128)} %bitcast.50), calls=%async_computation | async-start | bytes 131072 | tf_op jit(solution)/shard_map/all_to_all | solution.py:464
  34.8 4.3 %first_local.1.local_ref = f32[16,32,384]{2,1,0:T(8,128)S(1)} custom-call(f32[16,32,384]{2,1,0:T(8,128)S(1)} %bitcast.31, f32[16,32,384]{2,1,0:T(8,128)S(1)} %copy-done.1, f32[16,32,384]{2,1,0:T(8,128)S(1)} %copy-done.8, f32[16,32,384]{2,1,0:T(8,128)S(1)} %copy-done.11), custom_call_target="tpu_custom_call" | custom-call | tf_op jit(solution)/shard_map/first_local/pallas_call | solution.py:206
  49.6 3.1 %update_step.7 = (f32[16,32,384]{2,1,0:T(8,128)S(1)}, f32[16,32,384]{2,1,0:T(8,128)S(1)}, f32[7,32,384]{2,1,0:T(8,128)S(1)}, f32[7,32,384]{2,1,0:T(8,128)S(1)}) custom-call(f32[7,32,384]{2,1,0:T(8,128)} %collective-permute-done.pl_ref, f32[16,32,384]{2,1,0:T(8,128)S(1)} %bitcast.32, f32[7,32,384]{2,1,0:T(8,128)} %collective-permute-done.1.pr_ref, ...), custom_call_target="tpu_custom_call" | custom-call | tf_op jit(solution)/shard_map/update_step/pallas_call | solution.py:355
  55.6 5.9 %local_step.7 = (f32[16,32,384]{2,1,0:T(8,128)S(1)}, f32[16,32,384]{2,1,0:T(8,128)S(1)}) custom-call(f32[16,32,384]{2,1,0:T(8,128)S(1)} %get-tuple-element.48.refs_0_.pm_ref.before_ref, f32[16,32,384]{2,1,0:T(8,128)S(1)} %copy-done.1, f32[16,32,384]{2,1,0:T(8,128)S(1)} %copy-done.8, f32[16,32,384]{2,1,0:T(8,128)S(1)} %copy-done.11, ...), custom_call_target="tpu_custom_call" | custom-call | tf_op jit(solution)/shard_map/local_step/pallas_call | solution.py:255
  63.3 3.0 %update_step.8 = (f32[16,32,384]{2,1,0:T(8,128)S(1)}, f32[16,32,384]{2,1,0:T(8,128)S(1)}, f32[7,32,384]{2,1,0:T(8,128)S(1)}, f32[7,32,384]{2,1,0:T(8,128)S(1)}) custom-call(f32[7,32,384]{2,1,0:T(8,128)S(1)} %collective-permute-done.4.pl_ref, f32[16,32,384]{2,1,0:T(8,128)S(1)} %get-tuple-element.48.refs_0_.pm_ref.before_ref, ...), custom_call_target="tpu_custom_call" | custom-call | tf_op jit(solution)/shard_map/update_step/pallas_call | solution.py:355
  66.3 3.5 %collective-permute-start.6 = (f32[7,32,384]{2,1,0:T(8,128)S(1)}, f32[7,32,384]{2,1,0:T(8,128)S(1)}, u32[]{:S(2)}, u32[]{:S(2)}) collective-permute-start(f32[7,32,384]{2,1,0:T(8,128)S(1)} %get-tuple-element.52), channel_id=1, source_target_pairs={{0,1},{1,2},{2,3},{3,4},{4,5},{5,6},{6,7},{8,9},{9,10},{10,11},{11... | collective-permute-start | bytes 1032200 | tf_op jit(solution)/shard_map/ppermute | solution.py:445
  71.1 6.0 %local_step.8 = (f32[16,32,384]{2,1,0:T(8,128)S(1)}, f32[16,32,384]{2,1,0:T(8,128)S(1)}) custom-call(f32[16,32,384]{2,1,0:T(8,128)S(1)} %get-tuple-element.53.refs_0_.pm_ref.before_ref, f32[16,32,384]{2,1,0:T(8,128)S(1)} %copy-done.1, f32[16,32,384]{2,1,0:T(8,128)S(1)} %copy-done.8, f32[16,32,384]{2,1,0:T(8,128)S(1)} %copy-done.11, ...), custom_call_target="tpu_custom_call" | custom-call | tf_op jit(solution)/shard_map/local_step/pallas_call | solution.py:255
  81.9 4.3 %collective-permute-start.8 = (f32[7,32,384]{2,1,0:T(8,128)S(1)}, f32[7,32,384]{2,1,0:T(8,128)S(1)}, u32[]{:S(2)}, u32[]{:S(2)}) collective-permute-start(f32[7,32,384]{2,1,0:T(8,128)S(1)} %get-tuple-element.58), channel_id=1, source_target_pairs={{0,1},{1,2},{2,3},{3,4},{4,5},{5,6},{6,7},{8,9},{9,10},{10,11},{11... | collective-permute-start | bytes 1032200 | tf_op jit(solution)/shard_map/ppermute | solution.py:445
  87.5 6.0 %local_step.9 = (f32[16,32,384]{2,1,0:T(8,128)S(1)}, f32[16,32,384]{2,1,0:T(8,128)S(1)}) custom-call(f32[16,32,384]{2,1,0:T(8,128)S(1)} %get-tuple-element.59.refs_0_.pm_ref.before_ref, f32[16,32,384]{2,1,0:T(8,128)S(1)} %copy-done.1, f32[16,32,384]{2,1,0:T(8,128)S(1)} %copy-done.8, f32[16,32,384]{2,1,0:T(8,128)S(1)} %copy-done.11, ...), custom_call_target="tpu_custom_call" | custom-call | tf_op jit(solution)/shard_map/local_step/pallas_call | solution.py:255
  98.4 4.3 %collective-permute-start.10 = (f32[7,32,384]{2,1,0:T(8,128)S(1)}, f32[7,32,384]{2,1,0:T(8,128)S(1)}, u32[]{:S(2)}, u32[]{:S(2)}) collective-permute-start(f32[7,32,384]{2,1,0:T(8,128)S(1)} %get-tuple-element.64), channel_id=1, source_target_pairs={{0,1},{1,2},{2,3},{3,4},{4,5},{5,6},{6,7},{8,9},{9,10},{10,11},{11... | collective-permute-start | bytes 1032200 | tf_op jit(solution)/shard_map/ppermute | solution.py:445
  104.2 6.1 %local_step.10 = (f32[16,32,384]{2,1,0:T(8,128)S(1)}, f32[16,32,384]{2,1,0:T(8,128)S(1)}) custom-call(f32[16,32,384]{2,1,0:T(8,128)S(1)} %get-tuple-element.65.refs_0_.pm_ref.before_ref, f32[16,32,384]{2,1,0:T(8,128)S(1)} %copy-done.1, f32[16,32,384]{2,1,0:T(8,128)S(1)} %copy-done.8, f32[16,32,384]{2,1,0:T(8,128)S(1)} %copy-done.11, ...), custom_call_target="tpu_custom_call" | custom-call | tf_op jit(solution)/shard_map/local_step/pallas_call | solution.py:255
  112.1 3.8 %update_step.11 = (f32[16,32,384]{2,1,0:T(8,128)S(1)}, f32[16,32,384]{2,1,0:T(8,128)S(1)}, f32[7,32,384]{2,1,0:T(8,128)}, f32[7,32,384]{2,1,0:T(8,128)}) custom-call(f32[7,32,384]{2,1,0:T(8,128)S(1)} %collective-permute-done.10.pl_ref, f32[16,32,384]{2,1,0:T(8,128)S(1)} %get-tuple-element.65.refs_0_.pm_ref.before_ref, ...), custom_call_target="tpu_custom_call" | custom-call | tf_op jit(solution)/shard_map/update_step/pallas_call | solution.py:355
  116.8 4.3 %collective-permute-start.12 = (f32[7,32,384]{2,1,0:T(8,128)}, f32[7,32,384]{2,1,0:T(8,128)S(1)}, u32[]{:S(2)}, u32[]{:S(2)}) collective-permute-start(f32[7,32,384]{2,1,0:T(8,128)} %get-tuple-element.70), channel_id=1, source_target_pairs={{0,1},{1,2},{2,3},{3,4},{4,5},{5,6},{6,7},{8,9},{9,10},{10,11},{11... | collective-permute-start | bytes 1032200 | tf_op jit(solution)/shard_map/ppermute | solution.py:445
  124.7 4.8 %all-to-all-start.2 = ((f32[16,2,16,384]{3,2,1,0:T(8,128)}), f32[16,2,16,384]{3,2,1,0:T(8,128)}, u32[]{:S(2)}, u32[]{:S(2)}) async-start(f32[16,2,16,384]{3,2,1,0:T(8,128)} %light_sum.1), calls=%async_computation.2 | async-start | bytes 1572864 | tf_op jit(solution)/shard_map/all_to_all | solution.py:465
  134.8 6.1 %local_step.11 = (f32[16,32,384]{2,1,0:T(8,128)S(1)}, f32[16,32,384]{2,1,0:T(8,128)S(1)}) custom-call(f32[16,32,384]{2,1,0:T(8,128)S(1)} %copy-done.21, f32[16,32,384]{2,1,0:T(8,128)S(1)} %copy-done.3, f32[16,32,384]{2,1,0:T(8,128)S(1)} %copy-done.9, f32[16,32,384]{2,1,0:T(8,128)S(1)} %copy-done.12, bf16[8,16,32,384]{3,2,1,0:T(8,128)(2,1)} %bitcast.25, ...), custom_call_target="tpu_custom_call" | custom-call | tf_op jit(solution)/shard_map/local_step/pallas_call | solution.py:255
  142.8 3.3 %update_step.12 = (f32[16,32,384]{2,1,0:T(8,128)S(1)}, f32[16,32,384]{2,1,0:T(8,128)S(1)}, f32[7,32,384]{2,1,0:T(8,128)S(1)}, f32[7,32,384]{2,1,0:T(8,128)S(1)}) custom-call(f32[7,32,384]{2,1,0:T(8,128)S(1)} %collective-permute-done.12.pl_ref, f32[16,32,384]{2,1,0:T(8,128)S(1)} %copy-done.22, f32[7,32,384]{2,1,0:T(8,128)S(1)} %collective-permute-done.13.pr_ref, ...), custom_call_target="tpu_custom_call" | custom-call | tf_op jit(solution)/shard_map/update_step/pallas_call | solution.py:355
  146.1 4.0 %collective-permute-start.14 = (f32[7,32,384]{2,1,0:T(8,128)S(1)}, f32[7,32,384]{2,1,0:T(8,128)S(1)}, u32[]{:S(2)}, u32[]{:S(2)}) collective-permute-start(f32[7,32,384]{2,1,0:T(8,128)S(1)} %get-tuple-element.76), channel_id=1, source_target_pairs={{0,1},{1,2},{2,3},{3,4},{4,5},{5,6},{6,7},{8,9},{9,10},{10,11},{11... | collective-permute-start | bytes 1032200 | tf_op jit(solution)/shard_map/ppermute | solution.py:445
  151.4 6.0 %local_step.12 = (f32[16,32,384]{2,1,0:T(8,128)S(1)}, f32[16,32,384]{2,1,0:T(8,128)S(1)}) custom-call(f32[16,32,384]{2,1,0:T(8,128)S(1)} %get-tuple-element.77.refs_0_.pm_ref.before_ref, f32[16,32,384]{2,1,0:T(8,128)S(1)} %copy-done.3, f32[16,32,384]{2,1,0:T(8,128)S(1)} %copy-done.10, f32[16,32,384]{2,1,0:T(8,128)S(1)} %copy-done.13, ...), custom_call_target="tpu_custom_call" | custom-call | tf_op jit(solution)/shard_map/local_step/pallas_call | solution.py:255
  158.3 3.7 %update_step.13 = (f32[16,32,384]{2,1,0:T(8,128)}, f32[16,32,384]{2,1,0:T(8,128)S(1)}, f32[7,32,384]{2,1,0:T(8,128)}, f32[7,32,384]{2,1,0:T(8,128)}) custom-call(f32[7,32,384]{2,1,0:T(8,128)S(1)} %collective-permute-done.14.pl_ref, f32[16,32,384]{2,1,0:T(8,128)S(1)} %get-tuple-element.77.refs_0_.pm_ref.before_ref, ...), custom_call_target="tpu_custom_call" | custom-call | tf_op jit(solution)/shard_map/update_step/pallas_call | solution.py:355
  162.9 5.3 %collective-permute-start.16 = (f32[7,32,384]{2,1,0:T(8,128)}, f32[7,32,384]{2,1,0:T(8,128)}, u32[]{:S(2)}, u32[]{:S(2)}) collective-permute-start(f32[7,32,384]{2,1,0:T(8,128)} %get-tuple-element.82), channel_id=1, source_target_pairs={{0,1},{1,2},{2,3},{3,4},{4,5},{5,6},{6,7},{8,9},{9,10},{10,11},{11... | collective-permute-start | bytes 1032200 | tf_op jit(solution)/shard_map/ppermute | solution.py:445
  173.3 6.2 %local_step.13 = (f32[16,32,384]{2,1,0:T(8,128)S(1)}, f32[16,32,384]{2,1,0:T(8,128)S(1)}) custom-call(f32[16,32,384]{2,1,0:T(8,128)S(1)} %copy-done.32, f32[16,32,384]{2,1,0:T(8,128)S(1)} %copy-done.4, f32[16,32,384]{2,1,0:T(8,128)S(1)} %copy-done.10, f32[16,32,384]{2,1,0:T(8,128)S(1)} %copy-done.13, bf16[8,16,32,384]{3,2,1,0:T(8,128)(2,1)} %bitcast.27, ...), custom_call_target="tpu_custom_call" | custom-call | tf_op jit(solution)/shard_map/local_step/pallas_call | solution.py:255
  180.4 4.4 %last_step.1 = (f32[16,32,384]{2,1,0:T(8,128)}, f32[16,2,16,384]{3,2,1,0:T(8,128)S(1)}) custom-call(s32[4]{0:T(128)S(1)} %pad_add_fusion.place_ref, f32[7,32,384]{2,1,0:T(8,128)} %collective-permute-done.16.pl_ref, f32[16,32,384]{2,1,0:T(8,128)S(1)} %copy-done.33, f32[7,32,384]{2,1,0:T(8,128)} %collective-permute-done.17.pr_ref, ...), custom_call_target="tpu_custom_call" | custom-call | tf_op jit(solution)/shard_map/last_step/pallas_call | solution.py:373
  184.8 22.4 %all_to_all.21.refs_0_ = f32[16,2,16,384]{3,2,1,0:T(8,128)S(1)} all-to-all(f32[16,2,16,384]{3,2,1,0:T(8,128)S(1)} %get-tuple-element.89), channel_id=1, replica_groups=mesh['shot'=16,'sub'=8] {'shot'}, dimensions={0} | all-to-all | bytes 1572864 | tf_op jit(solution)/shard_map/all_to_all | solution.py:486
  (146 shorter events, 69.4 us)
Async XLA Ops:
  0.6 33.0 %copy-start.1 = (f32[16,32,384]{2,1,0:T(8,128)S(1)}, f32[16,32,384]{2,1,0:T(8,128)}, u32[]{:S(2)}) copy-start(f32[16,32,384]{2,1,0:T(8,128)} %k_ref.17) | copy-start | bytes 2359300
  0.6 33.0 %copy-start.8 = (f32[16,32,384]{2,1,0:T(8,128)S(1)}, f32[16,32,384]{2,1,0:T(8,128)}, u32[]{:S(2)}) copy-start(f32[16,32,384]{2,1,0:T(8,128)} %refs_2_.13) | copy-start | bytes 2359300
  0.7 33.0 %copy-start.11 = (f32[16,32,384]{2,1,0:T(8,128)S(1)}, f32[16,32,384]{2,1,0:T(8,128)}, u32[]{:S(2)}) copy-start(f32[16,32,384]{2,1,0:T(8,128)} %refs_3_.13) | copy-start | bytes 2359300
  2.8 45.7 %collective-permute-start = (f32[7,32,384]{2,1,0:T(8,128)}, f32[7,32,384]{2,1,0:T(8,128)}, u32[]{:S(2)}, u32[]{:S(2)}) collective-permute-start(f32[7,32,384]{2,1,0:T(8,128)} %get-tuple-element.92), channel_id=1, source_target_pairs={{0,1},{1,2},{2,3},{3,4},{4,5},{5,6},{6,7},{8,9},{9,10},{10,11},{11... | collective-permute-start | bytes 1032200 | tf_op jit(solution)/shard_map/ppermute | solution.py:445
  4.8 43.7 %collective-permute-start.1 = (f32[7,32,384]{2,1,0:T(8,128)}, f32[7,32,384]{2,1,0:T(8,128)}, u32[]{:S(2)}, u32[]{:S(2)}) collective-permute-start(f32[7,32,384]{2,1,0:T(8,128)} %get-tuple-element.91), channel_id=1, source_target_pairs={{1,0},{2,1},{3,2},{4,3},{5,4},{6,5},{7,6},{9,8},{10,9},{11,10},{12... | collective-permute-start | bytes 1032200 | tf_op jit(solution)/shard_map/ppermute | solution.py:446
  7.7 40.8 %collective-permute-start.2 = (f32[4,32,384]{2,1,0:T(8,128)}, f32[4,32,384]{2,1,0:T(8,128)S(1)}, u32[]{:S(2)}, u32[]{:S(2)}) collective-permute-start(f32[4,32,384]{2,1,0:T(8,128)} %slice.22), channel_id=1, source_target_pairs={{0,1},{1,2},{2,3},{3,4},{4,5},{5,6},{6,7},{8,9},{9,10},{10,11},{11... | collective-permute-start | bytes 589832 | tf_op jit(solution)/shard_map/ppermute | solution.py:445
  13.5 34.9 %collective-permute-start.3 = (f32[3,32,384]{2,1,0:T(8,128)}, f32[3,32,384]{2,1,0:T(8,128)S(1)}, u32[]{:S(2)}, u32[]{:S(2)}) collective-permute-start(f32[3,32,384]{2,1,0:T(8,128)} %slice.23), channel_id=1, source_target_pairs={{1,0},{2,1},{3,2},{4,3},{5,4},{6,5},{7,6},{9,8},{10,9},{11,10},{12... | collective-permute-start | bytes 442376 | tf_op jit(solution)/shard_map/ppermute | solution.py:446
  20.2 28.3 %copy-start.5 = (f32[16,32,384]{2,1,0:T(8,128)S(1)}, f32[16,32,384]{2,1,0:T(8,128)}, u32[]{:S(2)}) copy-start(f32[16,32,384]{2,1,0:T(8,128)} %bm_ref.15) | copy-start | bytes 2359300
  20.2 22.8 %all-to-all-start = ((f32[128,1,128]{2,1,0:T(1,128)}), f32[128,1,128]{2,1,0:T(1,128)S(1)}, u32[]{:S(2)}, u32[]{:S(2)}) async-start(f32[128,1,128]{2,1,0:T(1,128)} %bitcast.50), calls=%async_computation | async-start | bytes 131072 | tf_op jit(solution)/shard_map/all_to_all | solution.py:464
  52.7 10.6 %collective-permute-start.4 = (f32[7,32,384]{2,1,0:T(8,128)S(1)}, f32[7,32,384]{2,1,0:T(8,128)S(1)}, u32[]{:S(2)}, u32[]{:S(2)}) collective-permute-start(f32[7,32,384]{2,1,0:T(8,128)S(1)} %get-tuple-element.47), channel_id=1, source_target_pairs={{0,1},{1,2},{2,3},{3,4},{4,5},{5,6},{6,7},{8,9},{9,10},{10,11},{11... | collective-permute-start | bytes 1032200 | tf_op jit(solution)/shard_map/ppermute | solution.py:445
  54.3 9.0 %collective-permute-start.5 = (f32[7,32,384]{2,1,0:T(8,128)S(1)}, f32[7,32,384]{2,1,0:T(8,128)S(1)}, u32[]{:S(2)}, u32[]{:S(2)}) collective-permute-start(f32[7,32,384]{2,1,0:T(8,128)S(1)} %get-tuple-element.49), channel_id=1, source_target_pairs={{1,0},{2,1},{3,2},{4,3},{5,4},{6,5},{7,6},{9,8},{10,9},{11,10},{12... | collective-permute-start | bytes 1032200 | tf_op jit(solution)/shard_map/ppermute | solution.py:446
  66.3 12.6 %collective-permute-start.6 = (f32[7,32,384]{2,1,0:T(8,128)S(1)}, f32[7,32,384]{2,1,0:T(8,128)S(1)}, u32[]{:S(2)}, u32[]{:S(2)}) collective-permute-start(f32[7,32,384]{2,1,0:T(8,128)S(1)} %get-tuple-element.52), channel_id=1, source_target_pairs={{0,1},{1,2},{2,3},{3,4},{4,5},{5,6},{6,7},{8,9},{9,10},{10,11},{11... | collective-permute-start | bytes 1032200 | tf_op jit(solution)/shard_map/ppermute | solution.py:445
  69.8 9.1 %collective-permute-start.7 = (f32[7,32,384]{2,1,0:T(8,128)S(1)}, f32[7,32,384]{2,1,0:T(8,128)S(1)}, u32[]{:S(2)}, u32[]{:S(2)}) collective-permute-start(f32[7,32,384]{2,1,0:T(8,128)S(1)} %get-tuple-element.54), channel_id=1, source_target_pairs={{1,0},{2,1},{3,2},{4,3},{5,4},{6,5},{7,6},{9,8},{10,9},{11,10},{12... | collective-permute-start | bytes 1032200 | tf_op jit(solution)/shard_map/ppermute | solution.py:446
  81.9 13.4 %collective-permute-start.8 = (f32[7,32,384]{2,1,0:T(8,128)S(1)}, f32[7,32,384]{2,1,0:T(8,128)S(1)}, u32[]{:S(2)}, u32[]{:S(2)}) collective-permute-start(f32[7,32,384]{2,1,0:T(8,128)S(1)} %get-tuple-element.58), channel_id=1, source_target_pairs={{0,1},{1,2},{2,3},{3,4},{4,5},{5,6},{6,7},{8,9},{9,10},{10,11},{11... | collective-permute-start | bytes 1032200 | tf_op jit(solution)/shard_map/ppermute | solution.py:445
  86.2 9.1 %collective-permute-start.9 = (f32[7,32,384]{2,1,0:T(8,128)S(1)}, f32[7,32,384]{2,1,0:T(8,128)S(1)}, u32[]{:S(2)}, u32[]{:S(2)}) collective-permute-start(f32[7,32,384]{2,1,0:T(8,128)S(1)} %get-tuple-element.60), channel_id=1, source_target_pairs={{1,0},{2,1},{3,2},{4,3},{5,4},{6,5},{7,6},{9,8},{10,9},{11,10},{12... | collective-permute-start | bytes 1032200 | tf_op jit(solution)/shard_map/ppermute | solution.py:446
  98.4 13.7 %collective-permute-start.10 = (f32[7,32,384]{2,1,0:T(8,128)S(1)}, f32[7,32,384]{2,1,0:T(8,128)S(1)}, u32[]{:S(2)}, u32[]{:S(2)}) collective-permute-start(f32[7,32,384]{2,1,0:T(8,128)S(1)} %get-tuple-element.64), channel_id=1, source_target_pairs={{0,1},{1,2},{2,3},{3,4},{4,5},{5,6},{6,7},{8,9},{9,10},{10,11},{11... | collective-permute-start | bytes 1032200 | tf_op jit(solution)/shard_map/ppermute | solution.py:445
  102.6 9.4 %collective-permute-start.11 = (f32[7,32,384]{2,1,0:T(8,128)S(1)}, f32[7,32,384]{2,1,0:T(8,128)S(1)}, u32[]{:S(2)}, u32[]{:S(2)}) collective-permute-start(f32[7,32,384]{2,1,0:T(8,128)S(1)} %get-tuple-element.66), channel_id=1, source_target_pairs={{1,0},{2,1},{3,2},{4,3},{5,4},{6,5},{7,6},{9,8},{10,9},{11,10},{12... | collective-permute-start | bytes 1032200 | tf_op jit(solution)/shard_map/ppermute | solution.py:446
  116.8 25.9 %collective-permute-start.12 = (f32[7,32,384]{2,1,0:T(8,128)}, f32[7,32,384]{2,1,0:T(8,128)S(1)}, u32[]{:S(2)}, u32[]{:S(2)}) collective-permute-start(f32[7,32,384]{2,1,0:T(8,128)} %get-tuple-element.70), channel_id=1, source_target_pairs={{0,1},{1,2},{2,3},{3,4},{4,5},{5,6},{6,7},{8,9},{9,10},{10,11},{11... | collective-permute-start | bytes 1032200 | tf_op jit(solution)/shard_map/ppermute | solution.py:445
  121.1 21.7 %collective-permute-start.13 = (f32[7,32,384]{2,1,0:T(8,128)}, f32[7,32,384]{2,1,0:T(8,128)S(1)}, u32[]{:S(2)}, u32[]{:S(2)}) collective-permute-start(f32[7,32,384]{2,1,0:T(8,128)} %get-tuple-element.72), channel_id=1, source_target_pairs={{1,0},{2,1},{3,2},{4,3},{5,4},{6,5},{7,6},{9,8},{10,9},{11,10},{12... | collective-permute-start | bytes 1032200 | tf_op jit(solution)/shard_map/ppermute | solution.py:446
  124.7 60.2 %all-to-all-start.2 = ((f32[16,2,16,384]{3,2,1,0:T(8,128)}), f32[16,2,16,384]{3,2,1,0:T(8,128)}, u32[]{:S(2)}, u32[]{:S(2)}) async-start(f32[16,2,16,384]{3,2,1,0:T(8,128)} %light_sum.1), calls=%async_computation.2 | async-start | bytes 1572864 | tf_op jit(solution)/shard_map/all_to_all | solution.py:465
  146.1 12.2 %collective-permute-start.14 = (f32[7,32,384]{2,1,0:T(8,128)S(1)}, f32[7,32,384]{2,1,0:T(8,128)S(1)}, u32[]{:S(2)}, u32[]{:S(2)}) collective-permute-start(f32[7,32,384]{2,1,0:T(8,128)S(1)} %get-tuple-element.76), channel_id=1, source_target_pairs={{0,1},{1,2},{2,3},{3,4},{4,5},{5,6},{6,7},{8,9},{9,10},{10,11},{11... | collective-permute-start | bytes 1032200 | tf_op jit(solution)/shard_map/ppermute | solution.py:445
  150.1 8.2 %collective-permute-start.15 = (f32[7,32,384]{2,1,0:T(8,128)S(1)}, f32[7,32,384]{2,1,0:T(8,128)S(1)}, u32[]{:S(2)}, u32[]{:S(2)}) collective-permute-start(f32[7,32,384]{2,1,0:T(8,128)S(1)} %get-tuple-element.78), channel_id=1, source_target_pairs={{1,0},{2,1},{3,2},{4,3},{5,4},{6,5},{7,6},{9,8},{10,9},{11,10},{12... | collective-permute-start | bytes 1032200 | tf_op jit(solution)/shard_map/ppermute | solution.py:446
  162.9 17.4 %collective-permute-start.16 = (f32[7,32,384]{2,1,0:T(8,128)}, f32[7,32,384]{2,1,0:T(8,128)}, u32[]{:S(2)}, u32[]{:S(2)}) collective-permute-start(f32[7,32,384]{2,1,0:T(8,128)} %get-tuple-element.82), channel_id=1, source_target_pairs={{0,1},{1,2},{2,3},{3,4},{4,5},{5,6},{6,7},{8,9},{9,10},{10,11},{11... | collective-permute-start | bytes 1032200 | tf_op jit(solution)/shard_map/ppermute | solution.py:445
  168.2 12.2 %collective-permute-start.17 = (f32[7,32,384]{2,1,0:T(8,128)}, f32[7,32,384]{2,1,0:T(8,128)}, u32[]{:S(2)}, u32[]{:S(2)}) collective-permute-start(f32[7,32,384]{2,1,0:T(8,128)} %get-tuple-element.84), channel_id=1, source_target_pairs={{1,0},{2,1},{3,2},{4,3},{5,4},{6,5},{7,6},{9,8},{10,9},{11,10},{12... | collective-permute-start | bytes 1032200 | tf_op jit(solution)/shard_map/ppermute | solution.py:446
  (47 other events, 186.2 us)

commit v2 on v1

v2 whole, which is shorter than its diff:
```python
import jax
import jax.numpy as jnp
import numpy as np
from jax import lax
from jax.experimental import pallas as pl
from jax.experimental.pallas import tpu as pltpu
from jax.sharding import PartitionSpec as P

MUTE = 6
COEFFS = (1225.0 / 1024.0, -245.0 / 3072.0, 49.0 / 5120.0, -5.0 / 7168.0)
DAMP = 0.1
HALO = 7
SLOTS = 6
FIELDS = 16
F32 = jnp.float32
BF16 = jnp.bfloat16
PARAMS = pltpu.CompilerParams(vmem_limit_bytes=10 * 1024 * 1024)


def shape_of(*dims, dtype=F32):
    return jax.ShapeDtypeStruct(dims, dtype)


def split2(x):
    high = x.astype(BF16)
    return high, (x - high.astype(F32)).astype(BF16)


def split3(x):
    high = x.astype(BF16)
    rest = x - high.astype(F32)
    mid = rest.astype(BF16)
    return high, mid, (rest - mid.astype(F32)).astype(BF16)


def contract_last(left, right, **kwargs):
    return lax.dot_general(
        left, right, (((1,), (1,)), ((), ())), preferred_element_type=F32, **kwargs
    )


def prep_kernel(
    traces_ref, kernel_ref, target_ref, cell_ref, p_ref, b_ref,
    send_ref, right_ref, left_ref, sems, *, nz,
):
    nx = p_ref.shape[0]
    copies = [
        pltpu.make_async_copy(p_ref.at[pl.ds(nx - HALO, HALO)], right_ref.at[pl.ds(0, HALO)], sems.at[0]),
        pltpu.make_async_copy(b_ref.at[pl.ds(nx - 4, 4)], right_ref.at[pl.ds(HALO, 4)], sems.at[1]),
        pltpu.make_async_copy(p_ref.at[pl.ds(0, HALO)], left_ref.at[pl.ds(0, HALO)], sems.at[2]),
        pltpu.make_async_copy(b_ref.at[pl.ds(0, 3)], left_ref.at[pl.ds(HALO, 3)], sems.at[3]),
    ]
    for copy in copies:
        copy.start()
    rows = traces_ref.shape[0]
    values = contract_last(kernel_ref[...], traces_ref[...], precision=lax.Precision.HIGHEST)
    lane = lax.broadcasted_iota(jnp.int32, (128, rows), 0)
    hit = target_ref[...] == lane
    onehot = jnp.where(hit, 1.0, 0.0)
    upper = (
        lax.broadcasted_iota(jnp.int32, (rows, rows), 0)
        <= lax.broadcasted_iota(jnp.int32, (rows, rows), 1)
    )
    running = jnp.dot(
        onehot.astype(BF16),
        jnp.where(upper, 1.0, 0.0).astype(BF16),
        preferred_element_type=F32,
    )
    slot = (jnp.sum(jnp.where(hit, running, 0.0), axis=0, keepdims=True) - 1.0).astype(jnp.int32)
    cell = cell_ref[...]
    entries = jnp.where(lane % FIELDS == 8, (cell // nz).astype(F32), values)
    entries = jnp.where(lane % FIELDS == 9, (cell % nz).astype(F32), entries)
    entries = jnp.where(lane // FIELDS == slot, entries, 0.0)
    packed = jnp.zeros((128, 128), F32)
    for piece in split3(entries):
        packed = packed + contract_last(onehot.astype(BF16), piece)
    send_ref[...] = packed
    for copy in copies:
        copy.wait()


def prep(traces, target, cell, current, b1):
    nx, ny, nz = current.shape
    samples = traces.shape[1]
    position = np.arange(samples, dtype=np.float32)[None, :]
    centers = (np.arange(8, dtype=np.float32)[:, None] + np.float32(0.5)) * np.float32(samples / 8)
    kernel = (0.25 * np.exp(-np.abs(position - centers) / np.float32(samples / 8.0))).astype(np.float32)
    tiled = np.zeros((128, samples), np.float32)
    for slot in range(SLOTS):
        tiled[slot * FIELDS : slot * FIELDS + 8] = kernel
    vmem = pl.BlockSpec(memory_space=pltpu.VMEM)
    far = pl.BlockSpec(memory_space=pl.ANY)
    return pl.pallas_call(
        lambda *refs: prep_kernel(*refs, nz=nz),
        in_specs=[vmem] * 4 + [far] * 2,
        out_specs=[vmem] * 3,
        out_shape=[shape_of(128, 128), shape_of(HALO + 4, ny, nz), shape_of(HALO + 3, ny, nz)],
        scratch_shapes=[pltpu.SemaphoreType.DMA((4,))],
        compiler_params=PARAMS,
        name="prep",
    )(traces, jnp.asarray(tiled), target, cell, current, b1)


def fill_columns(got_ref, spread_ref, moment, nz):
    zlane = lax.broadcasted_iota(jnp.int32, (128, nz), 1)
    for slot in range(SLOTS):
        base = slot * FIELDS
        third = got_ref[:, base + 9 : base + 10].astype(jnp.int32)
        value = got_ref[:, base + moment : base + moment + 1]
        spread = jnp.where(third == zlane, value, 0.0)
        high, low = split2(spread)
        spread_ref[0, slot * 128 : (slot + 1) * 128, :] = high
        spread_ref[1, slot * 128 : (slot + 1) * 128, :] = low


def inject_rows(turned, spread_ref, first_row, count):
    row = first_row + lax.broadcasted_iota(jnp.int32, (count, 128), 0)
    picks = []
    for slot in range(SLOTS):
        base = slot * FIELDS
        line = turned[base + 8 : base + 9, :].astype(jnp.int32)
        picks.append(jnp.where(line == row, 1.0, 0.0).astype(BF16))
    pick = jnp.concatenate(picks, axis=1)
    return jnp.dot(pick, spread_ref[0], preferred_element_type=F32) + jnp.dot(
        pick, spread_ref[1], preferred_element_type=F32
    )


GROUP = 4


def inject_group(turned, spread_ref, out_ref, start, base_ref):
    ny = out_ref.shape[1]
    added = inject_rows(turned, spread_ref, start * ny, GROUP * ny)
    for x in range(GROUP):
        piece = added[x * ny : (x + 1) * ny]
        out_ref[start + x] = piece if base_ref is None else base_ref[start + x] + piece


def first_inject_kernel(got_ref, local_ref, out_ref, turned_ref, spread_ref):
    nx, ny, nz = local_ref.shape
    turned_ref[...] = got_ref[...].T
    fill_columns(got_ref, spread_ref, 0, nz)
    turned = turned_ref[...]
    for start in range(0, nx, GROUP):
        inject_group(turned, spread_ref, out_ref, start, local_ref)


def first_inject(got, local):
    nx, ny, nz = local.shape
    return pl.pallas_call(
        first_inject_kernel,
        out_shape=[shape_of(nx, ny, nz), shape_of(128, 128)],
        scratch_shapes=[pltpu.VMEM((2, SLOTS * 128, nz), BF16)],
        compiler_params=PARAMS,
        name="first_inject",
    )(got, local)


def weighted(pairs):
    total = None
    for k, (ahead, behind) in enumerate(pairs):
        term = COEFFS[k] * (ahead - behind)
        total = term if total is None else total + term
    return total


def along_lanes(tiles, amount, lane):
    if amount == 0:
        return tiles
    count = len(tiles)
    turned = [pltpu.roll(tile, (-amount) % 128, 1) for tile in tiles]
    zero = jnp.zeros_like(tiles[0])
    if amount > 0:
        keep = lane < 128 - amount
        return [
            jnp.where(keep, turned[c], turned[c + 1] if c + 1 < count else zero)
            for c in range(count)
        ]
    keep = lane >= -amount
    return [jnp.where(keep, turned[c], turned[c - 1] if c else zero) for c in range(count)]


def third_derivative(tiles, offset, lane):
    moved = {d: along_lanes(tiles, d, lane) for d in range(offset - 4, offset + 4)}
    return [
        weighted([(moved[offset - 1 + k][c], moved[offset - k][c]) for k in range(1, 5)])
        for c in range(len(tiles))
    ]


def second_derivative(ref, where, first, ny):
    return weighted(
        [
            (
                ref[where, 7 + first + k : 7 + first + k + ny, :],
                ref[where, 8 + first - k : 8 + first - k + ny, :],
            )
            for k in range(1, 5)
        ]
    )


def divergence_plane(p_ref, b2_ref, b3_ref, x, ps_ref, qs_ref, index):
    ny, nz = p_ref.shape[1:]
    count = nz // 128
    lane = lax.broadcasted_iota(jnp.int32, (8, 128), 1)
    across = []
    for c in range(count):
        where = index * count + c
        lanes = slice(c * 128, c * 128 + 128)
        ps_ref[where, 8 : 8 + ny, :] = p_ref[x, :, lanes]
        qs_ref[where, 8 : 8 + ny, :] = b2_ref[x, :, lanes] * second_derivative(ps_ref, where, 1, ny)
        across.append(second_derivative(qs_ref, where, 0, ny))
    for band in range(ny // 8):
        rows = slice(band * 8, band * 8 + 8)
        tiles = [p_ref[x, rows, c * 128 : c * 128 + 128] for c in range(count)]
        faces = third_derivative(tiles, 1, lane)
        faces = [faces[c] * b3_ref[x, rows, c * 128 : c * 128 + 128] for c in range(count)]
        along = third_derivative(faces, 0, lane)
        for c in range(count):
            yield rows, slice(c * 128, c * 128 + 128), across[c][rows] + along[c]


def clear_edges(ps_ref, qs_ref, ny):
    zero = jnp.zeros((ps_ref.shape[0], 8, 128), F32)
    for ref in (ps_ref, qs_ref):
        ref[:, 0:8, :] = zero
        ref[:, 8 + ny : 16 + ny, :] = zero


def first_local_kernel(p_ref, k_ref, b2_ref, b3_ref, out_ref, ps_ref, qs_ref):
    nx, ny, nz = p_ref.shape
    clear_edges(ps_ref, qs_ref, ny)

    def planes(group, carry):
        for index in range(GROUP):
            x = group * GROUP + index
            for rows, lanes, total in divergence_plane(p_ref, b2_ref, b3_ref, x, ps_ref, qs_ref, index):
                out_ref[x, rows, lanes] = k_ref[x, rows, lanes] * total
        return carry

    lax.fori_loop(0, nx // GROUP, planes, 0)


def shift_scratch(ny, nz):
    return pltpu.VMEM((GROUP * (nz // 128), ny + 16, 128), F32)


def first_local(current, stiffness, b2, b3):
    nx, ny, nz = current.shape
    return pl.pallas_call(
        first_local_kernel,
        out_shape=shape_of(nx, ny, nz),
        scratch_shapes=[shift_scratch(ny, nz)] * 2,
        compiler_params=PARAMS,
        name="first_local",
    )(current, stiffness, b2, b3)


def make_local_kernel(moment):
    def local_kernel(*refs):
        p_ref, k_ref, b2_ref, b3_ref, f_ref, change_ref = refs[:6]
        refs = refs[6:]
        if moment > 1:
            image_ref, refs = refs[0], refs[1:]
        got_ref, turned_ref, out_ref, image_out_ref, ps_ref, qs_ref, spread_ref, add_ref = refs
        nx, ny, nz = p_ref.shape
        clear_edges(ps_ref, qs_ref, ny)
        fill_columns(got_ref, spread_ref, moment, nz)
        turned = turned_ref[...]

        def planes(group, carry):
            added = inject_rows(turned, spread_ref, group * (GROUP * ny), GROUP * ny)
            add_ref[...] = added
            for index in range(GROUP):
                x = group * GROUP + index
                for rows, lanes, total in divergence_plane(p_ref, b2_ref, b3_ref, x, ps_ref, qs_ref, index):
                    low = index * ny + rows.start
                    out_ref[x, rows, lanes] = k_ref[x, rows, lanes] * total + add_ref[low : low + 8, lanes]
                image = f_ref[moment - 1, x].astype(F32) * change_ref[x]
                if moment > 1:
                    image = image + image_ref[x]
                image_out_ref[x] = image
            return carry

        lax.fori_loop(0, nx // GROUP, planes, 0)

    return local_kernel


def local_step(moment, current, stiffness, b2, b3, forward, change, image, got, turned):
    nx, ny, nz = current.shape
    images = [image] if moment > 1 else []
    return pl.pallas_call(
        make_local_kernel(moment),
        out_shape=[shape_of(nx, ny, nz)] * 2,
        scratch_shapes=[shift_scratch(ny, nz)] * 2
        + [pltpu.VMEM((2, SLOTS * 128, nz), BF16), pltpu.VMEM((GROUP * ny, nz), F32)],
        compiler_params=PARAMS,
        name="local_step",
    )(current, stiffness, b2, b3, forward, change, *images, got, turned)


def change_column(p_refs, b_refs, k_ref, local_ref, rows, lanes):
    pl_ref, pm_ref, pr_ref = p_refs
    bl_ref, bm_ref, br_ref = b_refs
    nx = pm_ref.shape[0]

    def cell(i):
        if i < 0:
            return pl_ref[HALO + i, rows, lanes]
        if i >= nx:
            return pr_ref[i - nx, rows, lanes]
        return pm_ref[i, rows, lanes]

    def face(i):
        if i < 0:
            return bl_ref[HALO + 4 + i, rows, lanes]
        if i >= nx:
            return br_ref[HALO + i - nx, rows, lanes]
        return bm_ref[i, rows, lanes]

    cells = {i: cell(i) for i in range(-HALO, 0)}
    fluxes = {}
    for ahead in range(0, nx + HALO):
        cells[ahead] = cell(ahead)
        j = ahead - 4
        if j >= -4:
            fluxes[j] = face(j) * weighted([(cells[j + k], cells[j + 1 - k]) for k in range(1, 5)])
        i = j - 3
        if i >= 0:
            total = weighted([(fluxes[i + k - 1], fluxes[i - k]) for k in range(1, 5)])
            yield i, cells[i], local_ref[i, rows, lanes] + k_ref[i, rows, lanes] * total


def columns(ny, nz):
    for band in range(ny // 8):
        for c in range(nz // 128):
            yield slice(band * 8, band * 8 + 8), slice(c * 128, c * 128 + 128)


def update_kernel(
    pl_ref, pm_ref, pr_ref, bl_ref, bm_ref, br_ref, k_ref, local_ref, before_ref,
    next_ref, change_ref, head_ref, tail_ref,
):
    nx, ny, nz = pm_ref.shape
    for rows, lanes in columns(ny, nz):
        for i, now, change in change_column(
            (pl_ref, pm_ref, pr_ref), (bl_ref, bm_ref, br_ref), k_ref, local_ref, rows, lanes
        ):
            following = 2.0 * now - before_ref[i, rows, lanes] + change
            next_ref[i, rows, lanes] = following
            change_ref[i, rows, lanes] = change
            if i < HALO:
                head_ref[i, rows, lanes] = following
            if i >= nx - HALO:
                tail_ref[i - (nx - HALO), rows, lanes] = following


def last_kernel(
    place_ref, first_ref, pl_ref, pm_ref, pr_ref, bl_ref, bm_ref, br_ref, k_ref, local_ref,
    before_ref, image_ref, f_ref, next_ref, muted_ref, kept_ref,
):
    nx, ny, nz = pm_ref.shape
    steps = f_ref.shape[0]
    second = lax.broadcasted_iota(jnp.int32, (8, 128), 0).astype(F32)
    third = lax.broadcasted_iota(jnp.int32, (8, 128), 1).astype(F32)
    first_at = (first_ref[0] - place_ref[0, 0]).astype(F32)
    second_at = place_ref[0, 1].astype(F32)
    third_at = place_ref[0, 2].astype(F32)
    for rows, lanes in columns(ny, nz):
        flat = (second + (float(rows.start) - second_at)) ** 2 + (
            third + (float(lanes.start) - third_at)
        ) ** 2
        for i, now, change in change_column(
            (pl_ref, pm_ref, pr_ref), (bl_ref, bm_ref, br_ref), k_ref, local_ref, rows, lanes
        ):
            next_ref[i, rows, lanes] = 2.0 * now - before_ref[i, rows, lanes] + change
            image = image_ref[i, rows, lanes] + f_ref[steps - 1, i, rows, lanes].astype(F32) * change
            distance = (first_at + float(i)) ** 2 + flat
            kept_ref[i, rows, lanes] = (1.0 - jnp.exp(distance * (-1.0 / (2.0 * MUTE * MUTE)))) * image
    for y in range(ny):
        muted_ref[y // 2, y % 2, :, :] = kept_ref[:, y, :]


def update_step(halos, current, b1_halos, b1, stiffness, local, before):
    nx, ny, nz = current.shape
    return pl.pallas_call(
        update_kernel,
        out_shape=[shape_of(nx, ny, nz)] * 2 + [shape_of(HALO, ny, nz)] * 2,
        compiler_params=PARAMS,
        name="update_step",
    )(halos[0], current, halos[1], b1_halos[0], b1, b1_halos[1], stiffness, local, before)


def last_step(place, first, halos, current, b1_halos, b1, stiffness, local, before, image, forward):
    nx, ny, nz = current.shape
    vmem = pl.BlockSpec(memory_space=pltpu.VMEM)
    smem = pl.BlockSpec(memory_space=pltpu.SMEM)
    return pl.pallas_call(
        last_kernel,
        in_specs=[smem] * 2 + [vmem] * 11,
        out_specs=[vmem] * 2,
        out_shape=[shape_of(nx, ny, nz), shape_of(ny // 2, 2, nx, nz)],
        scratch_shapes=[pltpu.VMEM((nx, ny, nz), F32)],
        compiler_params=PARAMS,
        name="last_step",
    )(
        place, first, halos[0], current, halos[1], b1_halos[0], b1, b1_halos[1], stiffness, local,
        before, image, forward,
    )


def light_kernel(f_ref, out_ref, kept_ref):
    steps, nx, ny, nz = f_ref.shape
    for i in range(nx):
        total = None
        for t in range(steps):
            frame = f_ref[t, i].astype(F32)
            total = frame * frame if total is None else total + frame * frame
        kept_ref[i] = total
    for y in range(ny):
        out_ref[y // 2, y % 2, :, :] = kept_ref[:, y, :]


def light_sum(forward):
    steps, nx, ny, nz = forward.shape
    return pl.pallas_call(
        light_kernel,
        out_shape=shape_of(ny // 2, 2, nx, nz),
        scratch_shapes=[pltpu.VMEM((nx, ny, nz), F32)],
        compiler_params=PARAMS,
        name="light_sum",
    )(forward)


def quotient_kernel(image_ref, light_ref, out_ref, *, scale):
    nz = image_ref.shape[-1]
    for side in range(2):
        image = image_ref[0, side]
        for shot in range(1, image_ref.shape[0]):
            image = image + image_ref[shot, side]
        out_ref[:, side * nz : (side + 1) * nz] = image / (light_ref[0, side] * scale + DAMP)


def quotient(images, light, scale):
    _, _, nx, nz = images.shape
    return pl.pallas_call(
        lambda *refs: quotient_kernel(*refs, scale=scale),
        out_shape=shape_of(nx, 2 * nz),
        compiler_params=PARAMS,
        name="quotient",
    )(images, light)


def exchange(head, tail):
    count = lax.axis_size("sub")
    from_left = lax.ppermute(tail, "sub", [(i, i + 1) for i in range(count - 1)])
    from_right = lax.ppermute(head, "sub", [(i + 1, i) for i in range(count - 1)])
    return from_left, from_right


def local(
    stiffness, b1, b2, b3, adjoint_before, adjoint_current, forward_field,
    traces, receiver_target, receiver_cell, source_cell,
):
    both = ("shot", "sub")
    steps = forward_field.shape[1]
    nx = stiffness.shape[0]
    rows = traces.shape[0]
    forward = forward_field[0]
    before = adjoint_before[0]
    current = adjoint_current[0]

    send, right, left = prep(
        traces, receiver_target.reshape(1, rows), receiver_cell.reshape(1, rows), current, b1
    )
    halos = exchange(left, right)
    b1_halos = halos
    got = lax.all_to_all(send, both, split_axis=0, concat_axis=0, tiled=True)
    light = lax.psum_scatter(light_sum(forward), "shot", scatter_dimension=0, tiled=True)
    nearby = first_local(current, stiffness, b2, b3)
    nearby, turned = first_inject(got, nearby)

    image = None
    for moment in range(steps - 1):
        following, change, head, tail = update_step(
            halos, current, b1_halos, b1, stiffness, nearby, before
        )
        halos = exchange(head, tail)
        before, current = current, following
        nearby, image = local_step(
            moment + 1, current, stiffness, b2, b3, forward, change, image, got, turned
        )
    first = (lax.axis_index("sub") * nx).astype(jnp.int32)[None]
    following, muted = last_step(
        source_cell, first, halos, current, b1_halos, b1, stiffness, nearby, before, image, forward
    )
    images = lax.all_to_all(muted, "shot", split_axis=0, concat_axis=0, tiled=True)
    gradient = quotient(images, light, 1.0 / (steps * lax.axis_size("shot")))
    return gradient, current[None], following[None]


def solution(mesh):
    placed = (
        P("sub", None, None),
        P("sub", None, None),
        P("sub", None, None),
        P("sub", None, None),
        P("shot", "sub", None, None),
        P("shot", "sub", None, None),
        P("shot", None, "sub", None, None),
        P(("shot", "sub"), None),
        P(("shot", "sub"), None),
        P(("shot", "sub")),
        P("shot", None),
    )
    return jax.shard_map(
        local,
        mesh=mesh,
        in_specs=placed,
        out_specs=(P("sub", "shot"), P("shot", "sub", None, None), P("shot", "sub", None, None)),
        check_vma=False,
    )
```

time: 212 us -> 216 us (1.019)
  blocking collectives: 22.4 us -> 0 us
  waiting for transfers between devices: 2.99 us -> 16.3 us
  between operations: 1.3 us -> 14.6 us
  Pallas kernels: 81.2 us -> 86 us
  starting transfers between devices: 63.4 us -> 61.1 us
    all_to_all x1 -> x0, blocking collectives: 22.4 us -> none  [local(): lax.all_to_all(muted, 'shot', split_axis=0, concat_axis=0, tiled=True)]
    unnamed x0 -> x2, waiting for transfers between devices: none -> 11.7 us
    pallas_call x19, Pallas kernels: 79.4 us -> 85.3 us  [the longest x7 53.2 us: local_step(): pl.pallas_call(make_local_kernel(moment), out_shape=[shape_of(nx, ny, nz)...]
    slice x3 -> x0, local copies, waits for them, and re-layouts: 5.32 us -> none  [the longest x2 3.19 us: local(): b1_halos = exchange(b1[:3], b1[nx - 4:])]
    unnamed x103 -> x100, local copies, waits for them, and re-layouts: 30.2 us -> 35.4 us
    all_to_all x1, waiting for transfers between devices: 0.01 us -> 4.59 us  [local(): lax.all_to_all(muted, 'shot', split_axis=0, concat_axis=0, tiled=True)]
    ppermute x9 -> x8, starting transfers between devices: 33.4 us -> 29.7 us  [exchange(): lax.ppermute(tail, 'sub', [(i, i + 1) for i in range(count - 1)])]
    all_to_all x1, waiting for transfers between devices: 2.94 us -> 0.01 us  [local(): got = lax.all_to_all(send, both, split_axis=0, concat_axis=0, tiled=True)]
  transfers between devices with their start and end apart: 20 -> 19, of which waited for: 1 -> 2; matrix products, arithmetic and copies ran while one was open for 3% -> 0% of each run, Pallas kernels for 30% -> 33%
where the time goes in v2:
time: 216 us; the launch traced here: 213 us
  Pallas kernels  86 us (40%)
  starting transfers between devices  61.1 us (28%)
  local copies, waits for them, and re-layouts  35.4 us (16%)
  waiting for transfers between devices  16.3 us (8%)
  between operations  14.6 us (7%)
    pallas_call x7, Pallas kernels, local_step(): pl.pallas_call(make_local_kernel(moment), out_shape=[shape_of(nx, ny, nz)...  53.2 us
    unnamed x100, local copies, waits for them, and re-layouts  35.4 us
    ppermute x8, starting transfers between devices, exchange(): lax.ppermute(tail, 'sub', [(i, i + 1) for i in range(count - 1)])  29.7 us
    pallas_call x7, Pallas kernels, update_step(): pl.pallas_call(update_kernel, out_shape=[shape_of(nx, ny, nz)] * 2 + [sha...  16.8 us
    all_to_all x1, starting transfers between devices, local(): got = lax.all_to_all(send, both, split_axis=0, concat_axis=0, tiled=True)  13.3 us
    unnamed x2, waiting for transfers between devices  11.7 us
    ppermute x8, starting transfers between devices, exchange(): lax.ppermute(head, 'sub', [(i + 1, i) for i in range(count - 1)])  10.7 us
    all_to_all x1, starting transfers between devices, local(): lax.all_to_all(muted, 'shot', split_axis=0, concat_axis=0, tiled=True)  7.26 us
  transfers between devices with their start and end apart: 19, of which 2 were waited for; matrix products, arithmetic and copies ran while one was open for 0% of the time, Pallas kernels for 33%

profile of v2, /device:TPU:0, one launch (start us, length us, event | category | flops | bytes accessed | tf_op | source)
XLA Modules:
  0.0 213.4 jit_solution(13512704868469604306)
XLA Ops:
  12.7 2.9 %prep.1 = (f32[128,128]{1,0:T(8,128)}, f32[11,32,384]{2,1,0:T(8,128)}, f32[10,32,384]{2,1,0:T(8,128)}) custom-call(f32[512,256]{1,0:T(8,128)S(1)} %copy-done.44, f32[128,256]{1,0:T(8,128)S(1)} %copy-done.45, s32[1,512]{1,0:T(1,128)S(1)} %bitcast.36, s32[1,512]{1,0:T(1,128)S(1)} %bitcast.37, f32[16,32,384]{2,1,0:T(8,128)S(1)} %bitcast.22, ...), custom_call_target="tpu_custom_call" | custom-call | tf_op jit(solution)/shard_map/prep/pallas_call | solution.py:93
  19.0 13.3 %all-to-all-start = ((f32[128,1,128]{2,1,0:T(1,128)}), f32[128,1,128]{2,1,0:T(1,128)S(1)}, u32[]{:S(2)}, u32[]{:S(2)}) async-start(f32[128,1,128]{2,1,0:T(1,128)} %bitcast.5), calls=%async_computation | async-start | bytes 131072 | tf_op jit(solution)/shard_map/all_to_all | solution.py:481
  36.9 7.1 %first_local.1.local_ref = f32[16,32,384]{2,1,0:T(8,128)S(1)} custom-call(f32[16,32,384]{2,1,0:T(8,128)S(1)} %bitcast.23, f32[16,32,384]{2,1,0:T(8,128)S(1)} %copy-done.1, f32[16,32,384]{2,1,0:T(8,128)S(1)} %copy-done.13, f32[16,32,384]{2,1,0:T(8,128)S(1)} %copy-done.17), custom_call_target="tpu_custom_call" | custom-call | tf_op jit(solution)/shard_map/first_local/pallas_call | solution.py:252
  50.2 2.5 %update_step.7 = (f32[16,32,384]{2,1,0:T(8,128)S(1)}, f32[16,32,384]{2,1,0:T(8,128)S(1)}, f32[7,32,384]{2,1,0:T(8,128)S(1)}, f32[7,32,384]{2,1,0:T(8,128)S(1)}) custom-call(f32[11,32,384]{2,1,0:T(8,128)} %collective-permute-done.pl_ref.bl_ref, f32[16,32,384]{2,1,0:T(8,128)S(1)} %bitcast.24, f32[10,32,384]{2,1,0:T(8,128)} %collective-permute-done.1.pr_ref.br_ref, ...), custom_call_target="tpu_custom_call" | custom-call | tf_op jit(solution)/shard_map/update_step/pallas_call | solution.py:389
  55.4 7.6 %local_step.7 = (f32[16,32,384]{2,1,0:T(8,128)S(1)}, f32[16,32,384]{2,1,0:T(8,128)S(1)}) custom-call(f32[16,32,384]{2,1,0:T(8,128)S(1)} %get-tuple-element.57.refs_0_.pm_ref.before_ref, f32[16,32,384]{2,1,0:T(8,128)S(1)} %copy-done.3, f32[16,32,384]{2,1,0:T(8,128)S(1)} %copy-done.14, f32[16,32,384]{2,1,0:T(8,128)S(1)} %copy-done.18, ...), custom_call_target="tpu_custom_call" | custom-call | tf_op jit(solution)/shard_map/local_step/pallas_call | solution.py:295
  65.0 4.2 %collective-permute-start.4 = (f32[7,32,384]{2,1,0:T(8,128)S(1)}, f32[7,32,384]{2,1,0:T(8,128)S(1)}, u32[]{:S(2)}, u32[]{:S(2)}) collective-permute-start(f32[7,32,384]{2,1,0:T(8,128)S(1)} %get-tuple-element.62), channel_id=1, source_target_pairs={{0,1},{1,2},{2,3},{3,4},{4,5},{5,6},{6,7},{8,9},{9,10},{10,11},{11... | collective-permute-start | bytes 1032200 | tf_op jit(solution)/shard_map/ppermute | solution.py:459
  70.5 7.6 %local_step.8 = (f32[16,32,384]{2,1,0:T(8,128)S(1)}, f32[16,32,384]{2,1,0:T(8,128)S(1)}) custom-call(f32[16,32,384]{2,1,0:T(8,128)S(1)} %get-tuple-element.63.refs_0_.pm_ref.before_ref, f32[16,32,384]{2,1,0:T(8,128)S(1)} %copy-done.3, f32[16,32,384]{2,1,0:T(8,128)S(1)} %copy-done.14, f32[16,32,384]{2,1,0:T(8,128)S(1)} %copy-done.18, ...), custom_call_target="tpu_custom_call" | custom-call | tf_op jit(solution)/shard_map/local_step/pallas_call | solution.py:295
  80.2 4.3 %collective-permute-start.6 = (f32[7,32,384]{2,1,0:T(8,128)S(1)}, f32[7,32,384]{2,1,0:T(8,128)S(1)}, u32[]{:S(2)}, u32[]{:S(2)}) collective-permute-start(f32[7,32,384]{2,1,0:T(8,128)S(1)} %get-tuple-element.68), channel_id=1, source_target_pairs={{0,1},{1,2},{2,3},{3,4},{4,5},{5,6},{6,7},{8,9},{9,10},{10,11},{11... | collective-permute-start | bytes 1032200 | tf_op jit(solution)/shard_map/ppermute | solution.py:459
  86.0 7.6 %local_step.9 = (f32[16,32,384]{2,1,0:T(8,128)S(1)}, f32[16,32,384]{2,1,0:T(8,128)S(1)}) custom-call(f32[16,32,384]{2,1,0:T(8,128)S(1)} %get-tuple-element.69.refs_0_.pm_ref.before_ref, f32[16,32,384]{2,1,0:T(8,128)S(1)} %copy-done.3, f32[16,32,384]{2,1,0:T(8,128)S(1)} %copy-done.14, f32[16,32,384]{2,1,0:T(8,128)S(1)} %copy-done.18, ...), custom_call_target="tpu_custom_call" | custom-call | tf_op jit(solution)/shard_map/local_step/pallas_call | solution.py:295
  95.7 4.3 %collective-permute-start.8 = (f32[7,32,384]{2,1,0:T(8,128)S(1)}, f32[7,32,384]{2,1,0:T(8,128)S(1)}, u32[]{:S(2)}, u32[]{:S(2)}) collective-permute-start(f32[7,32,384]{2,1,0:T(8,128)S(1)} %get-tuple-element.74), channel_id=1, source_target_pairs={{0,1},{1,2},{2,3},{3,4},{4,5},{5,6},{6,7},{8,9},{9,10},{10,11},{11... | collective-permute-start | bytes 1032200 | tf_op jit(solution)/shard_map/ppermute | solution.py:459
  101.2 7.6 %local_step.10 = (f32[16,32,384]{2,1,0:T(8,128)S(1)}, f32[16,32,384]{2,1,0:T(8,128)S(1)}) custom-call(f32[16,32,384]{2,1,0:T(8,128)S(1)} %get-tuple-element.75.refs_0_.pm_ref.before_ref, f32[16,32,384]{2,1,0:T(8,128)S(1)} %copy-done.3, f32[16,32,384]{2,1,0:T(8,128)S(1)} %copy-done.14, f32[16,32,384]{2,1,0:T(8,128)S(1)} %copy-done.18, ...), custom_call_target="tpu_custom_call" | custom-call | tf_op jit(solution)/shard_map/local_step/pallas_call | solution.py:295
  109.8 2.9 %update_step.11 = (f32[16,32,384]{2,1,0:T(8,128)S(1)}, f32[16,32,384]{2,1,0:T(8,128)S(1)}, f32[7,32,384]{2,1,0:T(8,128)}, f32[7,32,384]{2,1,0:T(8,128)}) custom-call(f32[7,32,384]{2,1,0:T(8,128)S(1)} %collective-permute-done.8.pl_ref, f32[16,32,384]{2,1,0:T(8,128)S(1)} %get-tuple-element.75.refs_0_.pm_ref.before_ref, ...), custom_call_target="tpu_custom_call" | custom-call | tf_op jit(solution)/shard_map/update_step/pallas_call | solution.py:389
  114.4 5.0 %collective-permute-start.10 = (f32[7,32,384]{2,1,0:T(8,128)}, f32[7,32,384]{2,1,0:T(8,128)}, u32[]{:S(2)}, u32[]{:S(2)}) collective-permute-start(f32[7,32,384]{2,1,0:T(8,128)} %get-tuple-element.80), channel_id=1, source_target_pairs={{0,1},{1,2},{2,3},{3,4},{4,5},{5,6},{6,7},{8,9},{9,10},{10,11},{11... | collective-permute-start | bytes 1032200 | tf_op jit(solution)/shard_map/ppermute | solution.py:459
  128.9 7.6 %local_step.11 = (f32[16,32,384]{2,1,0:T(8,128)S(1)}, f32[16,32,384]{2,1,0:T(8,128)S(1)}) custom-call(f32[16,32,384]{2,1,0:T(8,128)S(1)} %copy-done.30, f32[16,32,384]{2,1,0:T(8,128)S(1)} %copy-done.4, f32[16,32,384]{2,1,0:T(8,128)S(1)} %copy-done.15, f32[16,32,384]{2,1,0:T(8,128)S(1)} %copy-done.19, bf16[8,16,32,384]{3,2,1,0:T(8,128)(2,1)S(1)} %bitcast.18, ...), custom_call_target="tpu_custom_call" | custom-call | tf_op jit(solution)/shard_map/local_step/pallas_call | solution.py:295
  136.6 2.3 %update_step.12 = (f32[16,32,384]{2,1,0:T(8,128)S(1)}, f32[16,32,384]{2,1,0:T(8,128)S(1)}, f32[7,32,384]{2,1,0:T(8,128)S(1)}, f32[7,32,384]{2,1,0:T(8,128)S(1)}) custom-call(f32[7,32,384]{2,1,0:T(8,128)} %collective-permute-done.10.pl_ref, f32[16,32,384]{2,1,0:T(8,128)S(1)} %copy-done.31, f32[7,32,384]{2,1,0:T(8,128)} %collective-permute-done.11.pr_ref, ...), custom_call_target="tpu_custom_call" | custom-call | tf_op jit(solution)/shard_map/update_step/pallas_call | solution.py:389
  139.0 3.6 %collective-permute-start.12 = (f32[7,32,384]{2,1,0:T(8,128)S(1)}, f32[7,32,384]{2,1,0:T(8,128)S(1)}, u32[]{:S(2)}, u32[]{:S(2)}) collective-permute-start(f32[7,32,384]{2,1,0:T(8,128)S(1)} %get-tuple-element.86), channel_id=1, source_target_pairs={{0,1},{1,2},{2,3},{3,4},{4,5},{5,6},{6,7},{8,9},{9,10},{10,11},{11... | collective-permute-start | bytes 1032200 | tf_op jit(solution)/shard_map/ppermute | solution.py:459
  143.8 7.6 %local_step.12 = (f32[16,32,384]{2,1,0:T(8,128)S(1)}, f32[16,32,384]{2,1,0:T(8,128)S(1)}) custom-call(f32[16,32,384]{2,1,0:T(8,128)S(1)} %get-tuple-element.87.refs_0_.pm_ref.before_ref, f32[16,32,384]{2,1,0:T(8,128)S(1)} %copy-done.5, f32[16,32,384]{2,1,0:T(8,128)S(1)} %copy-done.15, f32[16,32,384]{2,1,0:T(8,128)S(1)} %copy-done.20, ...), custom_call_target="tpu_custom_call" | custom-call | tf_op jit(solution)/shard_map/local_step/pallas_call | solution.py:295
  152.4 3.0 %update_step.13 = (f32[16,32,384]{2,1,0:T(8,128)}, f32[16,32,384]{2,1,0:T(8,128)S(1)}, f32[7,32,384]{2,1,0:T(8,128)}, f32[7,32,384]{2,1,0:T(8,128)}) custom-call(f32[7,32,384]{2,1,0:T(8,128)S(1)} %collective-permute-done.12.pl_ref, f32[16,32,384]{2,1,0:T(8,128)S(1)} %get-tuple-element.87.refs_0_.pm_ref.before_ref, ...), custom_call_target="tpu_custom_call" | custom-call | tf_op jit(solution)/shard_map/update_step/pallas_call | solution.py:389
  156.3 5.0 %collective-permute-start.14 = (f32[7,32,384]{2,1,0:T(8,128)}, f32[7,32,384]{2,1,0:T(8,128)}, u32[]{:S(2)}, u32[]{:S(2)}) collective-permute-start(f32[7,32,384]{2,1,0:T(8,128)} %get-tuple-element.92), channel_id=1, source_target_pairs={{0,1},{1,2},{2,3},{3,4},{4,5},{5,6},{6,7},{8,9},{9,10},{10,11},{11... | collective-permute-start | bytes 1032200 | tf_op jit(solution)/shard_map/ppermute | solution.py:459
  169.6 7.6 %local_step.13 = (f32[16,32,384]{2,1,0:T(8,128)S(1)}, f32[16,32,384]{2,1,0:T(8,128)S(1)}) custom-call(f32[16,32,384]{2,1,0:T(8,128)S(1)} %copy-done.33, f32[16,32,384]{2,1,0:T(8,128)S(1)} %copy-done.6, f32[16,32,384]{2,1,0:T(8,128)S(1)} %copy-done.16, f32[16,32,384]{2,1,0:T(8,128)S(1)} %copy-done.21, bf16[8,16,32,384]{3,2,1,0:T(8,128)(2,1)S(1)} %bitcast.20, ...), custom_call_target="tpu_custom_call" | custom-call | tf_op jit(solution)/shard_map/local_step/pallas_call | solution.py:295
  177.3 3.4 %last_step.1 = (f32[16,32,384]{2,1,0:T(8,128)}, f32[16,2,16,384]{3,2,1,0:T(8,128)S(1)}) custom-call(s32[1,3]{1,0:T(1,128)S(1)} %copy-done.49, s32[1]{0:T(128)} %bitcast.first_ref, f32[7,32,384]{2,1,0:T(8,128)} %collective-permute-done.14.pl_ref, f32[16,32,384]{2,1,0:T(8,128)S(1)} %copy-done.33, f32[7,32,384]{2,1,0:T(8,128)} %collective-permute-done.15.pr_ref, ...), custom_call_target="tpu_custom_call" | custom-call | tf_op jit(solution)/shard_map/last_step/pallas_call | solution.py:401
  181.6 7.3 %all-to-all-start.1 = ((f32[16,2,16,384]{3,2,1,0:T(8,128)}), f32[16,2,16,384]{3,2,1,0:T(8,128)S(1)}, u32[]{:S(2)}, u32[]{:S(2)}) async-start(f32[16,2,16,384]{3,2,1,0:T(8,128)} %copy-done.34), calls=%async_computation.1 | async-start | bytes 1572864 | tf_op jit(solution)/shard_map/all_to_all | solution.py:500
  188.8 11.6 %reduce-scatter.4.cloned.1.call-done.refs_1_ = f32[1,2,16,384]{3,2,1,0:T(8,128)} async-done(((f32[16,2,16,384]{3,2,1,0:T(8,128)}), f32[1,2,16,384]{3,2,1,0:T(8,128)}) %reduce-scatter.4.cloned.1.call-update) | async-done | bytes 49168
  200.5 4.6 %all-to-all-done.1.refs_0_ = f32[16,2,16,384]{3,2,1,0:T(8,128)S(1)} async-done(((f32[16,2,16,384]{3,2,1,0:T(8,128)}), f32[16,2,16,384]{3,2,1,0:T(8,128)S(1)}, u32[]{:S(2)}, u32[]{:S(2)}) %all-to-all-start.1) | async-done | bytes 786464 | tf_op jit(solution)/shard_map/all_to_all | solution.py:500
  (135 shorter events, 58.4 us)
Async XLA Ops:
  15.6 29.9 %collective-permute-start = (f32[11,32,384]{2,1,0:T(8,128)}, f32[11,32,384]{2,1,0:T(8,128)}, u32[]{:S(2)}, u32[]{:S(2)}) collective-permute-start(f32[11,32,384]{2,1,0:T(8,128)} %get-tuple-element.52), channel_id=1, source_target_pairs={{0,1},{1,2},{2,3},{3,4},{4,5},{5,6},{6,7},{8,9},{9,10},{10,11},{11... | collective-permute-start | bytes 1622024 | tf_op jit(solution)/shard_map/ppermute | solution.py:459
  17.7 27.8 %collective-permute-start.1 = (f32[10,32,384]{2,1,0:T(8,128)}, f32[10,32,384]{2,1,0:T(8,128)}, u32[]{:S(2)}, u32[]{:S(2)}) collective-permute-start(f32[10,32,384]{2,1,0:T(8,128)} %get-tuple-element.53), channel_id=1, source_target_pairs={{1,0},{2,1},{3,2},{4,3},{5,4},{6,5},{7,6},{9,8},{10,9},{11,10},{12... | collective-permute-start | bytes 1474568 | tf_op jit(solution)/shard_map/ppermute | solution.py:460
  19.0 25.0 %all-to-all-start = ((f32[128,1,128]{2,1,0:T(1,128)}), f32[128,1,128]{2,1,0:T(1,128)S(1)}, u32[]{:S(2)}, u32[]{:S(2)}) async-start(f32[128,1,128]{2,1,0:T(1,128)} %bitcast.5), calls=%async_computation | async-start | bytes 131072 | tf_op jit(solution)/shard_map/all_to_all | solution.py:481
  32.3 168.1 %reduce-scatter.4.cloned.1.call-start = ((), (), s32[]{:S(2)}) async-start(), calls=%async_computation.3 | async-start | bytes 835584
  44.0 11.3 %copy-start.3 = (f32[16,32,384]{2,1,0:T(8,128)S(1)}, f32[16,32,384]{2,1,0:T(8,128)}, u32[]{:S(2)}) copy-start(f32[16,32,384]{2,1,0:T(8,128)} %k_ref.17) | copy-start | bytes 2359300
  45.5 9.9 %copy-start = (bf16[1,8,16,32,384]{4,3,2,1,0:T(8,128)(2,1)S(1)}, bf16[1,8,16,32,384]{4,3,2,1,0:T(8,128)(2,1)}, u32[]{:S(2)}) copy-start(bf16[1,8,16,32,384]{4,3,2,1,0:T(8,128)(2,1)} %param.18) | copy-start | bytes 9437188
  52.7 10.3 %collective-permute-start.2 = (f32[7,32,384]{2,1,0:T(8,128)S(1)}, f32[7,32,384]{2,1,0:T(8,128)S(1)}, u32[]{:S(2)}, u32[]{:S(2)}) collective-permute-start(f32[7,32,384]{2,1,0:T(8,128)S(1)} %get-tuple-element.56), channel_id=1, source_target_pairs={{0,1},{1,2},{2,3},{3,4},{4,5},{5,6},{6,7},{8,9},{9,10},{10,11},{11... | collective-permute-start | bytes 1032200 | tf_op jit(solution)/shard_map/ppermute | solution.py:459
  54.0 8.9 %collective-permute-start.3 = (f32[7,32,384]{2,1,0:T(8,128)S(1)}, f32[7,32,384]{2,1,0:T(8,128)S(1)}, u32[]{:S(2)}, u32[]{:S(2)}) collective-permute-start(f32[7,32,384]{2,1,0:T(8,128)S(1)} %get-tuple-element.58), channel_id=1, source_target_pairs={{1,0},{2,1},{3,2},{4,3},{5,4},{6,5},{7,6},{9,8},{10,9},{11,10},{12... | collective-permute-start | bytes 1032200 | tf_op jit(solution)/shard_map/ppermute | solution.py:460
  65.0 13.1 %collective-permute-start.4 = (f32[7,32,384]{2,1,0:T(8,128)S(1)}, f32[7,32,384]{2,1,0:T(8,128)S(1)}, u32[]{:S(2)}, u32[]{:S(2)}) collective-permute-start(f32[7,32,384]{2,1,0:T(8,128)S(1)} %get-tuple-element.62), channel_id=1, source_target_pairs={{0,1},{1,2},{2,3},{3,4},{4,5},{5,6},{6,7},{8,9},{9,10},{10,11},{11... | collective-permute-start | bytes 1032200 | tf_op jit(solution)/shard_map/ppermute | solution.py:459
  69.2 8.9 %collective-permute-start.5 = (f32[7,32,384]{2,1,0:T(8,128)S(1)}, f32[7,32,384]{2,1,0:T(8,128)S(1)}, u32[]{:S(2)}, u32[]{:S(2)}) collective-permute-start(f32[7,32,384]{2,1,0:T(8,128)S(1)} %get-tuple-element.64), channel_id=1, source_target_pairs={{1,0},{2,1},{3,2},{4,3},{5,4},{6,5},{7,6},{9,8},{10,9},{11,10},{12... | collective-permute-start | bytes 1032200 | tf_op jit(solution)/shard_map/ppermute | solution.py:460
  80.2 13.4 %collective-permute-start.6 = (f32[7,32,384]{2,1,0:T(8,128)S(1)}, f32[7,32,384]{2,1,0:T(8,128)S(1)}, u32[]{:S(2)}, u32[]{:S(2)}) collective-permute-start(f32[7,32,384]{2,1,0:T(8,128)S(1)} %get-tuple-element.68), channel_id=1, source_target_pairs={{0,1},{1,2},{2,3},{3,4},{4,5},{5,6},{6,7},{8,9},{9,10},{10,11},{11... | collective-permute-start | bytes 1032200 | tf_op jit(solution)/shard_map/ppermute | solution.py:459
  84.5 9.1 %collective-permute-start.7 = (f32[7,32,384]{2,1,0:T(8,128)S(1)}, f32[7,32,384]{2,1,0:T(8,128)S(1)}, u32[]{:S(2)}, u32[]{:S(2)}) collective-permute-start(f32[7,32,384]{2,1,0:T(8,128)S(1)} %get-tuple-element.70), channel_id=1, source_target_pairs={{1,0},{2,1},{3,2},{4,3},{5,4},{6,5},{7,6},{9,8},{10,9},{11,10},{12... | collective-permute-start | bytes 1032200 | tf_op jit(solution)/shard_map/ppermute | solution.py:460
  95.7 14.1 %copy-start.27 = (f32[16,32,384]{2,1,0:T(8,128)}, f32[16,32,384]{2,1,0:T(8,128)S(1)}, u32[]{:S(2)}) copy-start(f32[16,32,384]{2,1,0:T(8,128)S(1)} %get-tuple-element.75.refs_0_.pm_ref.before_ref) | copy-start | bytes 2359300
  95.7 14.1 %collective-permute-start.8 = (f32[7,32,384]{2,1,0:T(8,128)S(1)}, f32[7,32,384]{2,1,0:T(8,128)S(1)}, u32[]{:S(2)}, u32[]{:S(2)}) collective-permute-start(f32[7,32,384]{2,1,0:T(8,128)S(1)} %get-tuple-element.74), channel_id=1, source_target_pairs={{0,1},{1,2},{2,3},{3,4},{4,5},{5,6},{6,7},{8,9},{9,10},{10,11},{11... | collective-permute-start | bytes 1032200 | tf_op jit(solution)/shard_map/ppermute | solution.py:459
  99.9 9.8 %collective-permute-start.9 = (f32[7,32,384]{2,1,0:T(8,128)S(1)}, f32[7,32,384]{2,1,0:T(8,128)S(1)}, u32[]{:S(2)}, u32[]{:S(2)}) collective-permute-start(f32[7,32,384]{2,1,0:T(8,128)S(1)} %get-tuple-element.76), channel_id=1, source_target_pairs={{1,0},{2,1},{3,2},{4,3},{5,4},{6,5},{7,6},{9,8},{10,9},{11,10},{12... | collective-permute-start | bytes 1032200 | tf_op jit(solution)/shard_map/ppermute | solution.py:460
  114.4 22.2 %collective-permute-start.10 = (f32[7,32,384]{2,1,0:T(8,128)}, f32[7,32,384]{2,1,0:T(8,128)}, u32[]{:S(2)}, u32[]{:S(2)}) collective-permute-start(f32[7,32,384]{2,1,0:T(8,128)} %get-tuple-element.80), channel_id=1, source_target_pairs={{0,1},{1,2},{2,3},{3,4},{4,5},{5,6},{6,7},{8,9},{9,10},{10,11},{11... | collective-permute-start | bytes 1032200 | tf_op jit(solution)/shard_map/ppermute | solution.py:459
  119.4 17.2 %collective-permute-start.11 = (f32[7,32,384]{2,1,0:T(8,128)}, f32[7,32,384]{2,1,0:T(8,128)}, u32[]{:S(2)}, u32[]{:S(2)}) collective-permute-start(f32[7,32,384]{2,1,0:T(8,128)} %get-tuple-element.82), channel_id=1, source_target_pairs={{1,0},{2,1},{3,2},{4,3},{5,4},{6,5},{7,6},{9,8},{10,9},{11,10},{12... | collective-permute-start | bytes 1032200 | tf_op jit(solution)/shard_map/ppermute | solution.py:460
  128.9 7.7 %copy-start.31 = (f32[16,32,384]{2,1,0:T(8,128)S(1)}, f32[16,32,384]{2,1,0:T(8,128)}, u32[]{:S(2)}) copy-start(f32[16,32,384]{2,1,0:T(8,128)} %copy-done.29) | copy-start | bytes 2359300
  139.0 13.4 %copy-start.25 = (f32[16,32,384]{2,1,0:T(8,128)}, f32[16,32,384]{2,1,0:T(8,128)S(1)}, u32[]{:S(2)}) copy-start(f32[16,32,384]{2,1,0:T(8,128)S(1)} %get-tuple-element.87.refs_0_.pm_ref.before_ref) | copy-start | bytes 2359300
  139.0 13.4 %collective-permute-start.12 = (f32[7,32,384]{2,1,0:T(8,128)S(1)}, f32[7,32,384]{2,1,0:T(8,128)S(1)}, u32[]{:S(2)}, u32[]{:S(2)}) collective-permute-start(f32[7,32,384]{2,1,0:T(8,128)S(1)} %get-tuple-element.86), channel_id=1, source_target_pairs={{0,1},{1,2},{2,3},{3,4},{4,5},{5,6},{6,7},{8,9},{9,10},{10,11},{11... | collective-permute-start | bytes 1032200 | tf_op jit(solution)/shard_map/ppermute | solution.py:459
  142.5 9.8 %collective-permute-start.13 = (f32[7,32,384]{2,1,0:T(8,128)S(1)}, f32[7,32,384]{2,1,0:T(8,128)S(1)}, u32[]{:S(2)}, u32[]{:S(2)}) collective-permute-start(f32[7,32,384]{2,1,0:T(8,128)S(1)} %get-tuple-element.88), channel_id=1, source_target_pairs={{1,0},{2,1},{3,2},{4,3},{5,4},{6,5},{7,6},{9,8},{10,9},{11,10},{12... | collective-permute-start | bytes 1032200 | tf_op jit(solution)/shard_map/ppermute | solution.py:460
  156.3 20.9 %collective-permute-start.14 = (f32[7,32,384]{2,1,0:T(8,128)}, f32[7,32,384]{2,1,0:T(8,128)}, u32[]{:S(2)}, u32[]{:S(2)}) collective-permute-start(f32[7,32,384]{2,1,0:T(8,128)} %get-tuple-element.92), channel_id=1, source_target_pairs={{0,1},{1,2},{2,3},{3,4},{4,5},{5,6},{6,7},{8,9},{9,10},{10,11},{11... | collective-permute-start | bytes 1032200 | tf_op jit(solution)/shard_map/ppermute | solution.py:459
  161.3 16.0 %collective-permute-start.15 = (f32[7,32,384]{2,1,0:T(8,128)}, f32[7,32,384]{2,1,0:T(8,128)}, u32[]{:S(2)}, u32[]{:S(2)}) collective-permute-start(f32[7,32,384]{2,1,0:T(8,128)} %get-tuple-element.94), channel_id=1, source_target_pairs={{1,0},{2,1},{3,2},{4,3},{5,4},{6,5},{7,6},{9,8},{10,9},{11,10},{12... | collective-permute-start | bytes 1032200 | tf_op jit(solution)/shard_map/ppermute | solution.py:460
  181.6 23.5 %all-to-all-start.1 = ((f32[16,2,16,384]{3,2,1,0:T(8,128)}), f32[16,2,16,384]{3,2,1,0:T(8,128)S(1)}, u32[]{:S(2)}, u32[]{:S(2)}) async-start(f32[16,2,16,384]{3,2,1,0:T(8,128)} %copy-done.34), calls=%async_computation.1 | async-start | bytes 1572864 | tf_op jit(solution)/shard_map/all_to_all | solution.py:500
  (45 other events, 114.3 us)
Sparse Core Ops, SparseCore 0:
  122.2 78.1 reduce-scatter.3

commit v3 on v2

v3 whole, which is shorter than its diff:
```python
import jax
import jax.numpy as jnp
import ml_dtypes
import numpy as np
from jax import lax
from jax.experimental import pallas as pl
from jax.experimental.pallas import tpu as pltpu
from jax.sharding import PartitionSpec as P

MUTE = 6
COEFFS = (1225.0 / 1024.0, -245.0 / 3072.0, 49.0 / 5120.0, -5.0 / 7168.0)
DAMP = 0.1
HALO = 7
SLOTS = 6
FIELDS = 16
F32 = jnp.float32
BF16 = jnp.bfloat16
PARAMS = pltpu.CompilerParams(vmem_limit_bytes=8 * 1024 * 1024)


def shape_of(*dims, dtype=F32):
    return jax.ShapeDtypeStruct(dims, dtype)


def far_away(*arrays):
    return [pltpu.with_memory_space_constraint(a, pltpu.HBM) for a in arrays]


def split2(x):
    high = x.astype(BF16)
    return high, (x - high.astype(F32)).astype(BF16)


def split3(x):
    high = x.astype(BF16)
    rest = x - high.astype(F32)
    mid = rest.astype(BF16)
    return high, mid, (rest - mid.astype(F32)).astype(BF16)


def contract_last(left, right, **kwargs):
    return lax.dot_general(
        left, right, (((1,), (1,)), ((), ())), preferred_element_type=F32, **kwargs
    )


def prep_kernel(
    traces_far, kernel_far, target_far, cell_far, p_ref, b_ref,
    send_ref, right_ref, left_ref, traces_ref, kernel_ref, target_ref, cell_ref, sems, *, nz,
):
    nx = p_ref.shape[0]
    loads = [
        pltpu.make_async_copy(traces_far, traces_ref, sems.at[0]),
        pltpu.make_async_copy(kernel_far, kernel_ref, sems.at[1]),
        pltpu.make_async_copy(target_far, target_ref, sems.at[2]),
        pltpu.make_async_copy(cell_far, cell_ref, sems.at[3]),
    ]
    copies = [
        pltpu.make_async_copy(p_ref.at[pl.ds(nx - HALO, HALO)], right_ref.at[pl.ds(0, HALO)], sems.at[4]),
        pltpu.make_async_copy(b_ref.at[pl.ds(nx - 4, 4)], right_ref.at[pl.ds(HALO, 4)], sems.at[5]),
        pltpu.make_async_copy(p_ref.at[pl.ds(0, HALO)], left_ref.at[pl.ds(0, HALO)], sems.at[6]),
        pltpu.make_async_copy(b_ref.at[pl.ds(0, 3)], left_ref.at[pl.ds(HALO, 3)], sems.at[7]),
    ]
    for copy in loads + copies:
        copy.start()
    for load in loads:
        load.wait()
    rows = traces_ref.shape[0]
    values = contract_last(kernel_ref[...], traces_ref[...], precision=lax.Precision.HIGHEST)
    lane = lax.broadcasted_iota(jnp.int32, (128, rows), 0)
    hit = target_ref[...] == lane
    onehot = jnp.where(hit, 1.0, 0.0)
    upper = (
        lax.broadcasted_iota(jnp.int32, (rows, rows), 0)
        <= lax.broadcasted_iota(jnp.int32, (rows, rows), 1)
    )
    running = jnp.dot(
        onehot.astype(BF16),
        jnp.where(upper, 1.0, 0.0).astype(BF16),
        preferred_element_type=F32,
    )
    slot = (jnp.sum(jnp.where(hit, running, 0.0), axis=0, keepdims=True) - 1.0).astype(jnp.int32)
    cell = cell_ref[...]
    entries = jnp.where(lane % FIELDS == 8, (cell // nz).astype(F32), values)
    entries = jnp.where(lane % FIELDS == 9, (cell % nz).astype(F32), entries)
    entries = jnp.where(lane // FIELDS == slot, entries, 0.0)
    packed = jnp.zeros((128, 128), F32)
    for piece in split3(entries):
        packed = packed + contract_last(onehot.astype(BF16), piece)
    send_ref[...] = packed
    for copy in copies:
        copy.wait()


def prep(traces, target, cell, current, b1):
    nx, ny, nz = current.shape
    samples = traces.shape[1]
    position = np.arange(samples, dtype=np.float32)[None, :]
    centers = (np.arange(8, dtype=np.float32)[:, None] + np.float32(0.5)) * np.float32(samples / 8)
    kernel = (0.25 * np.exp(-np.abs(position - centers) / np.float32(samples / 8.0))).astype(np.float32)
    tiled = np.zeros((128, samples), np.float32)
    for slot in range(SLOTS):
        tiled[slot * FIELDS : slot * FIELDS + 8] = kernel
    vmem = pl.BlockSpec(memory_space=pltpu.VMEM)
    far = pl.BlockSpec(memory_space=pltpu.HBM)
    return pl.pallas_call(
        lambda *refs: prep_kernel(*refs, nz=nz),
        in_specs=[far] * 6,
        out_specs=[vmem] * 3,
        out_shape=[shape_of(128, 128), shape_of(HALO + 4, ny, nz), shape_of(HALO + 3, ny, nz)],
        scratch_shapes=[
            pltpu.VMEM(traces.shape, F32),
            pltpu.VMEM((128, samples), F32),
            pltpu.VMEM(target.shape, jnp.int32),
            pltpu.VMEM(cell.shape, jnp.int32),
            pltpu.SemaphoreType.DMA((8,)),
        ],
        compiler_params=PARAMS,
        name="prep",
    )(*far_away(traces, jnp.asarray(tiled), target, cell, current, b1))


def fill_columns(got_ref, spread_ref, moment, nz):
    zlane = lax.broadcasted_iota(jnp.int32, (128, nz), 1)
    for slot in range(SLOTS):
        base = slot * FIELDS
        third = got_ref[:, base + 9 : base + 10].astype(jnp.int32)
        value = got_ref[:, base + moment : base + moment + 1]
        spread = jnp.where(third == zlane, value, 0.0)
        high, low = split2(spread)
        spread_ref[0, slot * 128 : (slot + 1) * 128, :] = high
        spread_ref[1, slot * 128 : (slot + 1) * 128, :] = low


def inject_rows(turned, spread_ref, first_row, count):
    row = first_row + lax.broadcasted_iota(jnp.int32, (count, 128), 0)
    picks = []
    for slot in range(SLOTS):
        base = slot * FIELDS
        line = turned[base + 8 : base + 9, :].astype(jnp.int32)
        picks.append(jnp.where(line == row, 1.0, 0.0).astype(BF16))
    pick = jnp.concatenate(picks, axis=1)
    return jnp.dot(pick, spread_ref[0], preferred_element_type=F32) + jnp.dot(
        pick, spread_ref[1], preferred_element_type=F32
    )


def weighted(pairs):
    total = None
    for k, (ahead, behind) in enumerate(pairs):
        term = COEFFS[k] * (ahead - behind)
        total = term if total is None else total + term
    return total


def band_matrices(nz):
    forward = np.zeros((nz, nz), np.float64)
    for face in range(nz):
        for k in range(1, 5):
            if face + k < nz:
                forward[face + k, face] += COEFFS[k - 1]
            if face + 1 - k >= 0:
                forward[face + 1 - k, face] -= COEFFS[k - 1]
    pieces = []
    for matrix in (forward, -forward.T):
        full = matrix.astype(np.float32)
        high = full.astype(ml_dtypes.bfloat16)
        low = (full - high.astype(np.float32)).astype(ml_dtypes.bfloat16)
        pieces += [high, low]
    return np.stack(pieces)


def banded(value, bands_ref, first):
    high, low = split2(value)
    return (
        jnp.dot(high, bands_ref[first], preferred_element_type=F32)
        + jnp.dot(low, bands_ref[first], preferred_element_type=F32)
        + jnp.dot(high, bands_ref[first + 1], preferred_element_type=F32)
    )


def second_derivative(ref, where, first, ny):
    return weighted(
        [
            (
                ref[where, 7 + first + k : 7 + first + k + ny, :],
                ref[where, 8 + first - k : 8 + first - k + ny, :],
            )
            for k in range(1, 5)
        ]
    )


def along_third(p_ref, b3_ref, bands_ref):
    nx, ny, nz = p_ref.shape
    flux = b3_ref[...].reshape(nx * ny, nz) * banded(p_ref[...].reshape(nx * ny, nz), bands_ref, 0)
    return banded(flux, bands_ref, 2)


def along_second(p_ref, b2_ref, x, lanes, ps_ref, qs_ref, where):
    ny = p_ref.shape[1]
    ps_ref[where, 8 : 8 + ny, :] = p_ref[x, :, lanes]
    qs_ref[where, 8 : 8 + ny, :] = b2_ref[x, :, lanes] * second_derivative(ps_ref, where, 1, ny)
    return second_derivative(qs_ref, where, 0, ny)


def local_change(
    p_ref, k_ref, b2_ref, b3_ref, bands_ref, got_ref, turned, moment, out_ref, scratch, and_then=None
):
    ps_ref, qs_ref, spread_ref, added_ref, third_ref = scratch
    nx, ny, nz = p_ref.shape
    clear_edges(ps_ref, qs_ref, ny)
    fill_columns(got_ref, spread_ref, moment, nz)
    added_ref[...] = inject_rows(turned, spread_ref, 0, nx * ny).reshape(nx, ny, nz)
    third_ref[...] = along_third(p_ref, b3_ref, bands_ref).reshape(nx, ny, nz)
    count = nz // 128

    def planes(group, carry):
        for index in range(GROUP):
            x = group * GROUP + index
            for c in range(count):
                lanes = slice(c * 128, c * 128 + 128)
                second = along_second(p_ref, b2_ref, x, lanes, ps_ref, qs_ref, index * count + c)
                out_ref[x, :, lanes] = (
                    k_ref[x, :, lanes] * (second + third_ref[x, :, lanes]) + added_ref[x, :, lanes]
                )
            if and_then is not None:
                and_then(x)
        return carry

    lax.fori_loop(0, nx // GROUP, planes, 0)


def local_scratch(nx, ny, nz):
    return [shift_scratch(ny, nz)] * 2 + [
        pltpu.VMEM((2, SLOTS * 128, nz), BF16),
        pltpu.VMEM((nx, ny, nz), F32),
        pltpu.VMEM((nx, ny, nz), F32),
    ]


def clear_edges(ps_ref, qs_ref, ny):
    zero = jnp.zeros((ps_ref.shape[0], 8, 128), F32)
    for ref in (ps_ref, qs_ref):
        ref[:, 0:8, :] = zero
        ref[:, 8 + ny : 16 + ny, :] = zero


GROUP = 4
LOADS = 5


def first_local_kernel(
    got_ref, p_far, bands_far, k_far, b2_far, b3_far, b1_far, before_far, frames_far,
    out_ref, turned_ref, p_ref, bands_ref, k_ref, b2_ref, b3_ref, b1_ref, before_ref, frames_ref,
    *scratch,
):
    *scratch, sems = scratch
    far = (p_far, bands_far, k_far, b2_far, b3_far, b1_far, before_far, frames_far)
    near = (p_ref, bands_ref, k_ref, b2_ref, b3_ref, b1_ref, before_ref, frames_ref)
    copies = [pltpu.make_async_copy(f, n, sems.at[i]) for i, (f, n) in enumerate(zip(far, near))]
    for copy in copies:
        copy.start()
    turned_ref[...] = got_ref[...].T
    for copy in copies[:LOADS]:
        copy.wait()
    local_change(
        p_ref, k_ref, b2_ref, b3_ref, bands_ref, got_ref, turned_ref[...], 0, out_ref, scratch
    )
    for copy in copies[LOADS:]:
        copy.wait()


def shift_scratch(ny, nz):
    return pltpu.VMEM((GROUP * (nz // 128), ny + 16, 128), F32)


def first_local(got, *arrays):
    nx, ny, nz = arrays[0].shape
    vmem = pl.BlockSpec(memory_space=pltpu.VMEM)
    far = pl.BlockSpec(memory_space=pltpu.HBM)
    return pl.pallas_call(
        first_local_kernel,
        in_specs=[vmem] + [far] * len(arrays),
        out_specs=[vmem] * (2 + len(arrays)),
        out_shape=[shape_of(nx, ny, nz), shape_of(128, 128)]
        + [shape_of(*a.shape, dtype=a.dtype) for a in arrays],
        scratch_shapes=local_scratch(nx, ny, nz) + [pltpu.SemaphoreType.DMA((len(arrays),))],
        compiler_params=PARAMS,
        name="first_local",
    )(got, *far_away(*arrays))


def make_local_kernel(moment):
    def local_kernel(*refs):
        p_ref, bands_ref, k_ref, b2_ref, b3_ref, f_ref, change_ref = refs[:7]
        refs = refs[7:]
        if moment > 1:
            image_ref, refs = refs[0], refs[1:]
            light_ref, refs = refs[0], refs[1:]
        got_ref, turned_ref, out_ref, image_out_ref, light_out_ref, *scratch = refs

        def accumulate(x):
            frame = f_ref[moment - 1, x].astype(F32)
            image = frame * change_ref[x]
            light = frame * frame
            if moment > 1:
                image = image + image_ref[x]
                light = light + light_ref[x]
            if moment == f_ref.shape[0] - 1:
                frame = f_ref[moment, x].astype(F32)
                light = light + frame * frame
            image_out_ref[x] = image
            light_out_ref[x] = light

        local_change(
            p_ref, k_ref, b2_ref, b3_ref, bands_ref, got_ref, turned_ref[...], moment, out_ref,
            scratch, accumulate,
        )

    return local_kernel


def local_step(moment, current, bands, stiffness, b2, b3, frames, change, sums, got, turned):
    nx, ny, nz = current.shape
    images = list(sums) if moment > 1 else []
    return pl.pallas_call(
        make_local_kernel(moment),
        in_specs=[pl.BlockSpec(memory_space=pltpu.VMEM)] * (9 + len(images)),
        out_specs=[pl.BlockSpec(memory_space=pltpu.VMEM)] * 3,
        out_shape=[shape_of(nx, ny, nz)] * 3,
        scratch_shapes=local_scratch(nx, ny, nz),
        compiler_params=PARAMS,
        name="local_step",
    )(current, bands, stiffness, b2, b3, frames, change, *images, got, turned)


def edge_factors(place_ref, nx):
    first = place_ref[3]
    return (
        jnp.where(first > 0, 1.0, 0.0).astype(F32),
        jnp.where(first < place_ref[4], 1.0, 0.0).astype(F32),
    )


def change_column(edges, p_refs, b_refs, k_ref, local_ref, rows, lanes):
    pl_ref, pm_ref, pr_ref = p_refs
    bl_ref, bm_ref, br_ref = b_refs
    nx = pm_ref.shape[0]

    def cell(i):
        if i < 0:
            return edges[0] * pl_ref[HALO + i, rows, lanes]
        if i >= nx:
            return edges[1] * pr_ref[i - nx, rows, lanes]
        return pm_ref[i, rows, lanes]

    def face(i):
        if i < 0:
            return edges[0] * bl_ref[HALO + 4 + i, rows, lanes]
        if i >= nx:
            return edges[1] * br_ref[HALO + i - nx, rows, lanes]
        return bm_ref[i, rows, lanes]

    cells = {i: cell(i) for i in range(-HALO, 0)}
    fluxes = {}
    for ahead in range(0, nx + HALO):
        cells[ahead] = cell(ahead)
        j = ahead - 4
        if j >= -4:
            fluxes[j] = face(j) * weighted([(cells[j + k], cells[j + 1 - k]) for k in range(1, 5)])
        i = j - 3
        if i >= 0:
            total = weighted([(fluxes[i + k - 1], fluxes[i - k]) for k in range(1, 5)])
            yield i, cells[i], local_ref[i, rows, lanes] + k_ref[i, rows, lanes] * total


def each_column(ny, nz, work):
    def band(index, carry):
        for c in range(nz // 128):
            work(pl.ds(pl.multiple_of(index * 8, 8), 8), slice(c * 128, c * 128 + 128), index, c)
        return carry

    lax.fori_loop(0, ny // 8, band, 0)


def update_kernel(
    place_ref, pl_ref, pm_ref, pr_ref, bl_ref, bm_ref, br_ref, k_ref, local_ref, before_ref,
    next_ref, change_ref, head_ref, tail_ref,
):
    nx, ny, nz = pm_ref.shape
    edges = edge_factors(place_ref, nx)

    def work(rows, lanes, band, tile):
        for i, now, change in change_column(
            edges, (pl_ref, pm_ref, pr_ref), (bl_ref, bm_ref, br_ref), k_ref, local_ref, rows, lanes
        ):
            following = 2.0 * now - before_ref[i, rows, lanes] + change
            next_ref[i, rows, lanes] = following
            change_ref[i, rows, lanes] = change
            if i < HALO:
                head_ref[i, rows, lanes] = following
            if i >= nx - HALO:
                tail_ref[i - (nx - HALO), rows, lanes] = following

    each_column(ny, nz, work)


def last_kernel(
    place_ref, pl_ref, pm_ref, pr_ref, bl_ref, bm_ref, br_ref, k_ref, local_ref,
    before_ref, image_ref, f_ref, light_ref, next_ref, muted_ref, kept_ref,
):
    nx, ny, nz = pm_ref.shape
    steps = f_ref.shape[0]
    edges = edge_factors(place_ref, nx)
    second = lax.broadcasted_iota(jnp.int32, (8, 128), 0).astype(F32)
    third = lax.broadcasted_iota(jnp.int32, (8, 128), 1).astype(F32)
    first_at = (place_ref[3] - place_ref[0]).astype(F32)
    second_at = place_ref[1].astype(F32)
    third_at = place_ref[2].astype(F32)

    def work(rows, lanes, band, tile):
        flat = (second + ((band * 8).astype(F32) - second_at)) ** 2 + (
            third + (float(tile * 128) - third_at)
        ) ** 2
        for i, now, change in change_column(
            edges, (pl_ref, pm_ref, pr_ref), (bl_ref, bm_ref, br_ref), k_ref, local_ref, rows, lanes
        ):
            next_ref[i, rows, lanes] = 2.0 * now - before_ref[i, rows, lanes] + change
            image = image_ref[i, rows, lanes] + f_ref[steps - 1, i, rows, lanes].astype(F32) * change
            distance = (first_at + float(i)) ** 2 + flat
            kept_ref[i, rows, lanes] = (1.0 - jnp.exp(distance * (-1.0 / (2.0 * MUTE * MUTE)))) * image

    each_column(ny, nz, work)
    for y in range(ny):
        muted_ref[y // 2, y % 2, :, :] = kept_ref[:, y, :]
        muted_ref[y // 2, 2 + y % 2, :, :] = light_ref[:, y, :]


def update_step(place, halos, current, b1_halos, b1, stiffness, local, before):
    nx, ny, nz = current.shape
    return pl.pallas_call(
        update_kernel,
        in_specs=[pl.BlockSpec(memory_space=pltpu.SMEM)] + [pl.BlockSpec(memory_space=pltpu.VMEM)] * 9,
        out_specs=[pl.BlockSpec(memory_space=pltpu.VMEM)] * 4,
        out_shape=[shape_of(nx, ny, nz)] * 2 + [shape_of(HALO, ny, nz)] * 2,
        compiler_params=PARAMS,
        name="update_step",
    )(place, halos[0], current, halos[1], b1_halos[0], b1, b1_halos[1], stiffness, local, before)


def last_step(place, halos, current, b1_halos, b1, stiffness, local, before, image, forward, light):
    nx, ny, nz = current.shape
    vmem = pl.BlockSpec(memory_space=pltpu.VMEM)
    smem = pl.BlockSpec(memory_space=pltpu.SMEM)
    return pl.pallas_call(
        last_kernel,
        in_specs=[smem] + [vmem] * 12,
        out_specs=[vmem] * 2,
        out_shape=[shape_of(nx, ny, nz), shape_of(ny // 2, 4, nx, nz)],
        scratch_shapes=[pltpu.VMEM((nx, ny, nz), F32)],
        compiler_params=PARAMS,
        name="last_step",
    )(
        place, halos[0], current, halos[1], b1_halos[0], b1, b1_halos[1], stiffness, local,
        before, image, forward, light,
    )


def quotient_kernel(image_ref, out_ref, *, scale):
    nz = image_ref.shape[-1]
    for side in range(2):
        image = image_ref[0, side]
        light = image_ref[0, 2 + side]
        for shot in range(1, image_ref.shape[0]):
            image = image + image_ref[shot, side]
            light = light + image_ref[shot, 2 + side]
        out_ref[:, side * nz : (side + 1) * nz] = image / (light * scale + DAMP)


def quotient(images, scale):
    _, _, nx, nz = images.shape
    return pl.pallas_call(
        lambda *refs: quotient_kernel(*refs, scale=scale),
        out_shape=shape_of(nx, 2 * nz),
        compiler_params=PARAMS,
        name="quotient",
    )(images)


def exchange(head, tail):
    count = lax.axis_size("sub")
    from_left = lax.ppermute(tail, "sub", [(i, (i + 1) % count) for i in range(count)])
    from_right = lax.ppermute(head, "sub", [((i + 1) % count, i) for i in range(count)])
    return from_left, from_right


def local(
    stiffness, b1, b2, b3, adjoint_before, adjoint_current, forward_field,
    traces, receiver_target, receiver_cell, source_cell,
):
    both = ("shot", "sub")
    steps = forward_field.shape[1]
    nx = stiffness.shape[0]
    rows = traces.shape[0]
    forward = forward_field[0]
    before = adjoint_before[0]
    current = adjoint_current[0]

    nx_all = nx * lax.axis_size("sub")
    place = jnp.concatenate(
        [
            source_cell[0],
            (lax.axis_index("sub") * nx).astype(jnp.int32)[None],
            jnp.full((1,), nx_all - nx, jnp.int32),
        ]
    )
    send, right, left = prep(
        traces, receiver_target.reshape(1, rows), receiver_cell.reshape(1, rows), current, b1
    )
    got = lax.all_to_all(send, both, split_axis=0, concat_axis=0, tiled=True)
    halos = exchange(left, right)
    b1_halos = halos
    got, place = lax.optimization_barrier((got, place))
    bands = jnp.asarray(band_matrices(current.shape[2]))
    nearby, turned, current, bands, stiffness, b2, b3, b1, before, frames = first_local(
        got, current, bands, stiffness, b2, b3, b1, before, forward
    )

    image = light = None
    for moment in range(steps - 1):
        following, change, head, tail = update_step(
            place, halos, current, b1_halos, b1, stiffness, nearby, before
        )
        halos = exchange(head, tail)
        before, current = current, following
        nearby, image, light = local_step(
            moment + 1, current, bands, stiffness, b2, b3, frames, change, (image, light), got, turned
        )
    following, sums = last_step(
        place, halos, current, b1_halos, b1, stiffness, nearby, before, image, frames, light
    )
    sums = lax.all_to_all(sums, "shot", split_axis=0, concat_axis=0, tiled=True)
    gradient = quotient(sums, 1.0 / (steps * lax.axis_size("shot")))
    return gradient, current[None], following[None]


def solution(mesh):
    placed = (
        P("sub", None, None),
        P("sub", None, None),
        P("sub", None, None),
        P("sub", None, None),
        P("shot", "sub", None, None),
        P("shot", "sub", None, None),
        P("shot", None, "sub", None, None),
        P(("shot", "sub"), None),
        P(("shot", "sub"), None),
        P(("shot", "sub")),
        P("shot", None),
    )
    return jax.shard_map(
        local,
        mesh=mesh,
        in_specs=placed,
        out_specs=(P("sub", "shot"), P("shot", "sub", None, None), P("shot", "sub", None, None)),
        check_vma=False,
    )
```

time: 216 us -> 127 us (0.59)
  local copies, waits for them, and re-layouts: 35.4 us -> 1.14 us
  Pallas kernels: 86 us -> 52.6 us
  starting transfers between devices: 61.1 us -> 33.8 us
  blocking collectives: 0 us -> 23.5 us
  between operations: 14.6 us -> 0.88 us
  waiting for transfers between devices: 16.3 us -> 14 us
    unnamed x100 -> x6, local copies, waits for them, and re-layouts: 35.4 us -> 1.14 us
    pallas_call x19 -> x17, Pallas kernels: 85.3 us -> 51.9 us  [the longest x7 28.7 us: local_step(): pl.pallas_call(make_local_kernel(moment), in_specs=[pl.BlockSpec(memory_s...]
    all_to_all x0 -> x1, blocking collectives: none -> 23.5 us  [local(): sums = lax.all_to_all(sums, 'shot', split_axis=0, concat_axis=0, tiled=True)]
    ppermute x16, starting transfers between devices: 40.4 us -> 23.9 us  [the longest x8 23.8 us: exchange(): lax.ppermute(head, 'sub', [((i + 1) % count, i) for i in range(count)])]
    unnamed x2 -> x0, waiting for transfers between devices: 11.7 us -> none
    all_to_all x1, waiting for transfers between devices: 0.01 us -> 9.14 us  [local(): got = lax.all_to_all(send, both, split_axis=0, concat_axis=0, tiled=True)]
    all_to_all x1 -> x0, starting transfers between devices: 7.26 us -> none  [local(): lax.all_to_all(muted, 'shot', split_axis=0, concat_axis=0, tiled=True)]
    ppermute x16, waiting for transfers between devices: 0.04 us -> 4.87 us  [the longest x8 4.85 us: exchange(): lax.ppermute(tail, 'sub', [(i, (i + 1) % count) for i in range(count)])]
  transfers between devices with their start and end apart: 19 -> 17, of which waited for: 2 -> 7; matrix products, arithmetic and copies ran while one was open for 0% -> 0% of each run, Pallas kernels for 33% -> 28%
where the time goes in v3:
time: 127 us; the launch traced here: 126 us
  Pallas kernels  52.6 us (41%)
  starting transfers between devices  33.8 us (27%)
  blocking collectives  23.5 us (19%)
  waiting for transfers between devices  14 us (11%)
    pallas_call x7, Pallas kernels, local_step(): pl.pallas_call(make_local_kernel(moment), in_specs=[pl.BlockSpec(memory_s...  28.7 us
    ppermute x8, starting transfers between devices, exchange(): lax.ppermute(head, 'sub', [((i + 1) % count, i) for i in range(count)])  23.8 us
    all_to_all x1, blocking collectives, local(): sums = lax.all_to_all(sums, 'shot', split_axis=0, concat_axis=0, tiled=True)  23.5 us
    pallas_call x7, Pallas kernels, update_step(): pl.pallas_call(update_kernel, in_specs=[pl.BlockSpec(memory_space=pltpu.S...  11.4 us
    all_to_all x1, starting transfers between devices, local(): got = lax.all_to_all(send, both, split_axis=0, concat_axis=0, tiled=True)  9.93 us
    all_to_all x1, waiting for transfers between devices, local(): got = lax.all_to_all(send, both, split_axis=0, concat_axis=0, tiled=True)  9.14 us
    pallas_call x1, Pallas kernels, first_local(): pl.pallas_call(first_local_kernel, in_specs=[vmem] + [far] * len(arrays),...  6.23 us
    ppermute x8, waiting for transfers between devices, exchange(): lax.ppermute(tail, 'sub', [(i, (i + 1) % count) for i in range(count)])  4.85 us
  transfers between devices with their start and end apart: 17, of which 7 were waited for; matrix products, arithmetic and copies ran while one was open for 0% of the time, Pallas kernels for 28%

profile of v3, /device:TPU:0, one launch (start us, length us, event | category | flops | bytes accessed | tf_op | source)
XLA Modules:
  0.0 126.0 jit_solution(16188835489910943291)
XLA Ops:
  0.6 2.9 %prep.1 = (f32[128,128]{1,0:T(8,128)}, f32[11,32,384]{2,1,0:T(8,128)S(1)}, f32[10,32,384]{2,1,0:T(8,128)S(1)}) custom-call(f32[512,256]{1,0:T(8,128)} %refs_0_.1, f32[128,256]{1,0:T(8,128)} %constant.12.clone.refs_1_, s32[1,512]{1,0:T(1,128)} %bitcast.26, s32[1,512]{1,0:T(1,128)} %bitcast.27, f32[16,32,384]{2,1,0:T(8,128)} %bitcast.22, f32[16,32,384]{2,1,0:T(8,128)} %b1_far.1), custom_call_target="tpu_custom_call" | custom-call | tf_op jit(solution)/shard_map/prep/pallas_call | solution.py:106
  3.6 2.9 %collective-permute-start.1 = (f32[10,32,384]{2,1,0:T(8,128)S(1)}, f32[10,32,384]{2,1,0:T(8,128)S(1)}, u32[]{:S(2)}, u32[]{:S(2)}) collective-permute-start(f32[10,32,384]{2,1,0:T(8,128)S(1)} %get-tuple-element.74), channel_id=1, source_target_pairs={{1,0},{2,1},{3,2},{4,3},{5,4},{6,5},{7,6},{0,7},{9,8},{10,9},{11,1... | collective-permute-start | bytes 1474568 | tf_op jit(solution)/shard_map/ppermute | solution.py:494
  6.6 9.9 %all-to-all-start = ((f32[128,1,128]{2,1,0:T(1,128)}), f32[128,1,128]{2,1,0:T(1,128)S(1)}, u32[]{:S(2)}, u32[]{:S(2)}) async-start(f32[128,1,128]{2,1,0:T(1,128)} %bitcast.4), calls=%async_computation | async-start | bytes 131072 | tf_op jit(solution)/shard_map/all_to_all | solution.py:521
  16.6 9.1 %all-to-all-done = f32[128,1,128]{2,1,0:T(1,128)S(1)} async-done(((f32[128,1,128]{2,1,0:T(1,128)}), f32[128,1,128]{2,1,0:T(1,128)S(1)}, u32[]{:S(2)}, u32[]{:S(2)}) %all-to-all-start) | async-done | bytes 65568 | tf_op jit(solution)/shard_map/all_to_all | solution.py:521
  25.7 6.2 %first_local.1 = (f32[16,32,384]{2,1,0:T(8,128)S(1)}, f32[128,128]{1,0:T(8,128)S(1)}, f32[16,32,384]{2,1,0:T(8,128)S(1)}, bf16[4,384,384]{2,1,0:T(8,128)(2,1)S(1...) custom-call(f32[128,128]{1,0:T(8,128)S(1)} %bitcast.13, ...), custom_call_target="tpu_custom_call" | custom-call | tf_op jit(solution)/shard_map/first_local/pallas_call | solution.py:282
  33.5 2.9 %collective-permute-start.3 = (f32[7,32,384]{2,1,0:T(8,128)S(1)}, f32[7,32,384]{2,1,0:T(8,128)S(1)}, u32[]{:S(2)}, u32[]{:S(2)}) collective-permute-start(f32[7,32,384]{2,1,0:T(8,128)S(1)} %get-tuple-element.81), channel_id=1, source_target_pairs={{1,0},{2,1},{3,2},{4,3},{5,4},{6,5},{7,6},{0,7},{9,8},{10,9},{11,1... | collective-permute-start | bytes 1032200 | tf_op jit(solution)/shard_map/ppermute | solution.py:494
  36.4 4.0 %local_step.7 = (f32[16,32,384]{2,1,0:T(8,128)S(1)}, f32[16,32,384]{2,1,0:T(8,128)S(1)}, f32[16,32,384]{2,1,0:T(8,128)S(1)}) custom-call(f32[16,32,384]{2,1,0:T(8,128)S(1)} %get-tuple-element.80.refs_0_.pm_ref.before_ref, bf16[4,384,384]{2,1,0:T(8,128)(2,1)S(1)} %get-tuple-element.82.refs_1_, f32[16,32,384]{2,1,0:T(8,128)S(1)} %get-tuple-element.76.k_ref.refs_2_, ...), custom_call_target="tpu_custom_call" | custom-call | tf_op jit(solution)/shard_map/local_step/pallas_call | solution.py:327
  42.9 3.0 %collective-permute-start.5 = (f32[7,32,384]{2,1,0:T(8,128)S(1)}, f32[7,32,384]{2,1,0:T(8,128)S(1)}, u32[]{:S(2)}, u32[]{:S(2)}) collective-permute-start(f32[7,32,384]{2,1,0:T(8,128)S(1)} %get-tuple-element.91), channel_id=1, source_target_pairs={{1,0},{2,1},{3,2},{4,3},{5,4},{6,5},{7,6},{0,7},{9,8},{10,9},{11,1... | collective-permute-start | bytes 1032200 | tf_op jit(solution)/shard_map/ppermute | solution.py:494
  45.9 4.1 %local_step.8 = (f32[16,32,384]{2,1,0:T(8,128)S(1)}, f32[16,32,384]{2,1,0:T(8,128)S(1)}, f32[16,32,384]{2,1,0:T(8,128)S(1)}) custom-call(f32[16,32,384]{2,1,0:T(8,128)S(1)} %get-tuple-element.90.refs_0_.pm_ref.before_ref, bf16[4,384,384]{2,1,0:T(8,128)(2,1)S(1)} %get-tuple-element.82.refs_1_, f32[16,32,384]{2,1,0:T(8,128)S(1)} %get-tuple-element.76.k_ref.refs_2_, ...), custom_call_target="tpu_custom_call" | custom-call | tf_op jit(solution)/shard_map/local_step/pallas_call | solution.py:327
  52.3 3.0 %collective-permute-start.7 = (f32[7,32,384]{2,1,0:T(8,128)S(1)}, f32[7,32,384]{2,1,0:T(8,128)S(1)}, u32[]{:S(2)}, u32[]{:S(2)}) collective-permute-start(f32[7,32,384]{2,1,0:T(8,128)S(1)} %get-tuple-element.98), channel_id=1, source_target_pairs={{1,0},{2,1},{3,2},{4,3},{5,4},{6,5},{7,6},{0,7},{9,8},{10,9},{11,1... | collective-permute-start | bytes 1032200 | tf_op jit(solution)/shard_map/ppermute | solution.py:494
  55.3 4.1 %local_step.9 = (f32[16,32,384]{2,1,0:T(8,128)S(1)}, f32[16,32,384]{2,1,0:T(8,128)S(1)}, f32[16,32,384]{2,1,0:T(8,128)S(1)}) custom-call(f32[16,32,384]{2,1,0:T(8,128)S(1)} %get-tuple-element.97.refs_0_.pm_ref.before_ref, bf16[4,384,384]{2,1,0:T(8,128)(2,1)S(1)} %get-tuple-element.82.refs_1_, f32[16,32,384]{2,1,0:T(8,128)S(1)} %get-tuple-element.76.k_ref.refs_2_, ...), custom_call_target="tpu_custom_call" | custom-call | tf_op jit(solution)/shard_map/local_step/pallas_call | solution.py:327
  60.2 1.7 %update_step.10 = (f32[16,32,384]{2,1,0:T(8,128)S(1)}, f32[16,32,384]{2,1,0:T(8,128)S(1)}, f32[7,32,384]{2,1,0:T(8,128)S(1)}, f32[7,32,384]{2,1,0:T(8,128)S(1)}) custom-call(s32[5]{0:T(128)S(1)} %pad_add_fusion.place_ref, f32[7,32,384]{2,1,0:T(8,128)S(1)} %collective-permute-done.6.pl_ref, f32[16,32,384]{2,1,0:T(8,128)S(1)} %get-tuple-element.97.refs_0_.pm_ref.before_ref, ...), custom_call_target="tpu_custom_call" | custom-call | tf_op jit(solution)/shard_map/update_step/pallas_call | solution.py:442
  61.9 3.0 %collective-permute-start.9 = (f32[7,32,384]{2,1,0:T(8,128)S(1)}, f32[7,32,384]{2,1,0:T(8,128)S(1)}, u32[]{:S(2)}, u32[]{:S(2)}) collective-permute-start(f32[7,32,384]{2,1,0:T(8,128)S(1)} %get-tuple-element.105), channel_id=1, source_target_pairs={{1,0},{2,1},{3,2},{4,3},{5,4},{6,5},{7,6},{0,7},{9,8},{10,9},{11,1... | collective-permute-start | bytes 1032200 | tf_op jit(solution)/shard_map/ppermute | solution.py:494
  64.8 4.1 %local_step.10 = (f32[16,32,384]{2,1,0:T(8,128)S(1)}, f32[16,32,384]{2,1,0:T(8,128)S(1)}, f32[16,32,384]{2,1,0:T(8,128)S(1)}) custom-call(f32[16,32,384]{2,1,0:T(8,128)S(1)} %get-tuple-element.104.refs_0_.pm_ref.before_ref, bf16[4,384,384]{2,1,0:T(8,128)(2,1)S(1)} %get-tuple-element.82.refs_1_, f32[16,32,384]{2,1,0:T(8,128)S(1)} %get-tuple-element.76.k_ref.refs_2_, ...), custom_call_target="tpu_custom_call" | custom-call | tf_op jit(solution)/shard_map/local_step/pallas_call | solution.py:327
  71.3 3.0 %collective-permute-start.11 = (f32[7,32,384]{2,1,0:T(8,128)S(1)}, f32[7,32,384]{2,1,0:T(8,128)S(1)}, u32[]{:S(2)}, u32[]{:S(2)}) collective-permute-start(f32[7,32,384]{2,1,0:T(8,128)S(1)} %get-tuple-element.112), channel_id=1, source_target_pairs={{1,0},{2,1},{3,2},{4,3},{5,4},{6,5},{7,6},{0,7},{9,8},{10,9},{11,1... | collective-permute-start | bytes 1032200 | tf_op jit(solution)/shard_map/ppermute | solution.py:494
  74.2 4.1 %local_step.11 = (f32[16,32,384]{2,1,0:T(8,128)S(1)}, f32[16,32,384]{2,1,0:T(8,128)S(1)}, f32[16,32,384]{2,1,0:T(8,128)S(1)}) custom-call(f32[16,32,384]{2,1,0:T(8,128)S(1)} %get-tuple-element.111.refs_0_.pm_ref.before_ref, bf16[4,384,384]{2,1,0:T(8,128)(2,1)S(1)} %get-tuple-element.82.refs_1_, f32[16,32,384]{2,1,0:T(8,128)S(1)} %get-tuple-element.76.k_ref.refs_2_, ...), custom_call_target="tpu_custom_call" | custom-call | tf_op jit(solution)/shard_map/local_step/pallas_call | solution.py:327
  79.2 1.5 %update_step.12 = (f32[16,32,384]{2,1,0:T(8,128)S(1)}, f32[16,32,384]{2,1,0:T(8,128)S(1)}, f32[7,32,384]{2,1,0:T(8,128)S(1)}, f32[7,32,384]{2,1,0:T(8,128)S(1)}) custom-call(s32[5]{0:T(128)S(1)} %pad_add_fusion.place_ref, f32[7,32,384]{2,1,0:T(8,128)S(1)} %collective-permute-done.10.pl_ref, f32[16,32,384]{2,1,0:T(8,128)S(1)} %get-tuple-element.111.refs_0_.pm_ref.before_ref, ...), custom_call_target="tpu_custom_call" | custom-call | tf_op jit(solution)/shard_map/update_step/pallas_call | solution.py:442
  80.7 3.0 %collective-permute-start.13 = (f32[7,32,384]{2,1,0:T(8,128)S(1)}, f32[7,32,384]{2,1,0:T(8,128)S(1)}, u32[]{:S(2)}, u32[]{:S(2)}) collective-permute-start(f32[7,32,384]{2,1,0:T(8,128)S(1)} %get-tuple-element.119), channel_id=1, source_target_pairs={{1,0},{2,1},{3,2},{4,3},{5,4},{6,5},{7,6},{0,7},{9,8},{10,9},{11,1... | collective-permute-start | bytes 1032200 | tf_op jit(solution)/shard_map/ppermute | solution.py:494
  83.7 4.1 %local_step.12 = (f32[16,32,384]{2,1,0:T(8,128)S(1)}, f32[16,32,384]{2,1,0:T(8,128)S(1)}, f32[16,32,384]{2,1,0:T(8,128)S(1)}) custom-call(f32[16,32,384]{2,1,0:T(8,128)S(1)} %get-tuple-element.118.refs_0_.pm_ref.before_ref, bf16[4,384,384]{2,1,0:T(8,128)(2,1)S(1)} %get-tuple-element.82.refs_1_, f32[16,32,384]{2,1,0:T(8,128)S(1)} %get-tuple-element.76.k_ref.refs_2_, ...), custom_call_target="tpu_custom_call" | custom-call | tf_op jit(solution)/shard_map/local_step/pallas_call | solution.py:327
  88.6 2.4 %update_step.13 = (f32[16,32,384]{2,1,0:T(8,128)}, f32[16,32,384]{2,1,0:T(8,128)S(1)}, f32[7,32,384]{2,1,0:T(8,128)S(1)}, f32[7,32,384]{2,1,0:T(8,128)S(1)}) custom-call(s32[5]{0:T(128)S(1)} %pad_add_fusion.place_ref, f32[7,32,384]{2,1,0:T(8,128)S(1)} %collective-permute-done.12.pl_ref, f32[16,32,384]{2,1,0:T(8,128)S(1)} %get-tuple-element.118.refs_0_.pm_ref.before_ref, ...), custom_call_target="tpu_custom_call" | custom-call | tf_op jit(solution)/shard_map/update_step/pallas_call | solution.py:442
  90.9 3.0 %collective-permute-start.15 = (f32[7,32,384]{2,1,0:T(8,128)S(1)}, f32[7,32,384]{2,1,0:T(8,128)S(1)}, u32[]{:S(2)}, u32[]{:S(2)}) collective-permute-start(f32[7,32,384]{2,1,0:T(8,128)S(1)} %get-tuple-element.126), channel_id=1, source_target_pairs={{1,0},{2,1},{3,2},{4,3},{5,4},{6,5},{7,6},{0,7},{9,8},{10,9},{11,1... | collective-permute-start | bytes 1032200 | tf_op jit(solution)/shard_map/ppermute | solution.py:494
  95.0 4.1 %local_step.13 = (f32[16,32,384]{2,1,0:T(8,128)S(1)}, f32[16,32,384]{2,1,0:T(8,128)S(1)}, f32[16,32,384]{2,1,0:T(8,128)S(1)}) custom-call(f32[16,32,384]{2,1,0:T(8,128)S(1)} %copy-done, bf16[4,384,384]{2,1,0:T(8,128)(2,1)S(1)} %get-tuple-element.82.refs_1_, f32[16,32,384]{2,1,0:T(8,128)S(1)} %get-tuple-element.76.k_ref.refs_2_, ...), custom_call_target="tpu_custom_call" | custom-call | tf_op jit(solution)/shard_map/local_step/pallas_call | solution.py:327
  99.2 2.6 %last_step.1 = (f32[16,32,384]{2,1,0:T(8,128)}, f32[16,4,16,384]{3,2,1,0:T(8,128)S(1)}) custom-call(s32[5]{0:T(128)S(1)} %pad_add_fusion.place_ref, f32[7,32,384]{2,1,0:T(8,128)S(1)} %collective-permute-done.14.pl_ref, f32[16,32,384]{2,1,0:T(8,128)S(1)} %copy-done.1, f32[7,32,384]{2,1,0:T(8,128)S(1)} %collective-permute-done.15.pr_ref, ...), custom_call_target="tpu_custom_call" | custom-call | tf_op jit(solution)/shard_map/last_step/pallas_call | solution.py:456
  101.8 23.5 %all_to_all.17.refs_0_ = f32[16,4,16,384]{3,2,1,0:T(8,128)S(1)} all-to-all(f32[16,4,16,384]{3,2,1,0:T(8,128)S(1)} %get-tuple-element.133), channel_id=1, replica_groups=mesh['shot'=16,'sub'=8] {'shot'}, dimensions={0} | all-to-all | bytes 3145728 | tf_op jit(solution)/shard_map/all_to_all | solution.py:543
  (36 shorter events, 12.8 us)
Async XLA Ops:
  0.6 15.9 %copy-start.2 = (s32[1,3]{1,0:T(1,128)S(1)}, s32[1,3]{1,0:T(1,128)}, u32[]{:S(2)}) copy-start(s32[1,3]{1,0:T(1,128)} %param.23) | copy-start | bytes 40
  3.6 28.4 %collective-permute-start = (f32[11,32,384]{2,1,0:T(8,128)S(1)}, f32[11,32,384]{2,1,0:T(8,128)S(1)}, u32[]{:S(2)}, u32[]{:S(2)}) collective-permute-start(f32[11,32,384]{2,1,0:T(8,128)S(1)} %get-tuple-element.71), channel_id=1, source_target_pairs={{0,1},{1,2},{2,3},{3,4},{4,5},{5,6},{6,7},{7,0},{8,9},{9,10},{10,1... | collective-permute-start | bytes 1622024 | tf_op jit(solution)/shard_map/ppermute | solution.py:493
  3.6 28.4 %collective-permute-start.1 = (f32[10,32,384]{2,1,0:T(8,128)S(1)}, f32[10,32,384]{2,1,0:T(8,128)S(1)}, u32[]{:S(2)}, u32[]{:S(2)}) collective-permute-start(f32[10,32,384]{2,1,0:T(8,128)S(1)} %get-tuple-element.74), channel_id=1, source_target_pairs={{1,0},{2,1},{3,2},{4,3},{5,4},{6,5},{7,6},{0,7},{9,8},{10,9},{11,1... | collective-permute-start | bytes 1474568 | tf_op jit(solution)/shard_map/ppermute | solution.py:494
  6.6 19.2 %all-to-all-start = ((f32[128,1,128]{2,1,0:T(1,128)}), f32[128,1,128]{2,1,0:T(1,128)S(1)}, u32[]{:S(2)}, u32[]{:S(2)}) async-start(f32[128,1,128]{2,1,0:T(1,128)} %bitcast.4), calls=%async_computation | async-start | bytes 131072 | tf_op jit(solution)/shard_map/all_to_all | solution.py:521
  33.5 7.9 %collective-permute-start.2 = (f32[7,32,384]{2,1,0:T(8,128)S(1)}, f32[7,32,384]{2,1,0:T(8,128)S(1)}, u32[]{:S(2)}, u32[]{:S(2)}) collective-permute-start(f32[7,32,384]{2,1,0:T(8,128)S(1)} %get-tuple-element.79), channel_id=1, source_target_pairs={{0,1},{1,2},{2,3},{3,4},{4,5},{5,6},{6,7},{7,0},{8,9},{9,10},{10,1... | collective-permute-start | bytes 1032200 | tf_op jit(solution)/shard_map/ppermute | solution.py:493
  33.5 7.9 %collective-permute-start.3 = (f32[7,32,384]{2,1,0:T(8,128)S(1)}, f32[7,32,384]{2,1,0:T(8,128)S(1)}, u32[]{:S(2)}, u32[]{:S(2)}) collective-permute-start(f32[7,32,384]{2,1,0:T(8,128)S(1)} %get-tuple-element.81), channel_id=1, source_target_pairs={{1,0},{2,1},{3,2},{4,3},{5,4},{6,5},{7,6},{0,7},{9,8},{10,9},{11,1... | collective-permute-start | bytes 1032200 | tf_op jit(solution)/shard_map/ppermute | solution.py:494
  42.9 7.9 %collective-permute-start.4 = (f32[7,32,384]{2,1,0:T(8,128)S(1)}, f32[7,32,384]{2,1,0:T(8,128)S(1)}, u32[]{:S(2)}, u32[]{:S(2)}) collective-permute-start(f32[7,32,384]{2,1,0:T(8,128)S(1)} %get-tuple-element.89), channel_id=1, source_target_pairs={{0,1},{1,2},{2,3},{3,4},{4,5},{5,6},{6,7},{7,0},{8,9},{9,10},{10,1... | collective-permute-start | bytes 1032200 | tf_op jit(solution)/shard_map/ppermute | solution.py:493
  42.9 7.9 %collective-permute-start.5 = (f32[7,32,384]{2,1,0:T(8,128)S(1)}, f32[7,32,384]{2,1,0:T(8,128)S(1)}, u32[]{:S(2)}, u32[]{:S(2)}) collective-permute-start(f32[7,32,384]{2,1,0:T(8,128)S(1)} %get-tuple-element.91), channel_id=1, source_target_pairs={{1,0},{2,1},{3,2},{4,3},{5,4},{6,5},{7,6},{0,7},{9,8},{10,9},{11,1... | collective-permute-start | bytes 1032200 | tf_op jit(solution)/shard_map/ppermute | solution.py:494
  52.2 7.9 %collective-permute-start.6 = (f32[7,32,384]{2,1,0:T(8,128)S(1)}, f32[7,32,384]{2,1,0:T(8,128)S(1)}, u32[]{:S(2)}, u32[]{:S(2)}) collective-permute-start(f32[7,32,384]{2,1,0:T(8,128)S(1)} %get-tuple-element.96), channel_id=1, source_target_pairs={{0,1},{1,2},{2,3},{3,4},{4,5},{5,6},{6,7},{7,0},{8,9},{9,10},{10,1... | collective-permute-start | bytes 1032200 | tf_op jit(solution)/shard_map/ppermute | solution.py:493
  52.3 7.9 %collective-permute-start.7 = (f32[7,32,384]{2,1,0:T(8,128)S(1)}, f32[7,32,384]{2,1,0:T(8,128)S(1)}, u32[]{:S(2)}, u32[]{:S(2)}) collective-permute-start(f32[7,32,384]{2,1,0:T(8,128)S(1)} %get-tuple-element.98), channel_id=1, source_target_pairs={{1,0},{2,1},{3,2},{4,3},{5,4},{6,5},{7,6},{0,7},{9,8},{10,9},{11,1... | collective-permute-start | bytes 1032200 | tf_op jit(solution)/shard_map/ppermute | solution.py:494
  61.8 7.9 %collective-permute-start.8 = (f32[7,32,384]{2,1,0:T(8,128)S(1)}, f32[7,32,384]{2,1,0:T(8,128)S(1)}, u32[]{:S(2)}, u32[]{:S(2)}) collective-permute-start(f32[7,32,384]{2,1,0:T(8,128)S(1)} %get-tuple-element.103), channel_id=1, source_target_pairs={{0,1},{1,2},{2,3},{3,4},{4,5},{5,6},{6,7},{7,0},{8,9},{9,10},{10,1... | collective-permute-start | bytes 1032200 | tf_op jit(solution)/shard_map/ppermute | solution.py:493
  61.9 7.9 %collective-permute-start.9 = (f32[7,32,384]{2,1,0:T(8,128)S(1)}, f32[7,32,384]{2,1,0:T(8,128)S(1)}, u32[]{:S(2)}, u32[]{:S(2)}) collective-permute-start(f32[7,32,384]{2,1,0:T(8,128)S(1)} %get-tuple-element.105), channel_id=1, source_target_pairs={{1,0},{2,1},{3,2},{4,3},{5,4},{6,5},{7,6},{0,7},{9,8},{10,9},{11,1... | collective-permute-start | bytes 1032200 | tf_op jit(solution)/shard_map/ppermute | solution.py:494
  71.2 7.9 %collective-permute-start.10 = (f32[7,32,384]{2,1,0:T(8,128)S(1)}, f32[7,32,384]{2,1,0:T(8,128)S(1)}, u32[]{:S(2)}, u32[]{:S(2)}) collective-permute-start(f32[7,32,384]{2,1,0:T(8,128)S(1)} %get-tuple-element.110), channel_id=1, source_target_pairs={{0,1},{1,2},{2,3},{3,4},{4,5},{5,6},{6,7},{7,0},{8,9},{9,10},{10,1... | collective-permute-start | bytes 1032200 | tf_op jit(solution)/shard_map/ppermute | solution.py:493
  71.3 7.9 %collective-permute-start.11 = (f32[7,32,384]{2,1,0:T(8,128)S(1)}, f32[7,32,384]{2,1,0:T(8,128)S(1)}, u32[]{:S(2)}, u32[]{:S(2)}) collective-permute-start(f32[7,32,384]{2,1,0:T(8,128)S(1)} %get-tuple-element.112), channel_id=1, source_target_pairs={{1,0},{2,1},{3,2},{4,3},{5,4},{6,5},{7,6},{0,7},{9,8},{10,9},{11,1... | collective-permute-start | bytes 1032200 | tf_op jit(solution)/shard_map/ppermute | solution.py:494
  80.6 7.9 %collective-permute-start.12 = (f32[7,32,384]{2,1,0:T(8,128)S(1)}, f32[7,32,384]{2,1,0:T(8,128)S(1)}, u32[]{:S(2)}, u32[]{:S(2)}) collective-permute-start(f32[7,32,384]{2,1,0:T(8,128)S(1)} %get-tuple-element.117), channel_id=1, source_target_pairs={{0,1},{1,2},{2,3},{3,4},{4,5},{5,6},{6,7},{7,0},{8,9},{9,10},{10,1... | collective-permute-start | bytes 1032200 | tf_op jit(solution)/shard_map/ppermute | solution.py:493
  80.7 7.9 %collective-permute-start.13 = (f32[7,32,384]{2,1,0:T(8,128)S(1)}, f32[7,32,384]{2,1,0:T(8,128)S(1)}, u32[]{:S(2)}, u32[]{:S(2)}) collective-permute-start(f32[7,32,384]{2,1,0:T(8,128)S(1)} %get-tuple-element.119), channel_id=1, source_target_pairs={{1,0},{2,1},{3,2},{4,3},{5,4},{6,5},{7,6},{0,7},{9,8},{10,9},{11,1... | collective-permute-start | bytes 1032200 | tf_op jit(solution)/shard_map/ppermute | solution.py:494
  90.9 8.2 %collective-permute-start.14 = (f32[7,32,384]{2,1,0:T(8,128)S(1)}, f32[7,32,384]{2,1,0:T(8,128)S(1)}, u32[]{:S(2)}, u32[]{:S(2)}) collective-permute-start(f32[7,32,384]{2,1,0:T(8,128)S(1)} %get-tuple-element.124), channel_id=1, source_target_pairs={{0,1},{1,2},{2,3},{3,4},{4,5},{5,6},{6,7},{7,0},{8,9},{9,10},{10,1... | collective-permute-start | bytes 1032200 | tf_op jit(solution)/shard_map/ppermute | solution.py:493
  90.9 8.2 %collective-permute-start.15 = (f32[7,32,384]{2,1,0:T(8,128)S(1)}, f32[7,32,384]{2,1,0:T(8,128)S(1)}, u32[]{:S(2)}, u32[]{:S(2)}) collective-permute-start(f32[7,32,384]{2,1,0:T(8,128)S(1)} %get-tuple-element.126), channel_id=1, source_target_pairs={{1,0},{2,1},{3,2},{4,3},{5,4},{6,5},{7,6},{0,7},{9,8},{10,9},{11,1... | collective-permute-start | bytes 1032200 | tf_op jit(solution)/shard_map/ppermute | solution.py:494
  93.9 1.1 copy-start
  95.0 4.1 %copy-start.1 = (f32[16,32,384]{2,1,0:T(8,128)S(1)}, f32[16,32,384]{2,1,0:T(8,128)}, u32[]{:S(2)}) copy-start(f32[16,32,384]{2,1,0:T(8,128)} %get-tuple-element.125.refs_0_.pm_ref) | copy-start | bytes 2359300

commit v4 on v3

--- a/solution.py
+++ b/solution.py
@@ -1,6 +1,5 @@
 import jax
 import jax.numpy as jnp
-import ml_dtypes
 import numpy as np
 from jax import lax
 from jax.experimental import pallas as pl
@@ -153,21 +152,19 @@
     return total
 
 
-def band_matrices(nz):
-    forward = np.zeros((nz, nz), np.float64)
-    for face in range(nz):
+def fill_bands(bands_ref):
+    nz = bands_ref.shape[1]
+    gap = lax.broadcasted_iota(jnp.int32, (nz, nz), 0) - lax.broadcasted_iota(
+        jnp.int32, (nz, nz), 1
+    )
+    for side in range(2):
+        band = jnp.zeros((nz, nz), F32)
         for k in range(1, 5):
-            if face + k < nz:
-                forward[face + k, face] += COEFFS[k - 1]
-            if face + 1 - k >= 0:
-                forward[face + 1 - k, face] -= COEFFS[k - 1]
-    pieces = []
-    for matrix in (forward, -forward.T):
-        full = matrix.astype(np.float32)
-        high = full.astype(ml_dtypes.bfloat16)
-        low = (full - high.astype(np.float32)).astype(ml_dtypes.bfloat16)
-        pieces += [high, low]
-    return np.stack(pieces)
+            band = jnp.where(gap == k - side, COEFFS[k - 1], band)
+            band = jnp.where(gap == 1 - k - side, -COEFFS[k - 1], band)
+        high, low = split2(band)
+        bands_ref[2 * side] = high
+        bands_ref[2 * side + 1] = low
 
 
 def banded(value, bands_ref, first):
@@ -207,11 +204,13 @@
 def local_change(
     p_ref, k_ref, b2_ref, b3_ref, bands_ref, got_ref, turned, moment, out_ref, scratch, and_then=None
 ):
-    ps_ref, qs_ref, spread_ref, added_ref, third_ref = scratch
+    ps_ref, qs_ref, third_ref, *more = scratch
     nx, ny, nz = p_ref.shape
     clear_edges(ps_ref, qs_ref, ny)
-    fill_columns(got_ref, spread_ref, moment, nz)
-    added_ref[...] = inject_rows(turned, spread_ref, 0, nx * ny).reshape(nx, ny, nz)
+    if got_ref is not None:
+        spread_ref, added_ref = more
+        fill_columns(got_ref, spread_ref, moment, nz)
+        added_ref[...] = inject_rows(turned, spread_ref, 0, nx * ny).reshape(nx, ny, nz)
     third_ref[...] = along_third(p_ref, b3_ref, bands_ref).reshape(nx, ny, nz)
     count = nz // 128
 
@@ -221,9 +220,10 @@
             for c in range(count):
                 lanes = slice(c * 128, c * 128 + 128)
                 second = along_second(p_ref, b2_ref, x, lanes, ps_ref, qs_ref, index * count + c)
-                out_ref[x, :, lanes] = (
-                    k_ref[x, :, lanes] * (second + third_ref[x, :, lanes]) + added_ref[x, :, lanes]
-                )
+                value = k_ref[x, :, lanes] * (second + third_ref[x, :, lanes])
+                if got_ref is not None:
+                    value = value + added_ref[x, :, lanes]
+                out_ref[x, :, lanes] = value
             if and_then is not None:
                 and_then(x)
         return carry
@@ -231,12 +231,12 @@
     lax.fori_loop(0, nx // GROUP, planes, 0)
 
 
-def local_scratch(nx, ny, nz):
-    return [shift_scratch(ny, nz)] * 2 + [
-        pltpu.VMEM((2, SLOTS * 128, nz), BF16),
-        pltpu.VMEM((nx, ny, nz), F32),
-        pltpu.VMEM((nx, ny, nz), F32),
-    ]
+def local_scratch(nx, ny, nz, injects=True):
+    field = pltpu.VMEM((nx, ny, nz), F32)
+    found = [shift_scratch(ny, nz)] * 2 + [field]
+    if injects:
+        found += [pltpu.VMEM((2, SLOTS * 128, nz), BF16), field]
+    return found
 
 
 def clear_edges(ps_ref, qs_ref, ny):
@@ -247,48 +247,84 @@
 
 
 GROUP = 4
-LOADS = 5
 
 
 def first_local_kernel(
-    got_ref, p_far, bands_far, k_far, b2_far, b3_far, b1_far, before_far, frames_far,
-    out_ref, turned_ref, p_ref, bands_ref, k_ref, b2_ref, b3_ref, b1_ref, before_ref, frames_ref,
-    *scratch,
+    p_far, k_far, b2_far, b3_far, out_far,
+    p_ref, k_ref, b2_ref, b3_ref, out_ref, bands_ref, sems, *scratch,
 ):
-    *scratch, sems = scratch
-    far = (p_far, bands_far, k_far, b2_far, b3_far, b1_far, before_far, frames_far)
-    near = (p_ref, bands_ref, k_ref, b2_ref, b3_ref, b1_ref, before_ref, frames_ref)
+    far = (p_far, k_far, b2_far, b3_far)
+    near = (p_ref, k_ref, b2_ref, b3_ref)
     copies = [pltpu.make_async_copy(f, n, sems.at[i]) for i, (f, n) in enumerate(zip(far, near))]
     for copy in copies:
         copy.start()
-    turned_ref[...] = got_ref[...].T
-    for copy in copies[:LOADS]:
+    fill_bands(bands_ref)
+    for copy in copies:
         copy.wait()
-    local_change(
-        p_ref, k_ref, b2_ref, b3_ref, bands_ref, got_ref, turned_ref[...], 0, out_ref, scratch
-    )
-    for copy in copies[LOADS:]:
-        copy.wait()
+    local_change(p_ref, k_ref, b2_ref, b3_ref, bands_ref, None, None, 0, out_ref, scratch)
+    store = pltpu.make_async_copy(out_ref, out_far, sems.at[4])
+    store.start()
+    store.wait()
 
 
 def shift_scratch(ny, nz):
     return pltpu.VMEM((GROUP * (nz // 128), ny + 16, 128), F32)
 
 
-def first_local(got, *arrays):
+def first_local(*arrays):
     nx, ny, nz = arrays[0].shape
+    far = pl.BlockSpec(memory_space=pltpu.HBM)
+    return pl.pallas_call(
+        first_local_kernel,
+        in_specs=[far] * 4,
+        out_specs=far,
+        out_shape=shape_of(nx, ny, nz),
+        scratch_shapes=[pltpu.VMEM((nx, ny, nz), F32)] * 5
+        + [pltpu.VMEM((4, nz, nz), BF16), pltpu.SemaphoreType.DMA((5,))]
+        + local_scratch(nx, ny, nz, False),
+        compiler_params=pltpu.CompilerParams(vmem_limit_bytes=16 * 1024 * 1024),
+        name="first_local",
+    )(*far_away(*arrays))
+
+
+def first_inject_kernel(got_ref, local_far, *refs):
+    count = (len(refs) - 6) // 2
+    far, (out_ref, turned_ref, bands_ref), near = refs[:count], refs[count : count + 3], refs[count + 3 : -3]
+    near_local_ref, spread_ref, sems = refs[-3:]
+    first = pltpu.make_async_copy(local_far, near_local_ref, sems.at[0])
+    first.start()
+    copies = [pltpu.make_async_copy(f, n, sems.at[i + 1]) for i, (f, n) in enumerate(zip(far, near))]
+    for copy in copies:
+        copy.start()
+    nx, ny, nz = out_ref.shape
+    turned_ref[...] = got_ref[...].T
+    fill_columns(got_ref, spread_ref, 0, nz)
+    added = inject_rows(turned_ref[...], spread_ref, 0, nx * ny).reshape(nx, ny, nz)
+    first.wait()
+    out_ref[...] = near_local_ref[...] + added
+    fill_bands(bands_ref)
+    for copy in copies:
+        copy.wait()
+
+
+def first_inject(got, nearby, *arrays):
+    nx, ny, nz = nearby.shape
     vmem = pl.BlockSpec(memory_space=pltpu.VMEM)
     far = pl.BlockSpec(memory_space=pltpu.HBM)
     return pl.pallas_call(
-        first_local_kernel,
-        in_specs=[vmem] + [far] * len(arrays),
-        out_specs=[vmem] * (2 + len(arrays)),
-        out_shape=[shape_of(nx, ny, nz), shape_of(128, 128)]
+        first_inject_kernel,
+        in_specs=[vmem] + [far] * (1 + len(arrays)),
+        out_specs=[vmem] * (3 + len(arrays)),
+        out_shape=[shape_of(nx, ny, nz), shape_of(128, 128), shape_of(4, nz, nz, dtype=BF16)]
         + [shape_of(*a.shape, dtype=a.dtype) for a in arrays],
-        scratch_shapes=local_scratch(nx, ny, nz) + [pltpu.SemaphoreType.DMA((len(arrays),))],
+        scratch_shapes=[
+            pltpu.VMEM((nx, ny, nz), F32),
+            pltpu.VMEM((2, SLOTS * 128, nz), BF16),
+            pltpu.SemaphoreType.DMA((1 + len(arrays),)),
+        ],
         compiler_params=PARAMS,
-        name="first_local",
-    )(got, *far_away(*arrays))
+        name="first_inject",
+    )(got, *far_away(nearby, *arrays))
 
 
 def make_local_kernel(moment):
@@ -408,9 +444,11 @@
 
 def last_kernel(
     place_ref, pl_ref, pm_ref, pr_ref, bl_ref, bm_ref, br_ref, k_ref, local_ref,
-    before_ref, image_ref, f_ref, light_ref, next_ref, muted_ref, kept_ref,
+    before_ref, image_ref, f_ref, light_ref, now_far, next_ref, muted_ref, kept_ref, sem,
 ):
     nx, ny, nz = pm_ref.shape
+    store = pltpu.make_async_copy(pm_ref, now_far, sem)
+    store.start()
     steps = f_ref.shape[0]
     edges = edge_factors(place_ref, nx)
     second = lax.broadcasted_iota(jnp.int32, (8, 128), 0).astype(F32)
@@ -435,6 +473,7 @@
     for y in range(ny):
         muted_ref[y // 2, y % 2, :, :] = kept_ref[:, y, :]
         muted_ref[y // 2, 2 + y % 2, :, :] = light_ref[:, y, :]
+    store.wait()
 
 
 def update_step(place, halos, current, b1_halos, b1, stiffness, local, before):
@@ -456,9 +495,9 @@
     return pl.pallas_call(
         last_kernel,
         in_specs=[smem] + [vmem] * 12,
-        out_specs=[vmem] * 2,
-        out_shape=[shape_of(nx, ny, nz), shape_of(ny // 2, 4, nx, nz)],
-        scratch_shapes=[pltpu.VMEM((nx, ny, nz), F32)],
+        out_specs=[pl.BlockSpec(memory_space=pltpu.HBM)] + [vmem] * 2,
+        out_shape=[shape_of(nx, ny, nz)] * 2 + [shape_of(ny // 2, 4, nx, nz)],
+        scratch_shapes=[pltpu.VMEM((nx, ny, nz), F32), pltpu.SemaphoreType.DMA],
         compiler_params=PARAMS,
         name="last_step",
     )(
@@ -521,10 +560,10 @@
     got = lax.all_to_all(send, both, split_axis=0, concat_axis=0, tiled=True)
     halos = exchange(left, right)
     b1_halos = halos
+    nearby = first_local(current, stiffness, b2, b3)
     got, place = lax.optimization_barrier((got, place))
-    bands = jnp.asarray(band_matrices(current.shape[2]))
-    nearby, turned, current, bands, stiffness, b2, b3, b1, before, frames = first_local(
-        got, current, bands, stiffness, b2, b3, b1, before, forward
+    nearby, turned, bands, current, stiffness, b2, b3, b1, before, frames = first_inject(
+        got, nearby, current, stiffness, b2, b3, b1, before, forward
     )
 
     image = light = None
@@ -537,12 +576,12 @@
         nearby, image, light = local_step(
             moment + 1, current, bands, stiffness, b2, b3, frames, change, (image, light), got, turned
         )
-    following, sums = last_step(
+    now, following, sums = last_step(
         place, halos, current, b1_halos, b1, stiffness, nearby, before, image, frames, light
     )
     sums = lax.all_to_all(sums, "shot", split_axis=0, concat_axis=0, tiled=True)
     gradient = quotient(sums, 1.0 / (steps * lax.axis_size("shot")))
-    return gradient, current[None], following[None]
+    return gradient, now[None], following[None]
 
 
 def solution(mesh):

time: 127 us -> 124 us (0.976)
  waiting for transfers between devices: 14 us -> 9.07 us
  Pallas kernels: 52.6 us -> 55.1 us
    all_to_all x1, waiting for transfers between devices: 9.14 us -> 3.44 us  [local(): got = lax.all_to_all(send, both, split_axis=0, concat_axis=0, tiled=True)]
    pallas_call x2 -> x3, Pallas kernels: 8.85 us -> 12 us  [the longest x1 4.81 us: first_local(): pl.pallas_call(first_local_kernel, in_specs=[far] * 4, out_specs=far, out...]
  transfers between devices with their start and end apart: 17 -> 17, of which waited for: 7 -> 8; matrix products, arithmetic and copies ran while one was open for 0% -> 0% of each run, Pallas kernels for 28% -> 31%
where the time goes in v4:
time: 124 us; the launch traced here: 123 us
  Pallas kernels  55.1 us (44%)
  starting transfers between devices  33.9 us (27%)
  blocking collectives  22.9 us (18%)
  waiting for transfers between devices  9.07 us (7%)
    pallas_call x7, Pallas kernels, local_step(): pl.pallas_call(make_local_kernel(moment), in_specs=[pl.BlockSpec(memory_s...  28.7 us
    ppermute x8, starting transfers between devices, exchange(): lax.ppermute(head, 'sub', [((i + 1) % count, i) for i in range(count)])  23.8 us
    all_to_all x1, blocking collectives, local(): sums = lax.all_to_all(sums, 'shot', split_axis=0, concat_axis=0, tiled=True)  22.9 us
    pallas_call x7, Pallas kernels, update_step(): pl.pallas_call(update_kernel, in_specs=[pl.BlockSpec(memory_space=pltpu.S...  10.7 us
    all_to_all x1, starting transfers between devices, local(): got = lax.all_to_all(send, both, split_axis=0, concat_axis=0, tiled=True)  9.94 us
    ppermute x8, waiting for transfers between devices, exchange(): lax.ppermute(tail, 'sub', [(i, (i + 1) % count) for i in range(count)])  5.6 us
    pallas_call x1, Pallas kernels, first_local(): pl.pallas_call(first_local_kernel, in_specs=[far] * 4, out_specs=far, out...  4.81 us
    pallas_call x1, Pallas kernels, first_inject(): pl.pallas_call(first_inject_kernel, in_specs=[vmem] + [far] * (1 + len(ar...  4.2 us
  transfers between devices with their start and end apart: 17, of which 8 were waited for; matrix products, arithmetic and copies ran while one was open for 0% of the time, Pallas kernels for 31%

profile of v4, /device:TPU:0, one launch (start us, length us, event | category | flops | bytes accessed | tf_op | source)
XLA Modules:
  0.0 122.7 jit_solution(6146972310653328528)
XLA Ops:
  0.6 2.9 %prep.1 = (f32[128,128]{1,0:T(8,128)}, f32[11,32,384]{2,1,0:T(8,128)S(1)}, f32[10,32,384]{2,1,0:T(8,128)S(1)}) custom-call(f32[512,256]{1,0:T(8,128)} %refs_0_.1, f32[128,256]{1,0:T(8,128)} %constant.10.clone.refs_1_, s32[1,512]{1,0:T(1,128)} %bitcast.26, s32[1,512]{1,0:T(1,128)} %bitcast.27, f32[16,32,384]{2,1,0:T(8,128)} %bitcast.21, f32[16,32,384]{2,1,0:T(8,128)} %refs_4_.1), custom_call_target="tpu_custom_call" | custom-call | tf_op jit(solution)/shard_map/prep/pallas_call | solution.py:105
  3.6 2.9 %collective-permute-start.1 = (f32[10,32,384]{2,1,0:T(8,128)S(1)}, f32[10,32,384]{2,1,0:T(8,128)S(1)}, u32[]{:S(2)}, u32[]{:S(2)}) collective-permute-start(f32[10,32,384]{2,1,0:T(8,128)S(1)} %get-tuple-element.75), channel_id=1, source_target_pairs={{1,0},{2,1},{3,2},{4,3},{5,4},{6,5},{7,6},{0,7},{9,8},{10,9},{11,1... | collective-permute-start | bytes 1474568 | tf_op jit(solution)/shard_map/ppermute | solution.py:533
  6.5 9.9 %all-to-all-start = ((f32[128,1,128]{2,1,0:T(1,128)}), f32[128,1,128]{2,1,0:T(1,128)S(1)}, u32[]{:S(2)}, u32[]{:S(2)}) async-start(f32[128,1,128]{2,1,0:T(1,128)} %bitcast.4), calls=%async_computation | async-start | bytes 131072 | tf_op jit(solution)/shard_map/all_to_all | solution.py:560
  16.5 4.8 %first_local.1.local_far = f32[16,32,384]{2,1,0:T(8,128)S(1)} custom-call(f32[16,32,384]{2,1,0:T(8,128)} %bitcast.22, f32[16,32,384]{2,1,0:T(8,128)} %refs_1_.2, f32[16,32,384]{2,1,0:T(8,128)} %refs_2_.1, f32[16,32,384]{2,1,0:T(8,128)} %refs_3_.1), custom_call_target="tpu_custom_call" | custom-call | tf_op jit(solution)/shard_map/first_local/pallas_call | solution.py:277
  22.3 3.4 %all-to-all-done = f32[128,1,128]{2,1,0:T(1,128)S(1)} async-done(((f32[128,1,128]{2,1,0:T(1,128)}), f32[128,1,128]{2,1,0:T(1,128)S(1)}, u32[]{:S(2)}, u32[]{:S(2)}) %all-to-all-start) | async-done | bytes 65568 | tf_op jit(solution)/shard_map/all_to_all | solution.py:560
  25.7 4.2 %first_inject.1 = (f32[16,32,384]{2,1,0:T(8,128)S(1)}, f32[128,128]{1,0:T(8,128)S(1)}, bf16[4,384,384]{2,1,0:T(8,128)(2,1)S(1)}, f32[16,32,384]{2,1,0:T(8,128)S(...) custom-call(f32[128,128]{1,0:T(8,128)S(1)} %bitcast.13, ...), custom_call_target="tpu_custom_call" | custom-call | tf_op jit(solution)/shard_map/first_inject/pallas_call | solution.py:314
  31.5 2.9 %collective-permute-start.3 = (f32[7,32,384]{2,1,0:T(8,128)S(1)}, f32[7,32,384]{2,1,0:T(8,128)S(1)}, u32[]{:S(2)}, u32[]{:S(2)}) collective-permute-start(f32[7,32,384]{2,1,0:T(8,128)S(1)} %get-tuple-element.82), channel_id=1, source_target_pairs={{1,0},{2,1},{3,2},{4,3},{5,4},{6,5},{7,6},{0,7},{9,8},{10,9},{11,1... | collective-permute-start | bytes 1032200 | tf_op jit(solution)/shard_map/ppermute | solution.py:533
  34.4 4.0 %local_step.7 = (f32[16,32,384]{2,1,0:T(8,128)S(1)}, f32[16,32,384]{2,1,0:T(8,128)S(1)}, f32[16,32,384]{2,1,0:T(8,128)S(1)}) custom-call(f32[16,32,384]{2,1,0:T(8,128)S(1)} %get-tuple-element.81.refs_0_.pm_ref.before_ref, bf16[4,384,384]{2,1,0:T(8,128)(2,1)S(1)} %get-tuple-element.83.refs_1_, f32[16,32,384]{2,1,0:T(8,128)S(1)} %get-tuple-element.77.k_ref.refs_2_, ...), custom_call_target="tpu_custom_call" | custom-call | tf_op jit(solution)/shard_map/local_step/pallas_call | solution.py:363
  40.8 3.0 %collective-permute-start.5 = (f32[7,32,384]{2,1,0:T(8,128)S(1)}, f32[7,32,384]{2,1,0:T(8,128)S(1)}, u32[]{:S(2)}, u32[]{:S(2)}) collective-permute-start(f32[7,32,384]{2,1,0:T(8,128)S(1)} %get-tuple-element.92), channel_id=1, source_target_pairs={{1,0},{2,1},{3,2},{4,3},{5,4},{6,5},{7,6},{0,7},{9,8},{10,9},{11,1... | collective-permute-start | bytes 1032200 | tf_op jit(solution)/shard_map/ppermute | solution.py:533
  43.8 4.1 %local_step.8 = (f32[16,32,384]{2,1,0:T(8,128)S(1)}, f32[16,32,384]{2,1,0:T(8,128)S(1)}, f32[16,32,384]{2,1,0:T(8,128)S(1)}) custom-call(f32[16,32,384]{2,1,0:T(8,128)S(1)} %get-tuple-element.91.refs_0_.pm_ref.before_ref, bf16[4,384,384]{2,1,0:T(8,128)(2,1)S(1)} %get-tuple-element.83.refs_1_, f32[16,32,384]{2,1,0:T(8,128)S(1)} %get-tuple-element.77.k_ref.refs_2_, ...), custom_call_target="tpu_custom_call" | custom-call | tf_op jit(solution)/shard_map/local_step/pallas_call | solution.py:363
  48.7 1.7 %update_step.9 = (f32[16,32,384]{2,1,0:T(8,128)S(1)}, f32[16,32,384]{2,1,0:T(8,128)S(1)}, f32[7,32,384]{2,1,0:T(8,128)S(1)}, f32[7,32,384]{2,1,0:T(8,128)S(1)}) custom-call(s32[5]{0:T(128)S(1)} %pad_add_fusion.place_ref, f32[7,32,384]{2,1,0:T(8,128)S(1)} %collective-permute-done.4.pl_ref, f32[16,32,384]{2,1,0:T(8,128)S(1)} %get-tuple-element.91.refs_0_.pm_ref.before_ref, ...), custom_call_target="tpu_custom_call" | custom-call | tf_op jit(solution)/shard_map/update_step/pallas_call | solution.py:481
  50.4 3.0 %collective-permute-start.7 = (f32[7,32,384]{2,1,0:T(8,128)S(1)}, f32[7,32,384]{2,1,0:T(8,128)S(1)}, u32[]{:S(2)}, u32[]{:S(2)}) collective-permute-start(f32[7,32,384]{2,1,0:T(8,128)S(1)} %get-tuple-element.99), channel_id=1, source_target_pairs={{1,0},{2,1},{3,2},{4,3},{5,4},{6,5},{7,6},{0,7},{9,8},{10,9},{11,1... | collective-permute-start | bytes 1032200 | tf_op jit(solution)/shard_map/ppermute | solution.py:533
  53.4 4.1 %local_step.9 = (f32[16,32,384]{2,1,0:T(8,128)S(1)}, f32[16,32,384]{2,1,0:T(8,128)S(1)}, f32[16,32,384]{2,1,0:T(8,128)S(1)}) custom-call(f32[16,32,384]{2,1,0:T(8,128)S(1)} %get-tuple-element.98.refs_0_.pm_ref.before_ref, bf16[4,384,384]{2,1,0:T(8,128)(2,1)S(1)} %get-tuple-element.83.refs_1_, f32[16,32,384]{2,1,0:T(8,128)S(1)} %get-tuple-element.77.k_ref.refs_2_, ...), custom_call_target="tpu_custom_call" | custom-call | tf_op jit(solution)/shard_map/local_step/pallas_call | solution.py:363
  59.8 3.0 %collective-permute-start.9 = (f32[7,32,384]{2,1,0:T(8,128)S(1)}, f32[7,32,384]{2,1,0:T(8,128)S(1)}, u32[]{:S(2)}, u32[]{:S(2)}) collective-permute-start(f32[7,32,384]{2,1,0:T(8,128)S(1)} %get-tuple-element.106), channel_id=1, source_target_pairs={{1,0},{2,1},{3,2},{4,3},{5,4},{6,5},{7,6},{0,7},{9,8},{10,9},{11,1... | collective-permute-start | bytes 1032200 | tf_op jit(solution)/shard_map/ppermute | solution.py:533
  62.8 4.1 %local_step.10 = (f32[16,32,384]{2,1,0:T(8,128)S(1)}, f32[16,32,384]{2,1,0:T(8,128)S(1)}, f32[16,32,384]{2,1,0:T(8,128)S(1)}) custom-call(f32[16,32,384]{2,1,0:T(8,128)S(1)} %get-tuple-element.105.refs_0_.pm_ref.before_ref, bf16[4,384,384]{2,1,0:T(8,128)(2,1)S(1)} %get-tuple-element.83.refs_1_, f32[16,32,384]{2,1,0:T(8,128)S(1)} %get-tuple-element.77.k_ref.refs_2_, ...), custom_call_target="tpu_custom_call" | custom-call | tf_op jit(solution)/shard_map/local_step/pallas_call | solution.py:363
  69.2 3.0 %collective-permute-start.11 = (f32[7,32,384]{2,1,0:T(8,128)S(1)}, f32[7,32,384]{2,1,0:T(8,128)S(1)}, u32[]{:S(2)}, u32[]{:S(2)}) collective-permute-start(f32[7,32,384]{2,1,0:T(8,128)S(1)} %get-tuple-element.113), channel_id=1, source_target_pairs={{1,0},{2,1},{3,2},{4,3},{5,4},{6,5},{7,6},{0,7},{9,8},{10,9},{11,1... | collective-permute-start | bytes 1032200 | tf_op jit(solution)/shard_map/ppermute | solution.py:533
  72.2 4.1 %local_step.11 = (f32[16,32,384]{2,1,0:T(8,128)S(1)}, f32[16,32,384]{2,1,0:T(8,128)S(1)}, f32[16,32,384]{2,1,0:T(8,128)S(1)}) custom-call(f32[16,32,384]{2,1,0:T(8,128)S(1)} %get-tuple-element.112.refs_0_.pm_ref.before_ref, bf16[4,384,384]{2,1,0:T(8,128)(2,1)S(1)} %get-tuple-element.83.refs_1_, f32[16,32,384]{2,1,0:T(8,128)S(1)} %get-tuple-element.77.k_ref.refs_2_, ...), custom_call_target="tpu_custom_call" | custom-call | tf_op jit(solution)/shard_map/local_step/pallas_call | solution.py:363
  78.6 3.0 %collective-permute-start.13 = (f32[7,32,384]{2,1,0:T(8,128)S(1)}, f32[7,32,384]{2,1,0:T(8,128)S(1)}, u32[]{:S(2)}, u32[]{:S(2)}) collective-permute-start(f32[7,32,384]{2,1,0:T(8,128)S(1)} %get-tuple-element.120), channel_id=1, source_target_pairs={{1,0},{2,1},{3,2},{4,3},{5,4},{6,5},{7,6},{0,7},{9,8},{10,9},{11,1... | collective-permute-start | bytes 1032200 | tf_op jit(solution)/shard_map/ppermute | solution.py:533
  81.6 4.1 %local_step.12 = (f32[16,32,384]{2,1,0:T(8,128)S(1)}, f32[16,32,384]{2,1,0:T(8,128)S(1)}, f32[16,32,384]{2,1,0:T(8,128)S(1)}) custom-call(f32[16,32,384]{2,1,0:T(8,128)S(1)} %get-tuple-element.119.refs_0_.pm_ref.before_ref, bf16[4,384,384]{2,1,0:T(8,128)(2,1)S(1)} %get-tuple-element.83.refs_1_, f32[16,32,384]{2,1,0:T(8,128)S(1)} %get-tuple-element.77.k_ref.refs_2_, ...), custom_call_target="tpu_custom_call" | custom-call | tf_op jit(solution)/shard_map/local_step/pallas_call | solution.py:363
  86.5 1.7 %update_step.13 = (f32[16,32,384]{2,1,0:T(8,128)S(1)}, f32[16,32,384]{2,1,0:T(8,128)S(1)}, f32[7,32,384]{2,1,0:T(8,128)S(1)}, f32[7,32,384]{2,1,0:T(8,128)S(1)}) custom-call(s32[5]{0:T(128)S(1)} %pad_add_fusion.place_ref, f32[7,32,384]{2,1,0:T(8,128)S(1)} %collective-permute-done.12.pl_ref, f32[16,32,384]{2,1,0:T(8,128)S(1)} %get-tuple-element.119.refs_0_.pm_ref.before_ref, ...), custom_call_target="tpu_custom_call" | custom-call | tf_op jit(solution)/shard_map/update_step/pallas_call | solution.py:481
  88.2 3.0 %collective-permute-start.15 = (f32[7,32,384]{2,1,0:T(8,128)S(1)}, f32[7,32,384]{2,1,0:T(8,128)S(1)}, u32[]{:S(2)}, u32[]{:S(2)}) collective-permute-start(f32[7,32,384]{2,1,0:T(8,128)S(1)} %get-tuple-element.127), channel_id=1, source_target_pairs={{1,0},{2,1},{3,2},{4,3},{5,4},{6,5},{7,6},{0,7},{9,8},{10,9},{11,1... | collective-permute-start | bytes 1032200 | tf_op jit(solution)/shard_map/ppermute | solution.py:533
  91.2 4.2 %local_step.13 = (f32[16,32,384]{2,1,0:T(8,128)S(1)}, f32[16,32,384]{2,1,0:T(8,128)S(1)}, f32[16,32,384]{2,1,0:T(8,128)S(1)}) custom-call(f32[16,32,384]{2,1,0:T(8,128)S(1)} %get-tuple-element.126.refs_0_.pm_ref, bf16[4,384,384]{2,1,0:T(8,128)(2,1)S(1)} %get-tuple-element.83.refs_1_, f32[16,32,384]{2,1,0:T(8,128)S(1)} %get-tuple-element.77.k_ref.refs_2_, ...), custom_call_target="tpu_custom_call" | custom-call | tf_op jit(solution)/shard_map/local_step/pallas_call | solution.py:363
  96.1 3.0 %last_step.1 = (f32[16,32,384]{2,1,0:T(8,128)}, f32[16,32,384]{2,1,0:T(8,128)}, f32[16,4,16,384]{3,2,1,0:T(8,128)S(1)}) custom-call(s32[5]{0:T(128)S(1)} %pad_add_fusion.place_ref, f32[7,32,384]{2,1,0:T(8,128)S(1)} %collective-permute-done.14.pl_ref, f32[16,32,384]{2,1,0:T(8,128)S(1)} %get-tuple-element.126.refs_0_.pm_ref, ...), custom_call_target="tpu_custom_call" | custom-call | tf_op jit(solution)/shard_map/last_step/pallas_call | solution.py:495
  99.1 22.9 %all_to_all.17.refs_0_ = f32[16,4,16,384]{3,2,1,0:T(8,128)S(1)} all-to-all(f32[16,4,16,384]{3,2,1,0:T(8,128)S(1)} %get-tuple-element.134), channel_id=1, replica_groups=mesh['shot'=16,'sub'=8] {'shot'}, dimensions={0} | all-to-all | bytes 3145728 | tf_op jit(solution)/shard_map/all_to_all | solution.py:582
  (35 shorter events, 14.8 us)
Async XLA Ops:
  3.6 26.4 %collective-permute-start = (f32[11,32,384]{2,1,0:T(8,128)S(1)}, f32[11,32,384]{2,1,0:T(8,128)S(1)}, u32[]{:S(2)}, u32[]{:S(2)}) collective-permute-start(f32[11,32,384]{2,1,0:T(8,128)S(1)} %get-tuple-element.72), channel_id=1, source_target_pairs={{0,1},{1,2},{2,3},{3,4},{4,5},{5,6},{6,7},{7,0},{8,9},{9,10},{10,1... | collective-permute-start | bytes 1622024 | tf_op jit(solution)/shard_map/ppermute | solution.py:532
  3.6 26.3 %collective-permute-start.1 = (f32[10,32,384]{2,1,0:T(8,128)S(1)}, f32[10,32,384]{2,1,0:T(8,128)S(1)}, u32[]{:S(2)}, u32[]{:S(2)}) collective-permute-start(f32[10,32,384]{2,1,0:T(8,128)S(1)} %get-tuple-element.75), channel_id=1, source_target_pairs={{1,0},{2,1},{3,2},{4,3},{5,4},{6,5},{7,6},{0,7},{9,8},{10,9},{11,1... | collective-permute-start | bytes 1474568 | tf_op jit(solution)/shard_map/ppermute | solution.py:533
  6.5 19.2 %all-to-all-start = ((f32[128,1,128]{2,1,0:T(1,128)}), f32[128,1,128]{2,1,0:T(1,128)S(1)}, u32[]{:S(2)}, u32[]{:S(2)}) async-start(f32[128,1,128]{2,1,0:T(1,128)} %bitcast.4), calls=%async_computation | async-start | bytes 131072 | tf_op jit(solution)/shard_map/all_to_all | solution.py:560
  16.5 5.7 %copy-start.1 = (s32[1,3]{1,0:T(1,128)S(1)}, s32[1,3]{1,0:T(1,128)}, u32[]{:S(2)}) copy-start(s32[1,3]{1,0:T(1,128)} %param.22) | copy-start | bytes 40
  21.3 0.9 copy-start
  31.4 7.9 %collective-permute-start.2 = (f32[7,32,384]{2,1,0:T(8,128)S(1)}, f32[7,32,384]{2,1,0:T(8,128)S(1)}, u32[]{:S(2)}, u32[]{:S(2)}) collective-permute-start(f32[7,32,384]{2,1,0:T(8,128)S(1)} %get-tuple-element.80), channel_id=1, source_target_pairs={{0,1},{1,2},{2,3},{3,4},{4,5},{5,6},{6,7},{7,0},{8,9},{9,10},{10,1... | collective-permute-start | bytes 1032200 | tf_op jit(solution)/shard_map/ppermute | solution.py:532
  31.5 7.9 %collective-permute-start.3 = (f32[7,32,384]{2,1,0:T(8,128)S(1)}, f32[7,32,384]{2,1,0:T(8,128)S(1)}, u32[]{:S(2)}, u32[]{:S(2)}) collective-permute-start(f32[7,32,384]{2,1,0:T(8,128)S(1)} %get-tuple-element.82), channel_id=1, source_target_pairs={{1,0},{2,1},{3,2},{4,3},{5,4},{6,5},{7,6},{0,7},{9,8},{10,9},{11,1... | collective-permute-start | bytes 1032200 | tf_op jit(solution)/shard_map/ppermute | solution.py:533
  40.8 7.9 %collective-permute-start.4 = (f32[7,32,384]{2,1,0:T(8,128)S(1)}, f32[7,32,384]{2,1,0:T(8,128)S(1)}, u32[]{:S(2)}, u32[]{:S(2)}) collective-permute-start(f32[7,32,384]{2,1,0:T(8,128)S(1)} %get-tuple-element.90), channel_id=1, source_target_pairs={{0,1},{1,2},{2,3},{3,4},{4,5},{5,6},{6,7},{7,0},{8,9},{9,10},{10,1... | collective-permute-start | bytes 1032200 | tf_op jit(solution)/shard_map/ppermute | solution.py:532
  40.8 7.9 %collective-permute-start.5 = (f32[7,32,384]{2,1,0:T(8,128)S(1)}, f32[7,32,384]{2,1,0:T(8,128)S(1)}, u32[]{:S(2)}, u32[]{:S(2)}) collective-permute-start(f32[7,32,384]{2,1,0:T(8,128)S(1)} %get-tuple-element.92), channel_id=1, source_target_pairs={{1,0},{2,1},{3,2},{4,3},{5,4},{6,5},{7,6},{0,7},{9,8},{10,9},{11,1... | collective-permute-start | bytes 1032200 | tf_op jit(solution)/shard_map/ppermute | solution.py:533
  50.4 7.9 %collective-permute-start.6 = (f32[7,32,384]{2,1,0:T(8,128)S(1)}, f32[7,32,384]{2,1,0:T(8,128)S(1)}, u32[]{:S(2)}, u32[]{:S(2)}) collective-permute-start(f32[7,32,384]{2,1,0:T(8,128)S(1)} %get-tuple-element.97), channel_id=1, source_target_pairs={{0,1},{1,2},{2,3},{3,4},{4,5},{5,6},{6,7},{7,0},{8,9},{9,10},{10,1... | collective-permute-start | bytes 1032200 | tf_op jit(solution)/shard_map/ppermute | solution.py:532
  50.4 7.9 %collective-permute-start.7 = (f32[7,32,384]{2,1,0:T(8,128)S(1)}, f32[7,32,384]{2,1,0:T(8,128)S(1)}, u32[]{:S(2)}, u32[]{:S(2)}) collective-permute-start(f32[7,32,384]{2,1,0:T(8,128)S(1)} %get-tuple-element.99), channel_id=1, source_target_pairs={{1,0},{2,1},{3,2},{4,3},{5,4},{6,5},{7,6},{0,7},{9,8},{10,9},{11,1... | collective-permute-start | bytes 1032200 | tf_op jit(solution)/shard_map/ppermute | solution.py:533
  59.8 7.9 %collective-permute-start.8 = (f32[7,32,384]{2,1,0:T(8,128)S(1)}, f32[7,32,384]{2,1,0:T(8,128)S(1)}, u32[]{:S(2)}, u32[]{:S(2)}) collective-permute-start(f32[7,32,384]{2,1,0:T(8,128)S(1)} %get-tuple-element.104), channel_id=1, source_target_pairs={{0,1},{1,2},{2,3},{3,4},{4,5},{5,6},{6,7},{7,0},{8,9},{9,10},{10,1... | collective-permute-start | bytes 1032200 | tf_op jit(solution)/shard_map/ppermute | solution.py:532
  59.8 7.9 %collective-permute-start.9 = (f32[7,32,384]{2,1,0:T(8,128)S(1)}, f32[7,32,384]{2,1,0:T(8,128)S(1)}, u32[]{:S(2)}, u32[]{:S(2)}) collective-permute-start(f32[7,32,384]{2,1,0:T(8,128)S(1)} %get-tuple-element.106), channel_id=1, source_target_pairs={{1,0},{2,1},{3,2},{4,3},{5,4},{6,5},{7,6},{0,7},{9,8},{10,9},{11,1... | collective-permute-start | bytes 1032200 | tf_op jit(solution)/shard_map/ppermute | solution.py:533
  69.2 7.9 %collective-permute-start.10 = (f32[7,32,384]{2,1,0:T(8,128)S(1)}, f32[7,32,384]{2,1,0:T(8,128)S(1)}, u32[]{:S(2)}, u32[]{:S(2)}) collective-permute-start(f32[7,32,384]{2,1,0:T(8,128)S(1)} %get-tuple-element.111), channel_id=1, source_target_pairs={{0,1},{1,2},{2,3},{3,4},{4,5},{5,6},{6,7},{7,0},{8,9},{9,10},{10,1... | collective-permute-start | bytes 1032200 | tf_op jit(solution)/shard_map/ppermute | solution.py:532
  69.2 7.9 %collective-permute-start.11 = (f32[7,32,384]{2,1,0:T(8,128)S(1)}, f32[7,32,384]{2,1,0:T(8,128)S(1)}, u32[]{:S(2)}, u32[]{:S(2)}) collective-permute-start(f32[7,32,384]{2,1,0:T(8,128)S(1)} %get-tuple-element.113), channel_id=1, source_target_pairs={{1,0},{2,1},{3,2},{4,3},{5,4},{6,5},{7,6},{0,7},{9,8},{10,9},{11,1... | collective-permute-start | bytes 1032200 | tf_op jit(solution)/shard_map/ppermute | solution.py:533
  78.6 7.9 %collective-permute-start.12 = (f32[7,32,384]{2,1,0:T(8,128)S(1)}, f32[7,32,384]{2,1,0:T(8,128)S(1)}, u32[]{:S(2)}, u32[]{:S(2)}) collective-permute-start(f32[7,32,384]{2,1,0:T(8,128)S(1)} %get-tuple-element.118), channel_id=1, source_target_pairs={{0,1},{1,2},{2,3},{3,4},{4,5},{5,6},{6,7},{7,0},{8,9},{9,10},{10,1... | collective-permute-start | bytes 1032200 | tf_op jit(solution)/shard_map/ppermute | solution.py:532
  78.6 7.9 %collective-permute-start.13 = (f32[7,32,384]{2,1,0:T(8,128)S(1)}, f32[7,32,384]{2,1,0:T(8,128)S(1)}, u32[]{:S(2)}, u32[]{:S(2)}) collective-permute-start(f32[7,32,384]{2,1,0:T(8,128)S(1)} %get-tuple-element.120), channel_id=1, source_target_pairs={{1,0},{2,1},{3,2},{4,3},{5,4},{6,5},{7,6},{0,7},{9,8},{10,9},{11,1... | collective-permute-start | bytes 1032200 | tf_op jit(solution)/shard_map/ppermute | solution.py:533
  88.2 7.9 %collective-permute-start.14 = (f32[7,32,384]{2,1,0:T(8,128)S(1)}, f32[7,32,384]{2,1,0:T(8,128)S(1)}, u32[]{:S(2)}, u32[]{:S(2)}) collective-permute-start(f32[7,32,384]{2,1,0:T(8,128)S(1)} %get-tuple-element.125), channel_id=1, source_target_pairs={{0,1},{1,2},{2,3},{3,4},{4,5},{5,6},{6,7},{7,0},{8,9},{9,10},{10,1... | collective-permute-start | bytes 1032200 | tf_op jit(solution)/shard_map/ppermute | solution.py:532
  88.2 7.9 %collective-permute-start.15 = (f32[7,32,384]{2,1,0:T(8,128)S(1)}, f32[7,32,384]{2,1,0:T(8,128)S(1)}, u32[]{:S(2)}, u32[]{:S(2)}) collective-permute-start(f32[7,32,384]{2,1,0:T(8,128)S(1)} %get-tuple-element.127), channel_id=1, source_target_pairs={{1,0},{2,1},{3,2},{4,3},{5,4},{6,5},{7,6},{0,7},{9,8},{10,9},{11,1... | collective-permute-start | bytes 1032200 | tf_op jit(solution)/shard_map/ppermute | solution.py:533

commit v5 on v4

--- a/solution.py
+++ b/solution.py
@@ -202,7 +202,8 @@
 
 
 def local_change(
-    p_ref, k_ref, b2_ref, b3_ref, bands_ref, got_ref, turned, moment, out_ref, scratch, and_then=None
+    p_ref, k_ref, b2_ref, b3_ref, bands_ref, got_ref, turned, moment, out_ref, scratch, and_then=None,
+    loads=(),
 ):
     ps_ref, qs_ref, third_ref, *more = scratch
     nx, ny, nz = p_ref.shape
@@ -211,8 +212,12 @@
         spread_ref, added_ref = more
         fill_columns(got_ref, spread_ref, moment, nz)
         added_ref[...] = inject_rows(turned, spread_ref, 0, nx * ny).reshape(nx, ny, nz)
+    for load in loads[:1]:
+        load.wait()
     third_ref[...] = along_third(p_ref, b3_ref, bands_ref).reshape(nx, ny, nz)
     count = nz // 128
+    for load in loads[1:]:
+        load.wait()
 
     def planes(group, carry):
         for index in range(GROUP):
@@ -335,6 +340,14 @@
             image_ref, refs = refs[0], refs[1:]
             light_ref, refs = refs[0], refs[1:]
         got_ref, turned_ref, out_ref, image_out_ref, light_out_ref, *scratch = refs
+        loads = ()
+        if moment == 1:
+            far = (b3_ref, b2_ref, f_ref)
+            b3_ref, b2_ref, f_ref, *scratch, sems = scratch
+            near = (b3_ref, b2_ref, f_ref)
+            loads = [pltpu.make_async_copy(f, n, sems.at[i]) for i, (f, n) in enumerate(zip(far, near))]
+            for load in loads:
+                load.start()
 
         def accumulate(x):
             frame = f_ref[moment - 1, x].astype(F32)
@@ -351,7 +364,7 @@
 
         local_change(
             p_ref, k_ref, b2_ref, b3_ref, bands_ref, got_ref, turned_ref[...], moment, out_ref,
-            scratch, accumulate,
+            scratch, accumulate, loads,
         )
 
     return local_kernel
@@ -359,13 +372,19 @@
 
 def local_step(moment, current, bands, stiffness, b2, b3, frames, change, sums, got, turned):
     nx, ny, nz = current.shape
-    images = list(sums) if moment > 1 else []
+    vmem = pl.BlockSpec(memory_space=pltpu.VMEM)
+    images, wide, moved, sems = list(sums), [vmem] * 3, [], []
+    if moment == 1:
+        images, wide = [], [pl.BlockSpec(memory_space=pltpu.HBM)] * 3
+        moved = [shape_of(*a.shape, dtype=a.dtype) for a in (b3, b2, frames)]
+        sems = [pltpu.SemaphoreType.DMA((3,))]
+        b2, b3, frames = far_away(b2, b3, frames)
     return pl.pallas_call(
         make_local_kernel(moment),
-        in_specs=[pl.BlockSpec(memory_space=pltpu.VMEM)] * (9 + len(images)),
-        out_specs=[pl.BlockSpec(memory_space=pltpu.VMEM)] * 3,
-        out_shape=[shape_of(nx, ny, nz)] * 3,
-        scratch_shapes=local_scratch(nx, ny, nz),
+        in_specs=[vmem] * 3 + wide + [vmem] * (3 + len(images)),
+        out_specs=[vmem] * (3 + len(moved)),
+        out_shape=[shape_of(nx, ny, nz)] * 3 + moved,
+        scratch_shapes=local_scratch(nx, ny, nz) + sems,
         compiler_params=PARAMS,
         name="local_step",
     )(current, bands, stiffness, b2, b3, frames, change, *images, got, turned)
@@ -562,9 +581,10 @@
     b1_halos = halos
     nearby = first_local(current, stiffness, b2, b3)
     got, place = lax.optimization_barrier((got, place))
-    nearby, turned, bands, current, stiffness, b2, b3, b1, before, frames = first_inject(
-        got, nearby, current, stiffness, b2, b3, b1, before, forward
-    )
+    nearby, turned, bands, current, stiffness, b1, before = first_inject(
+        got, nearby, current, stiffness, b1, before
+    )
+    frames = forward
 
     image = light = None
     for moment in range(steps - 1):
@@ -573,9 +593,11 @@
         )
         halos = exchange(head, tail)
         before, current = current, following
-        nearby, image, light = local_step(
+        nearby, image, light, *moved = local_step(
             moment + 1, current, bands, stiffness, b2, b3, frames, change, (image, light), got, turned
         )
+        if moved:
+            b3, b2, frames = moved
     now, following, sums = last_step(
         place, halos, current, b1_halos, b1, stiffness, nearby, before, image, frames, light
     )

time: 124 us -> 123 us (level)
  Pallas kernels: 55.1 us -> 53.7 us
    pallas_call x1, Pallas kernels: 4.2 us -> 2.68 us  [first_inject(): pl.pallas_call(first_inject_kernel, in_specs=[vmem] + [far] * (1 + len(ar...]
  transfers between devices with their start and end apart: 17 -> 17, of which waited for: 8 -> 8; matrix products, arithmetic and copies ran while one was open for 0% -> 0% of each run, Pallas kernels for 31% -> 30%
where the time goes in v5:
time: 123 us; the launch traced here: 121 us
  Pallas kernels  53.7 us (44%)
  starting transfers between devices  33.9 us (28%)
  blocking collectives  22.8 us (19%)
  waiting for transfers between devices  8.91 us (7%)
    pallas_call x7, Pallas kernels, local_step(): pl.pallas_call(make_local_kernel(moment), in_specs=[vmem] * 3 + wide + [v...  28.9 us
    ppermute x8, starting transfers between devices, exchange(): lax.ppermute(head, 'sub', [((i + 1) % count, i) for i in range(count)])  23.8 us
    all_to_all x1, blocking collectives, local(): sums = lax.all_to_all(sums, 'shot', split_axis=0, concat_axis=0, tiled=True)  22.8 us
    pallas_call x7, Pallas kernels, update_step(): pl.pallas_call(update_kernel, in_specs=[pl.BlockSpec(memory_space=pltpu.S...  10.7 us
    all_to_all x1, starting transfers between devices, local(): got = lax.all_to_all(send, both, split_axis=0, concat_axis=0, tiled=True)  9.94 us
    ppermute x8, waiting for transfers between devices, exchange(): lax.ppermute(tail, 'sub', [(i, (i + 1) % count) for i in range(count)])  5.44 us
    pallas_call x1, Pallas kernels, first_local(): pl.pallas_call(first_local_kernel, in_specs=[far] * 4, out_specs=far, out...  4.81 us
    all_to_all x1, waiting for transfers between devices, local(): got = lax.all_to_all(send, both, split_axis=0, concat_axis=0, tiled=True)  3.44 us
  transfers between devices with their start and end apart: 17, of which 8 were waited for; matrix products, arithmetic and copies ran while one was open for 0% of the time, Pallas kernels for 30%

profile of v5, /device:TPU:0, one launch (start us, length us, event | category | flops | bytes accessed | tf_op | source)
XLA Modules:
  0.0 121.1 jit_solution(15222918913218056201)
XLA Ops:
  0.6 2.9 %prep.1 = (f32[128,128]{1,0:T(8,128)}, f32[11,32,384]{2,1,0:T(8,128)S(1)}, f32[10,32,384]{2,1,0:T(8,128)S(1)}) custom-call(f32[512,256]{1,0:T(8,128)} %refs_0_.1, f32[128,256]{1,0:T(8,128)} %constant.10.clone.refs_1_, s32[1,512]{1,0:T(1,128)} %bitcast.26, s32[1,512]{1,0:T(1,128)} %bitcast.27, f32[16,32,384]{2,1,0:T(8,128)} %bitcast.21, f32[16,32,384]{2,1,0:T(8,128)} %refs_2_.1), custom_call_target="tpu_custom_call" | custom-call | tf_op jit(solution)/shard_map/prep/pallas_call | solution.py:105
  3.6 2.9 %collective-permute-start.1 = (f32[10,32,384]{2,1,0:T(8,128)S(1)}, f32[10,32,384]{2,1,0:T(8,128)S(1)}, u32[]{:S(2)}, u32[]{:S(2)}) collective-permute-start(f32[10,32,384]{2,1,0:T(8,128)S(1)} %get-tuple-element.75), channel_id=1, source_target_pairs={{1,0},{2,1},{3,2},{4,3},{5,4},{6,5},{7,6},{0,7},{9,8},{10,9},{11,1... | collective-permute-start | bytes 1474568 | tf_op jit(solution)/shard_map/ppermute | solution.py:552
  6.5 9.9 %all-to-all-start = ((f32[128,1,128]{2,1,0:T(1,128)}), f32[128,1,128]{2,1,0:T(1,128)S(1)}, u32[]{:S(2)}, u32[]{:S(2)}) async-start(f32[128,1,128]{2,1,0:T(1,128)} %bitcast.4), calls=%async_computation | async-start | bytes 131072 | tf_op jit(solution)/shard_map/all_to_all | solution.py:579
  16.5 4.8 %first_local.1.local_far = f32[16,32,384]{2,1,0:T(8,128)S(1)} custom-call(f32[16,32,384]{2,1,0:T(8,128)} %bitcast.22, f32[16,32,384]{2,1,0:T(8,128)} %refs_1_.2, f32[16,32,384]{2,1,0:T(8,128)} %refs_3_.1, f32[16,32,384]{2,1,0:T(8,128)} %refs_4_.1), custom_call_target="tpu_custom_call" | custom-call | tf_op jit(solution)/shard_map/first_local/pallas_call | solution.py:282
  22.3 3.4 %all-to-all-done = f32[128,1,128]{2,1,0:T(1,128)S(1)} async-done(((f32[128,1,128]{2,1,0:T(1,128)}), f32[128,1,128]{2,1,0:T(1,128)S(1)}, u32[]{:S(2)}, u32[]{:S(2)}) %all-to-all-start) | async-done | bytes 65568 | tf_op jit(solution)/shard_map/all_to_all | solution.py:579
  25.7 2.7 %first_inject.1 = (f32[16,32,384]{2,1,0:T(8,128)S(1)}, f32[128,128]{1,0:T(8,128)S(1)}, bf16[4,384,384]{2,1,0:T(8,128)(2,1)S(1)}, f32[16,32,384]{2,1,0:T(8,128)S(...) custom-call(f32[128,128]{1,0:T(8,128)S(1)} %bitcast.13, ...), custom_call_target="tpu_custom_call" | custom-call | tf_op jit(solution)/shard_map/first_inject/pallas_call | solution.py:319
  29.9 2.9 %collective-permute-start.3 = (f32[7,32,384]{2,1,0:T(8,128)S(1)}, f32[7,32,384]{2,1,0:T(8,128)S(1)}, u32[]{:S(2)}, u32[]{:S(2)}) collective-permute-start(f32[7,32,384]{2,1,0:T(8,128)S(1)} %get-tuple-element.82), channel_id=1, source_target_pairs={{1,0},{2,1},{3,2},{4,3},{5,4},{6,5},{7,6},{0,7},{9,8},{10,9},{11,1... | collective-permute-start | bytes 1032200 | tf_op jit(solution)/shard_map/ppermute | solution.py:552
  32.9 4.2 %local_step.7 = (f32[16,32,384]{2,1,0:T(8,128)S(1)}, f32[16,32,384]{2,1,0:T(8,128)S(1)}, f32[16,32,384]{2,1,0:T(8,128)S(1)}, f32[16,32,384]{2,1,0:T(8,128)S(1)},...) custom-call(f32[16,32,384]{2,1,0:T(8,128)S(1)} %get-tuple-element.81.refs_0_.pm_ref.before_ref, ...), custom_call_target="tpu_custom_call" | custom-call | tf_op jit(solution)/shard_map/local_step/pallas_call | solution.py:382
  39.3 3.0 %collective-permute-start.5 = (f32[7,32,384]{2,1,0:T(8,128)S(1)}, f32[7,32,384]{2,1,0:T(8,128)S(1)}, u32[]{:S(2)}, u32[]{:S(2)}) collective-permute-start(f32[7,32,384]{2,1,0:T(8,128)S(1)} %get-tuple-element.89), channel_id=1, source_target_pairs={{1,0},{2,1},{3,2},{4,3},{5,4},{6,5},{7,6},{0,7},{9,8},{10,9},{11,1... | collective-permute-start | bytes 1032200 | tf_op jit(solution)/shard_map/ppermute | solution.py:552
  42.3 4.1 %local_step.8 = (f32[16,32,384]{2,1,0:T(8,128)S(1)}, f32[16,32,384]{2,1,0:T(8,128)S(1)}, f32[16,32,384]{2,1,0:T(8,128)S(1)}) custom-call(f32[16,32,384]{2,1,0:T(8,128)S(1)} %get-tuple-element.88.refs_0_.pm_ref.before_ref, bf16[4,384,384]{2,1,0:T(8,128)(2,1)S(1)} %get-tuple-element.83.refs_1_, f32[16,32,384]{2,1,0:T(8,128)S(1)} %get-tuple-element.77.k_ref.refs_2_, ...), custom_call_target="tpu_custom_call" | custom-call | tf_op jit(solution)/shard_map/local_step/pallas_call | solution.py:382
  47.2 1.7 %update_step.9 = (f32[16,32,384]{2,1,0:T(8,128)S(1)}, f32[16,32,384]{2,1,0:T(8,128)S(1)}, f32[7,32,384]{2,1,0:T(8,128)S(1)}, f32[7,32,384]{2,1,0:T(8,128)S(1)}) custom-call(s32[5]{0:T(128)S(1)} %pad_add_fusion.place_ref, f32[7,32,384]{2,1,0:T(8,128)S(1)} %collective-permute-done.4.pl_ref, f32[16,32,384]{2,1,0:T(8,128)S(1)} %get-tuple-element.88.refs_0_.pm_ref.before_ref, ...), custom_call_target="tpu_custom_call" | custom-call | tf_op jit(solution)/shard_map/update_step/pallas_call | solution.py:500
  48.9 3.0 %collective-permute-start.7 = (f32[7,32,384]{2,1,0:T(8,128)S(1)}, f32[7,32,384]{2,1,0:T(8,128)S(1)}, u32[]{:S(2)}, u32[]{:S(2)}) collective-permute-start(f32[7,32,384]{2,1,0:T(8,128)S(1)} %get-tuple-element.99), channel_id=1, source_target_pairs={{1,0},{2,1},{3,2},{4,3},{5,4},{6,5},{7,6},{0,7},{9,8},{10,9},{11,1... | collective-permute-start | bytes 1032200 | tf_op jit(solution)/shard_map/ppermute | solution.py:552
  51.9 4.1 %local_step.9 = (f32[16,32,384]{2,1,0:T(8,128)S(1)}, f32[16,32,384]{2,1,0:T(8,128)S(1)}, f32[16,32,384]{2,1,0:T(8,128)S(1)}) custom-call(f32[16,32,384]{2,1,0:T(8,128)S(1)} %get-tuple-element.98.refs_0_.pm_ref.before_ref, bf16[4,384,384]{2,1,0:T(8,128)(2,1)S(1)} %get-tuple-element.83.refs_1_, f32[16,32,384]{2,1,0:T(8,128)S(1)} %get-tuple-element.77.k_ref.refs_2_, ...), custom_call_target="tpu_custom_call" | custom-call | tf_op jit(solution)/shard_map/local_step/pallas_call | solution.py:382
  58.3 3.0 %collective-permute-start.9 = (f32[7,32,384]{2,1,0:T(8,128)S(1)}, f32[7,32,384]{2,1,0:T(8,128)S(1)}, u32[]{:S(2)}, u32[]{:S(2)}) collective-permute-start(f32[7,32,384]{2,1,0:T(8,128)S(1)} %get-tuple-element.106), channel_id=1, source_target_pairs={{1,0},{2,1},{3,2},{4,3},{5,4},{6,5},{7,6},{0,7},{9,8},{10,9},{11,1... | collective-permute-start | bytes 1032200 | tf_op jit(solution)/shard_map/ppermute | solution.py:552
  61.3 4.1 %local_step.10 = (f32[16,32,384]{2,1,0:T(8,128)S(1)}, f32[16,32,384]{2,1,0:T(8,128)S(1)}, f32[16,32,384]{2,1,0:T(8,128)S(1)}) custom-call(f32[16,32,384]{2,1,0:T(8,128)S(1)} %get-tuple-element.105.refs_0_.pm_ref.before_ref, bf16[4,384,384]{2,1,0:T(8,128)(2,1)S(1)} %get-tuple-element.83.refs_1_, f32[16,32,384]{2,1,0:T(8,128)S(1)} %get-tuple-element.77.k_ref.refs_2_, ...), custom_call_target="tpu_custom_call" | custom-call | tf_op jit(solution)/shard_map/local_step/pallas_call | solution.py:382
  67.7 3.0 %collective-permute-start.11 = (f32[7,32,384]{2,1,0:T(8,128)S(1)}, f32[7,32,384]{2,1,0:T(8,128)S(1)}, u32[]{:S(2)}, u32[]{:S(2)}) collective-permute-start(f32[7,32,384]{2,1,0:T(8,128)S(1)} %get-tuple-element.113), channel_id=1, source_target_pairs={{1,0},{2,1},{3,2},{4,3},{5,4},{6,5},{7,6},{0,7},{9,8},{10,9},{11,1... | collective-permute-start | bytes 1032200 | tf_op jit(solution)/shard_map/ppermute | solution.py:552
  70.7 4.1 %local_step.11 = (f32[16,32,384]{2,1,0:T(8,128)S(1)}, f32[16,32,384]{2,1,0:T(8,128)S(1)}, f32[16,32,384]{2,1,0:T(8,128)S(1)}) custom-call(f32[16,32,384]{2,1,0:T(8,128)S(1)} %get-tuple-element.112.refs_0_.pm_ref.before_ref, bf16[4,384,384]{2,1,0:T(8,128)(2,1)S(1)} %get-tuple-element.83.refs_1_, f32[16,32,384]{2,1,0:T(8,128)S(1)} %get-tuple-element.77.k_ref.refs_2_, ...), custom_call_target="tpu_custom_call" | custom-call | tf_op jit(solution)/shard_map/local_step/pallas_call | solution.py:382
  77.1 3.0 %collective-permute-start.13 = (f32[7,32,384]{2,1,0:T(8,128)S(1)}, f32[7,32,384]{2,1,0:T(8,128)S(1)}, u32[]{:S(2)}, u32[]{:S(2)}) collective-permute-start(f32[7,32,384]{2,1,0:T(8,128)S(1)} %get-tuple-element.120), channel_id=1, source_target_pairs={{1,0},{2,1},{3,2},{4,3},{5,4},{6,5},{7,6},{0,7},{9,8},{10,9},{11,1... | collective-permute-start | bytes 1032200 | tf_op jit(solution)/shard_map/ppermute | solution.py:552
  80.1 4.1 %local_step.12 = (f32[16,32,384]{2,1,0:T(8,128)S(1)}, f32[16,32,384]{2,1,0:T(8,128)S(1)}, f32[16,32,384]{2,1,0:T(8,128)S(1)}) custom-call(f32[16,32,384]{2,1,0:T(8,128)S(1)} %get-tuple-element.119.refs_0_.pm_ref.before_ref, bf16[4,384,384]{2,1,0:T(8,128)(2,1)S(1)} %get-tuple-element.83.refs_1_, f32[16,32,384]{2,1,0:T(8,128)S(1)} %get-tuple-element.77.k_ref.refs_2_, ...), custom_call_target="tpu_custom_call" | custom-call | tf_op jit(solution)/shard_map/local_step/pallas_call | solution.py:382
  85.0 1.7 %update_step.13 = (f32[16,32,384]{2,1,0:T(8,128)S(1)}, f32[16,32,384]{2,1,0:T(8,128)S(1)}, f32[7,32,384]{2,1,0:T(8,128)S(1)}, f32[7,32,384]{2,1,0:T(8,128)S(1)}) custom-call(s32[5]{0:T(128)S(1)} %pad_add_fusion.place_ref, f32[7,32,384]{2,1,0:T(8,128)S(1)} %collective-permute-done.12.pl_ref, f32[16,32,384]{2,1,0:T(8,128)S(1)} %get-tuple-element.119.refs_0_.pm_ref.before_ref, ...), custom_call_target="tpu_custom_call" | custom-call | tf_op jit(solution)/shard_map/update_step/pallas_call | solution.py:500
  86.7 3.0 %collective-permute-start.15 = (f32[7,32,384]{2,1,0:T(8,128)S(1)}, f32[7,32,384]{2,1,0:T(8,128)S(1)}, u32[]{:S(2)}, u32[]{:S(2)}) collective-permute-start(f32[7,32,384]{2,1,0:T(8,128)S(1)} %get-tuple-element.127), channel_id=1, source_target_pairs={{1,0},{2,1},{3,2},{4,3},{5,4},{6,5},{7,6},{0,7},{9,8},{10,9},{11,1... | collective-permute-start | bytes 1032200 | tf_op jit(solution)/shard_map/ppermute | solution.py:552
  89.7 4.1 %local_step.13 = (f32[16,32,384]{2,1,0:T(8,128)S(1)}, f32[16,32,384]{2,1,0:T(8,128)S(1)}, f32[16,32,384]{2,1,0:T(8,128)S(1)}) custom-call(f32[16,32,384]{2,1,0:T(8,128)S(1)} %get-tuple-element.126.refs_0_.pm_ref, bf16[4,384,384]{2,1,0:T(8,128)(2,1)S(1)} %get-tuple-element.83.refs_1_, f32[16,32,384]{2,1,0:T(8,128)S(1)} %get-tuple-element.77.k_ref.refs_2_, ...), custom_call_target="tpu_custom_call" | custom-call | tf_op jit(solution)/shard_map/local_step/pallas_call | solution.py:382
  94.6 3.0 %last_step.1 = (f32[16,32,384]{2,1,0:T(8,128)}, f32[16,32,384]{2,1,0:T(8,128)}, f32[16,4,16,384]{3,2,1,0:T(8,128)S(1)}) custom-call(s32[5]{0:T(128)S(1)} %pad_add_fusion.place_ref, f32[7,32,384]{2,1,0:T(8,128)S(1)} %collective-permute-done.14.pl_ref, f32[16,32,384]{2,1,0:T(8,128)S(1)} %get-tuple-element.126.refs_0_.pm_ref, ...), custom_call_target="tpu_custom_call" | custom-call | tf_op jit(solution)/shard_map/last_step/pallas_call | solution.py:514
  97.6 22.8 %all_to_all.17.refs_0_ = f32[16,4,16,384]{3,2,1,0:T(8,128)S(1)} all-to-all(f32[16,4,16,384]{3,2,1,0:T(8,128)S(1)} %get-tuple-element.134), channel_id=1, replica_groups=mesh['shot'=16,'sub'=8] {'shot'}, dimensions={0} | all-to-all | bytes 3145728 | tf_op jit(solution)/shard_map/all_to_all | solution.py:604
  (35 shorter events, 14.6 us)
Async XLA Ops:
  3.6 24.9 %collective-permute-start = (f32[11,32,384]{2,1,0:T(8,128)S(1)}, f32[11,32,384]{2,1,0:T(8,128)S(1)}, u32[]{:S(2)}, u32[]{:S(2)}) collective-permute-start(f32[11,32,384]{2,1,0:T(8,128)S(1)} %get-tuple-element.72), channel_id=1, source_target_pairs={{0,1},{1,2},{2,3},{3,4},{4,5},{5,6},{6,7},{7,0},{8,9},{9,10},{10,1... | collective-permute-start | bytes 1622024 | tf_op jit(solution)/shard_map/ppermute | solution.py:551
  3.6 24.8 %collective-permute-start.1 = (f32[10,32,384]{2,1,0:T(8,128)S(1)}, f32[10,32,384]{2,1,0:T(8,128)S(1)}, u32[]{:S(2)}, u32[]{:S(2)}) collective-permute-start(f32[10,32,384]{2,1,0:T(8,128)S(1)} %get-tuple-element.75), channel_id=1, source_target_pairs={{1,0},{2,1},{3,2},{4,3},{5,4},{6,5},{7,6},{0,7},{9,8},{10,9},{11,1... | collective-permute-start | bytes 1474568 | tf_op jit(solution)/shard_map/ppermute | solution.py:552
  6.5 19.2 %all-to-all-start = ((f32[128,1,128]{2,1,0:T(1,128)}), f32[128,1,128]{2,1,0:T(1,128)S(1)}, u32[]{:S(2)}, u32[]{:S(2)}) async-start(f32[128,1,128]{2,1,0:T(1,128)} %bitcast.4), calls=%async_computation | async-start | bytes 131072 | tf_op jit(solution)/shard_map/all_to_all | solution.py:579
  16.5 5.7 %copy-start.1 = (s32[1,3]{1,0:T(1,128)S(1)}, s32[1,3]{1,0:T(1,128)}, u32[]{:S(2)}) copy-start(s32[1,3]{1,0:T(1,128)} %param.22) | copy-start | bytes 40
  21.3 0.9 copy-start
  29.9 7.9 %collective-permute-start.2 = (f32[7,32,384]{2,1,0:T(8,128)S(1)}, f32[7,32,384]{2,1,0:T(8,128)S(1)}, u32[]{:S(2)}, u32[]{:S(2)}) collective-permute-start(f32[7,32,384]{2,1,0:T(8,128)S(1)} %get-tuple-element.80), channel_id=1, source_target_pairs={{0,1},{1,2},{2,3},{3,4},{4,5},{5,6},{6,7},{7,0},{8,9},{9,10},{10,1... | collective-permute-start | bytes 1032200 | tf_op jit(solution)/shard_map/ppermute | solution.py:551
  29.9 7.9 %collective-permute-start.3 = (f32[7,32,384]{2,1,0:T(8,128)S(1)}, f32[7,32,384]{2,1,0:T(8,128)S(1)}, u32[]{:S(2)}, u32[]{:S(2)}) collective-permute-start(f32[7,32,384]{2,1,0:T(8,128)S(1)} %get-tuple-element.82), channel_id=1, source_target_pairs={{1,0},{2,1},{3,2},{4,3},{5,4},{6,5},{7,6},{0,7},{9,8},{10,9},{11,1... | collective-permute-start | bytes 1032200 | tf_op jit(solution)/shard_map/ppermute | solution.py:552
  39.3 7.9 %collective-permute-start.4 = (f32[7,32,384]{2,1,0:T(8,128)S(1)}, f32[7,32,384]{2,1,0:T(8,128)S(1)}, u32[]{:S(2)}, u32[]{:S(2)}) collective-permute-start(f32[7,32,384]{2,1,0:T(8,128)S(1)} %get-tuple-element.87), channel_id=1, source_target_pairs={{0,1},{1,2},{2,3},{3,4},{4,5},{5,6},{6,7},{7,0},{8,9},{9,10},{10,1... | collective-permute-start | bytes 1032200 | tf_op jit(solution)/shard_map/ppermute | solution.py:551
  39.3 7.9 %collective-permute-start.5 = (f32[7,32,384]{2,1,0:T(8,128)S(1)}, f32[7,32,384]{2,1,0:T(8,128)S(1)}, u32[]{:S(2)}, u32[]{:S(2)}) collective-permute-start(f32[7,32,384]{2,1,0:T(8,128)S(1)} %get-tuple-element.89), channel_id=1, source_target_pairs={{1,0},{2,1},{3,2},{4,3},{5,4},{6,5},{7,6},{0,7},{9,8},{10,9},{11,1... | collective-permute-start | bytes 1032200 | tf_op jit(solution)/shard_map/ppermute | solution.py:552
  48.9 7.9 %collective-permute-start.6 = (f32[7,32,384]{2,1,0:T(8,128)S(1)}, f32[7,32,384]{2,1,0:T(8,128)S(1)}, u32[]{:S(2)}, u32[]{:S(2)}) collective-permute-start(f32[7,32,384]{2,1,0:T(8,128)S(1)} %get-tuple-element.97), channel_id=1, source_target_pairs={{0,1},{1,2},{2,3},{3,4},{4,5},{5,6},{6,7},{7,0},{8,9},{9,10},{10,1... | collective-permute-start | bytes 1032200 | tf_op jit(solution)/shard_map/ppermute | solution.py:551
  48.9 7.9 %collective-permute-start.7 = (f32[7,32,384]{2,1,0:T(8,128)S(1)}, f32[7,32,384]{2,1,0:T(8,128)S(1)}, u32[]{:S(2)}, u32[]{:S(2)}) collective-permute-start(f32[7,32,384]{2,1,0:T(8,128)S(1)} %get-tuple-element.99), channel_id=1, source_target_pairs={{1,0},{2,1},{3,2},{4,3},{5,4},{6,5},{7,6},{0,7},{9,8},{10,9},{11,1... | collective-permute-start | bytes 1032200 | tf_op jit(solution)/shard_map/ppermute | solution.py:552
  58.3 7.9 %collective-permute-start.8 = (f32[7,32,384]{2,1,0:T(8,128)S(1)}, f32[7,32,384]{2,1,0:T(8,128)S(1)}, u32[]{:S(2)}, u32[]{:S(2)}) collective-permute-start(f32[7,32,384]{2,1,0:T(8,128)S(1)} %get-tuple-element.104), channel_id=1, source_target_pairs={{0,1},{1,2},{2,3},{3,4},{4,5},{5,6},{6,7},{7,0},{8,9},{9,10},{10,1... | collective-permute-start | bytes 1032200 | tf_op jit(solution)/shard_map/ppermute | solution.py:551
  58.3 7.9 %collective-permute-start.9 = (f32[7,32,384]{2,1,0:T(8,128)S(1)}, f32[7,32,384]{2,1,0:T(8,128)S(1)}, u32[]{:S(2)}, u32[]{:S(2)}) collective-permute-start(f32[7,32,384]{2,1,0:T(8,128)S(1)} %get-tuple-element.106), channel_id=1, source_target_pairs={{1,0},{2,1},{3,2},{4,3},{5,4},{6,5},{7,6},{0,7},{9,8},{10,9},{11,1... | collective-permute-start | bytes 1032200 | tf_op jit(solution)/shard_map/ppermute | solution.py:552
  67.7 7.9 %collective-permute-start.10 = (f32[7,32,384]{2,1,0:T(8,128)S(1)}, f32[7,32,384]{2,1,0:T(8,128)S(1)}, u32[]{:S(2)}, u32[]{:S(2)}) collective-permute-start(f32[7,32,384]{2,1,0:T(8,128)S(1)} %get-tuple-element.111), channel_id=1, source_target_pairs={{0,1},{1,2},{2,3},{3,4},{4,5},{5,6},{6,7},{7,0},{8,9},{9,10},{10,1... | collective-permute-start | bytes 1032200 | tf_op jit(solution)/shard_map/ppermute | solution.py:551
  67.7 7.9 %collective-permute-start.11 = (f32[7,32,384]{2,1,0:T(8,128)S(1)}, f32[7,32,384]{2,1,0:T(8,128)S(1)}, u32[]{:S(2)}, u32[]{:S(2)}) collective-permute-start(f32[7,32,384]{2,1,0:T(8,128)S(1)} %get-tuple-element.113), channel_id=1, source_target_pairs={{1,0},{2,1},{3,2},{4,3},{5,4},{6,5},{7,6},{0,7},{9,8},{10,9},{11,1... | collective-permute-start | bytes 1032200 | tf_op jit(solution)/shard_map/ppermute | solution.py:552
  77.1 7.9 %collective-permute-start.12 = (f32[7,32,384]{2,1,0:T(8,128)S(1)}, f32[7,32,384]{2,1,0:T(8,128)S(1)}, u32[]{:S(2)}, u32[]{:S(2)}) collective-permute-start(f32[7,32,384]{2,1,0:T(8,128)S(1)} %get-tuple-element.118), channel_id=1, source_target_pairs={{0,1},{1,2},{2,3},{3,4},{4,5},{5,6},{6,7},{7,0},{8,9},{9,10},{10,1... | collective-permute-start | bytes 1032200 | tf_op jit(solution)/shard_map/ppermute | solution.py:551
  77.1 7.9 %collective-permute-start.13 = (f32[7,32,384]{2,1,0:T(8,128)S(1)}, f32[7,32,384]{2,1,0:T(8,128)S(1)}, u32[]{:S(2)}, u32[]{:S(2)}) collective-permute-start(f32[7,32,384]{2,1,0:T(8,128)S(1)} %get-tuple-element.120), channel_id=1, source_target_pairs={{1,0},{2,1},{3,2},{4,3},{5,4},{6,5},{7,6},{0,7},{9,8},{10,9},{11,1... | collective-permute-start | bytes 1032200 | tf_op jit(solution)/shard_map/ppermute | solution.py:552
  86.7 7.9 %collective-permute-start.14 = (f32[7,32,384]{2,1,0:T(8,128)S(1)}, f32[7,32,384]{2,1,0:T(8,128)S(1)}, u32[]{:S(2)}, u32[]{:S(2)}) collective-permute-start(f32[7,32,384]{2,1,0:T(8,128)S(1)} %get-tuple-element.125), channel_id=1, source_target_pairs={{0,1},{1,2},{2,3},{3,4},{4,5},{5,6},{6,7},{7,0},{8,9},{9,10},{10,1... | collective-permute-start | bytes 1032200 | tf_op jit(solution)/shard_map/ppermute | solution.py:551
  86.7 7.9 %collective-permute-start.15 = (f32[7,32,384]{2,1,0:T(8,128)S(1)}, f32[7,32,384]{2,1,0:T(8,128)S(1)}, u32[]{:S(2)}, u32[]{:S(2)}) collective-permute-start(f32[7,32,384]{2,1,0:T(8,128)S(1)} %get-tuple-element.127), channel_id=1, source_target_pairs={{1,0},{2,1},{3,2},{4,3},{5,4},{6,5},{7,6},{0,7},{9,8},{10,9},{11,1... | collective-permute-start | bytes 1032200 | tf_op jit(solution)/shard_map/ppermute | solution.py:552

commit v6 on v5

--- a/solution.py
+++ b/solution.py
@@ -463,11 +463,16 @@
 
 def last_kernel(
     place_ref, pl_ref, pm_ref, pr_ref, bl_ref, bm_ref, br_ref, k_ref, local_ref,
-    before_ref, image_ref, f_ref, light_ref, now_far, next_ref, muted_ref, kept_ref, sem,
+    before_ref, image_ref, f_ref, light_ref, now_far, next_far, sums_far,
+    next_ref, muted_ref, kept_ref, sems,
 ):
     nx, ny, nz = pm_ref.shape
-    store = pltpu.make_async_copy(pm_ref, now_far, sem)
+    store = pltpu.make_async_copy(pm_ref, now_far, sems.at[0])
     store.start()
+    for y in range(ny):
+        muted_ref[1, y // 2, y % 2, :, :] = light_ref[:, y, :]
+    store_light = pltpu.make_async_copy(muted_ref.at[1], sums_far.at[:, pl.ds(2, 2)], sems.at[1])
+    store_light.start()
     steps = f_ref.shape[0]
     edges = edge_factors(place_ref, nx)
     second = lax.broadcasted_iota(jnp.int32, (8, 128), 0).astype(F32)
@@ -489,10 +494,14 @@
             kept_ref[i, rows, lanes] = (1.0 - jnp.exp(distance * (-1.0 / (2.0 * MUTE * MUTE)))) * image
 
     each_column(ny, nz, work)
+    store_next = pltpu.make_async_copy(next_ref, next_far, sems.at[2])
+    store_next.start()
     for y in range(ny):
-        muted_ref[y // 2, y % 2, :, :] = kept_ref[:, y, :]
-        muted_ref[y // 2, 2 + y % 2, :, :] = light_ref[:, y, :]
-    store.wait()
+        muted_ref[0, y // 2, y % 2, :, :] = kept_ref[:, y, :]
+    store_image = pltpu.make_async_copy(muted_ref.at[0], sums_far.at[:, pl.ds(0, 2)], sems.at[3])
+    store_image.start()
+    for copy in (store, store_light, store_next, store_image):
+        copy.wait()
 
 
 def update_step(place, halos, current, b1_halos, b1, stiffness, local, before):
@@ -514,9 +523,14 @@
     return pl.pallas_call(
         last_kernel,
         in_specs=[smem] + [vmem] * 12,
-        out_specs=[pl.BlockSpec(memory_space=pltpu.HBM)] + [vmem] * 2,
+        out_specs=[pl.BlockSpec(memory_space=pltpu.HBM)] * 3,
         out_shape=[shape_of(nx, ny, nz)] * 2 + [shape_of(ny // 2, 4, nx, nz)],
-        scratch_shapes=[pltpu.VMEM((nx, ny, nz), F32), pltpu.SemaphoreType.DMA],
+        scratch_shapes=[
+            pltpu.VMEM((nx, ny, nz), F32),
+            pltpu.VMEM((2, ny // 2, 2, nx, nz), F32),
+            pltpu.VMEM((nx, ny, nz), F32),
+            pltpu.SemaphoreType.DMA((4,)),
+        ],
         compiler_params=PARAMS,
         name="last_step",
     )(

time: 123 us -> 123 us (level)
  no operation moved by 1% of the time
where the time goes in v6:
time: 123 us; the launch traced here: 121 us
  Pallas kernels  53.6 us (44%)
  starting transfers between devices  33.9 us (28%)
  blocking collectives  22.8 us (19%)
  waiting for transfers between devices  8.91 us (7%)
    pallas_call x7, Pallas kernels, local_step(): pl.pallas_call(make_local_kernel(moment), in_specs=[vmem] * 3 + wide + [v...  28.9 us
    ppermute x8, starting transfers between devices, exchange(): lax.ppermute(head, 'sub', [((i + 1) % count, i) for i in range(count)])  23.8 us
    all_to_all x1, blocking collectives, local(): sums = lax.all_to_all(sums, 'shot', split_axis=0, concat_axis=0, tiled=True)  22.8 us
    pallas_call x7, Pallas kernels, update_step(): pl.pallas_call(update_kernel, in_specs=[pl.BlockSpec(memory_space=pltpu.S...  10.7 us
    all_to_all x1, starting transfers between devices, local(): got = lax.all_to_all(send, both, split_axis=0, concat_axis=0, tiled=True)  9.94 us
    ppermute x8, waiting for transfers between devices, exchange(): lax.ppermute(tail, 'sub', [(i, (i + 1) % count) for i in range(count)])  5.44 us
    pallas_call x1, Pallas kernels, first_local(): pl.pallas_call(first_local_kernel, in_specs=[far] * 4, out_specs=far, out...  4.81 us
    all_to_all x1, waiting for transfers between devices, local(): got = lax.all_to_all(send, both, split_axis=0, concat_axis=0, tiled=True)  3.44 us
  transfers between devices with their start and end apart: 17, of which 8 were waited for; matrix products, arithmetic and copies ran while one was open for 0% of the time, Pallas kernels for 30%

profile of v6, /device:TPU:0, one launch (start us, length us, event | category | flops | bytes accessed | tf_op | source)
XLA Modules:
  0.0 121.0 jit_solution(17725692615868531918)
XLA Ops:
  0.6 2.9 %prep.1 = (f32[128,128]{1,0:T(8,128)}, f32[11,32,384]{2,1,0:T(8,128)S(1)}, f32[10,32,384]{2,1,0:T(8,128)S(1)}) custom-call(f32[512,256]{1,0:T(8,128)} %refs_0_.1, f32[128,256]{1,0:T(8,128)} %constant.10.clone.refs_1_, s32[1,512]{1,0:T(1,128)} %bitcast.26, s32[1,512]{1,0:T(1,128)} %bitcast.27, f32[16,32,384]{2,1,0:T(8,128)} %bitcast.21, f32[16,32,384]{2,1,0:T(8,128)} %refs_2_.1), custom_call_target="tpu_custom_call" | custom-call | tf_op jit(solution)/shard_map/prep/pallas_call | solution.py:105
  3.6 2.9 %collective-permute-start.1 = (f32[10,32,384]{2,1,0:T(8,128)S(1)}, f32[10,32,384]{2,1,0:T(8,128)S(1)}, u32[]{:S(2)}, u32[]{:S(2)}) collective-permute-start(f32[10,32,384]{2,1,0:T(8,128)S(1)} %get-tuple-element.75), channel_id=1, source_target_pairs={{1,0},{2,1},{3,2},{4,3},{5,4},{6,5},{7,6},{0,7},{9,8},{10,9},{11,1... | collective-permute-start | bytes 1474568 | tf_op jit(solution)/shard_map/ppermute | solution.py:566
  6.5 9.9 %all-to-all-start = ((f32[128,1,128]{2,1,0:T(1,128)}), f32[128,1,128]{2,1,0:T(1,128)S(1)}, u32[]{:S(2)}, u32[]{:S(2)}) async-start(f32[128,1,128]{2,1,0:T(1,128)} %bitcast.4), calls=%async_computation | async-start | bytes 131072 | tf_op jit(solution)/shard_map/all_to_all | solution.py:593
  16.5 4.8 %first_local.1.local_far = f32[16,32,384]{2,1,0:T(8,128)S(1)} custom-call(f32[16,32,384]{2,1,0:T(8,128)} %bitcast.22, f32[16,32,384]{2,1,0:T(8,128)} %refs_1_.2, f32[16,32,384]{2,1,0:T(8,128)} %refs_3_.1, f32[16,32,384]{2,1,0:T(8,128)} %refs_4_.1), custom_call_target="tpu_custom_call" | custom-call | tf_op jit(solution)/shard_map/first_local/pallas_call | solution.py:282
  22.3 3.4 %all-to-all-done = f32[128,1,128]{2,1,0:T(1,128)S(1)} async-done(((f32[128,1,128]{2,1,0:T(1,128)}), f32[128,1,128]{2,1,0:T(1,128)S(1)}, u32[]{:S(2)}, u32[]{:S(2)}) %all-to-all-start) | async-done | bytes 65568 | tf_op jit(solution)/shard_map/all_to_all | solution.py:593
  25.7 2.7 %first_inject.1 = (f32[16,32,384]{2,1,0:T(8,128)S(1)}, f32[128,128]{1,0:T(8,128)S(1)}, bf16[4,384,384]{2,1,0:T(8,128)(2,1)S(1)}, f32[16,32,384]{2,1,0:T(8,128)S(...) custom-call(f32[128,128]{1,0:T(8,128)S(1)} %bitcast.13, ...), custom_call_target="tpu_custom_call" | custom-call | tf_op jit(solution)/shard_map/first_inject/pallas_call | solution.py:319
  29.9 2.9 %collective-permute-start.3 = (f32[7,32,384]{2,1,0:T(8,128)S(1)}, f32[7,32,384]{2,1,0:T(8,128)S(1)}, u32[]{:S(2)}, u32[]{:S(2)}) collective-permute-start(f32[7,32,384]{2,1,0:T(8,128)S(1)} %get-tuple-element.82), channel_id=1, source_target_pairs={{1,0},{2,1},{3,2},{4,3},{5,4},{6,5},{7,6},{0,7},{9,8},{10,9},{11,1... | collective-permute-start | bytes 1032200 | tf_op jit(solution)/shard_map/ppermute | solution.py:566
  32.9 4.2 %local_step.7 = (f32[16,32,384]{2,1,0:T(8,128)S(1)}, f32[16,32,384]{2,1,0:T(8,128)S(1)}, f32[16,32,384]{2,1,0:T(8,128)S(1)}, f32[16,32,384]{2,1,0:T(8,128)S(1)},...) custom-call(f32[16,32,384]{2,1,0:T(8,128)S(1)} %get-tuple-element.81.refs_0_.pm_ref.before_ref, ...), custom_call_target="tpu_custom_call" | custom-call | tf_op jit(solution)/shard_map/local_step/pallas_call | solution.py:382
  39.3 3.0 %collective-permute-start.5 = (f32[7,32,384]{2,1,0:T(8,128)S(1)}, f32[7,32,384]{2,1,0:T(8,128)S(1)}, u32[]{:S(2)}, u32[]{:S(2)}) collective-permute-start(f32[7,32,384]{2,1,0:T(8,128)S(1)} %get-tuple-element.89), channel_id=1, source_target_pairs={{1,0},{2,1},{3,2},{4,3},{5,4},{6,5},{7,6},{0,7},{9,8},{10,9},{11,1... | collective-permute-start | bytes 1032200 | tf_op jit(solution)/shard_map/ppermute | solution.py:566
  42.3 4.1 %local_step.8 = (f32[16,32,384]{2,1,0:T(8,128)S(1)}, f32[16,32,384]{2,1,0:T(8,128)S(1)}, f32[16,32,384]{2,1,0:T(8,128)S(1)}) custom-call(f32[16,32,384]{2,1,0:T(8,128)S(1)} %get-tuple-element.88.refs_0_.pm_ref.before_ref, bf16[4,384,384]{2,1,0:T(8,128)(2,1)S(1)} %get-tuple-element.83.refs_1_, f32[16,32,384]{2,1,0:T(8,128)S(1)} %get-tuple-element.77.k_ref.refs_2_, ...), custom_call_target="tpu_custom_call" | custom-call | tf_op jit(solution)/shard_map/local_step/pallas_call | solution.py:382
  47.2 1.7 %update_step.9 = (f32[16,32,384]{2,1,0:T(8,128)S(1)}, f32[16,32,384]{2,1,0:T(8,128)S(1)}, f32[7,32,384]{2,1,0:T(8,128)S(1)}, f32[7,32,384]{2,1,0:T(8,128)S(1)}) custom-call(s32[5]{0:T(128)S(1)} %pad_add_fusion.place_ref, f32[7,32,384]{2,1,0:T(8,128)S(1)} %collective-permute-done.4.pl_ref, f32[16,32,384]{2,1,0:T(8,128)S(1)} %get-tuple-element.88.refs_0_.pm_ref.before_ref, ...), custom_call_target="tpu_custom_call" | custom-call | tf_op jit(solution)/shard_map/update_step/pallas_call | solution.py:509
  48.9 3.0 %collective-permute-start.7 = (f32[7,32,384]{2,1,0:T(8,128)S(1)}, f32[7,32,384]{2,1,0:T(8,128)S(1)}, u32[]{:S(2)}, u32[]{:S(2)}) collective-permute-start(f32[7,32,384]{2,1,0:T(8,128)S(1)} %get-tuple-element.99), channel_id=1, source_target_pairs={{1,0},{2,1},{3,2},{4,3},{5,4},{6,5},{7,6},{0,7},{9,8},{10,9},{11,1... | collective-permute-start | bytes 1032200 | tf_op jit(solution)/shard_map/ppermute | solution.py:566
  51.9 4.1 %local_step.9 = (f32[16,32,384]{2,1,0:T(8,128)S(1)}, f32[16,32,384]{2,1,0:T(8,128)S(1)}, f32[16,32,384]{2,1,0:T(8,128)S(1)}) custom-call(f32[16,32,384]{2,1,0:T(8,128)S(1)} %get-tuple-element.98.refs_0_.pm_ref.before_ref, bf16[4,384,384]{2,1,0:T(8,128)(2,1)S(1)} %get-tuple-element.83.refs_1_, f32[16,32,384]{2,1,0:T(8,128)S(1)} %get-tuple-element.77.k_ref.refs_2_, ...), custom_call_target="tpu_custom_call" | custom-call | tf_op jit(solution)/shard_map/local_step/pallas_call | solution.py:382
  58.3 3.0 %collective-permute-start.9 = (f32[7,32,384]{2,1,0:T(8,128)S(1)}, f32[7,32,384]{2,1,0:T(8,128)S(1)}, u32[]{:S(2)}, u32[]{:S(2)}) collective-permute-start(f32[7,32,384]{2,1,0:T(8,128)S(1)} %get-tuple-element.106), channel_id=1, source_target_pairs={{1,0},{2,1},{3,2},{4,3},{5,4},{6,5},{7,6},{0,7},{9,8},{10,9},{11,1... | collective-permute-start | bytes 1032200 | tf_op jit(solution)/shard_map/ppermute | solution.py:566
  61.3 4.1 %local_step.10 = (f32[16,32,384]{2,1,0:T(8,128)S(1)}, f32[16,32,384]{2,1,0:T(8,128)S(1)}, f32[16,32,384]{2,1,0:T(8,128)S(1)}) custom-call(f32[16,32,384]{2,1,0:T(8,128)S(1)} %get-tuple-element.105.refs_0_.pm_ref.before_ref, bf16[4,384,384]{2,1,0:T(8,128)(2,1)S(1)} %get-tuple-element.83.refs_1_, f32[16,32,384]{2,1,0:T(8,128)S(1)} %get-tuple-element.77.k_ref.refs_2_, ...), custom_call_target="tpu_custom_call" | custom-call | tf_op jit(solution)/shard_map/local_step/pallas_call | solution.py:382
  67.7 3.0 %collective-permute-start.11 = (f32[7,32,384]{2,1,0:T(8,128)S(1)}, f32[7,32,384]{2,1,0:T(8,128)S(1)}, u32[]{:S(2)}, u32[]{:S(2)}) collective-permute-start(f32[7,32,384]{2,1,0:T(8,128)S(1)} %get-tuple-element.113), channel_id=1, source_target_pairs={{1,0},{2,1},{3,2},{4,3},{5,4},{6,5},{7,6},{0,7},{9,8},{10,9},{11,1... | collective-permute-start | bytes 1032200 | tf_op jit(solution)/shard_map/ppermute | solution.py:566
  70.7 4.1 %local_step.11 = (f32[16,32,384]{2,1,0:T(8,128)S(1)}, f32[16,32,384]{2,1,0:T(8,128)S(1)}, f32[16,32,384]{2,1,0:T(8,128)S(1)}) custom-call(f32[16,32,384]{2,1,0:T(8,128)S(1)} %get-tuple-element.112.refs_0_.pm_ref.before_ref, bf16[4,384,384]{2,1,0:T(8,128)(2,1)S(1)} %get-tuple-element.83.refs_1_, f32[16,32,384]{2,1,0:T(8,128)S(1)} %get-tuple-element.77.k_ref.refs_2_, ...), custom_call_target="tpu_custom_call" | custom-call | tf_op jit(solution)/shard_map/local_step/pallas_call | solution.py:382
  77.1 3.0 %collective-permute-start.13 = (f32[7,32,384]{2,1,0:T(8,128)S(1)}, f32[7,32,384]{2,1,0:T(8,128)S(1)}, u32[]{:S(2)}, u32[]{:S(2)}) collective-permute-start(f32[7,32,384]{2,1,0:T(8,128)S(1)} %get-tuple-element.120), channel_id=1, source_target_pairs={{1,0},{2,1},{3,2},{4,3},{5,4},{6,5},{7,6},{0,7},{9,8},{10,9},{11,1... | collective-permute-start | bytes 1032200 | tf_op jit(solution)/shard_map/ppermute | solution.py:566
  80.1 4.1 %local_step.12 = (f32[16,32,384]{2,1,0:T(8,128)S(1)}, f32[16,32,384]{2,1,0:T(8,128)S(1)}, f32[16,32,384]{2,1,0:T(8,128)S(1)}) custom-call(f32[16,32,384]{2,1,0:T(8,128)S(1)} %get-tuple-element.119.refs_0_.pm_ref.before_ref, bf16[4,384,384]{2,1,0:T(8,128)(2,1)S(1)} %get-tuple-element.83.refs_1_, f32[16,32,384]{2,1,0:T(8,128)S(1)} %get-tuple-element.77.k_ref.refs_2_, ...), custom_call_target="tpu_custom_call" | custom-call | tf_op jit(solution)/shard_map/local_step/pallas_call | solution.py:382
  85.0 1.7 %update_step.13 = (f32[16,32,384]{2,1,0:T(8,128)S(1)}, f32[16,32,384]{2,1,0:T(8,128)S(1)}, f32[7,32,384]{2,1,0:T(8,128)S(1)}, f32[7,32,384]{2,1,0:T(8,128)S(1)}) custom-call(s32[5]{0:T(128)S(1)} %pad_add_fusion.place_ref, f32[7,32,384]{2,1,0:T(8,128)S(1)} %collective-permute-done.12.pl_ref, f32[16,32,384]{2,1,0:T(8,128)S(1)} %get-tuple-element.119.refs_0_.pm_ref.before_ref, ...), custom_call_target="tpu_custom_call" | custom-call | tf_op jit(solution)/shard_map/update_step/pallas_call | solution.py:509
  86.7 3.0 %collective-permute-start.15 = (f32[7,32,384]{2,1,0:T(8,128)S(1)}, f32[7,32,384]{2,1,0:T(8,128)S(1)}, u32[]{:S(2)}, u32[]{:S(2)}) collective-permute-start(f32[7,32,384]{2,1,0:T(8,128)S(1)} %get-tuple-element.127), channel_id=1, source_target_pairs={{1,0},{2,1},{3,2},{4,3},{5,4},{6,5},{7,6},{0,7},{9,8},{10,9},{11,1... | collective-permute-start | bytes 1032200 | tf_op jit(solution)/shard_map/ppermute | solution.py:566
  89.7 4.1 %local_step.13 = (f32[16,32,384]{2,1,0:T(8,128)S(1)}, f32[16,32,384]{2,1,0:T(8,128)S(1)}, f32[16,32,384]{2,1,0:T(8,128)S(1)}) custom-call(f32[16,32,384]{2,1,0:T(8,128)S(1)} %get-tuple-element.126.refs_0_.pm_ref, bf16[4,384,384]{2,1,0:T(8,128)(2,1)S(1)} %get-tuple-element.83.refs_1_, f32[16,32,384]{2,1,0:T(8,128)S(1)} %get-tuple-element.77.k_ref.refs_2_, ...), custom_call_target="tpu_custom_call" | custom-call | tf_op jit(solution)/shard_map/local_step/pallas_call | solution.py:382
  94.6 2.9 %last_step.1 = (f32[16,32,384]{2,1,0:T(8,128)}, f32[16,32,384]{2,1,0:T(8,128)}, f32[16,4,16,384]{3,2,1,0:T(8,128)S(1)}) custom-call(s32[5]{0:T(128)S(1)} %pad_add_fusion.place_ref, f32[7,32,384]{2,1,0:T(8,128)S(1)} %collective-permute-done.14.pl_ref, f32[16,32,384]{2,1,0:T(8,128)S(1)} %get-tuple-element.126.refs_0_.pm_ref, ...), custom_call_target="tpu_custom_call" | custom-call | tf_op jit(solution)/shard_map/last_step/pallas_call | solution.py:523
  97.5 22.8 %all_to_all.17.refs_0_ = f32[16,4,16,384]{3,2,1,0:T(8,128)S(1)} all-to-all(f32[16,4,16,384]{3,2,1,0:T(8,128)S(1)} %get-tuple-element.134), channel_id=1, replica_groups=mesh['shot'=16,'sub'=8] {'shot'}, dimensions={0} | all-to-all | bytes 3145728 | tf_op jit(solution)/shard_map/all_to_all | solution.py:618
  (35 shorter events, 14.6 us)
Async XLA Ops:
  3.6 24.9 %collective-permute-start = (f32[11,32,384]{2,1,0:T(8,128)S(1)}, f32[11,32,384]{2,1,0:T(8,128)S(1)}, u32[]{:S(2)}, u32[]{:S(2)}) collective-permute-start(f32[11,32,384]{2,1,0:T(8,128)S(1)} %get-tuple-element.72), channel_id=1, source_target_pairs={{0,1},{1,2},{2,3},{3,4},{4,5},{5,6},{6,7},{7,0},{8,9},{9,10},{10,1... | collective-permute-start | bytes 1622024 | tf_op jit(solution)/shard_map/ppermute | solution.py:565
  3.6 24.8 %collective-permute-start.1 = (f32[10,32,384]{2,1,0:T(8,128)S(1)}, f32[10,32,384]{2,1,0:T(8,128)S(1)}, u32[]{:S(2)}, u32[]{:S(2)}) collective-permute-start(f32[10,32,384]{2,1,0:T(8,128)S(1)} %get-tuple-element.75), channel_id=1, source_target_pairs={{1,0},{2,1},{3,2},{4,3},{5,4},{6,5},{7,6},{0,7},{9,8},{10,9},{11,1... | collective-permute-start | bytes 1474568 | tf_op jit(solution)/shard_map/ppermute | solution.py:566
  6.5 19.2 %all-to-all-start = ((f32[128,1,128]{2,1,0:T(1,128)}), f32[128,1,128]{2,1,0:T(1,128)S(1)}, u32[]{:S(2)}, u32[]{:S(2)}) async-start(f32[128,1,128]{2,1,0:T(1,128)} %bitcast.4), calls=%async_computation | async-start | bytes 131072 | tf_op jit(solution)/shard_map/all_to_all | solution.py:593
  16.5 5.7 %copy-start.1 = (s32[1,3]{1,0:T(1,128)S(1)}, s32[1,3]{1,0:T(1,128)}, u32[]{:S(2)}) copy-start(s32[1,3]{1,0:T(1,128)} %param.22) | copy-start | bytes 40
  21.3 0.9 copy-start
  29.9 7.9 %collective-permute-start.2 = (f32[7,32,384]{2,1,0:T(8,128)S(1)}, f32[7,32,384]{2,1,0:T(8,128)S(1)}, u32[]{:S(2)}, u32[]{:S(2)}) collective-permute-start(f32[7,32,384]{2,1,0:T(8,128)S(1)} %get-tuple-element.80), channel_id=1, source_target_pairs={{0,1},{1,2},{2,3},{3,4},{4,5},{5,6},{6,7},{7,0},{8,9},{9,10},{10,1... | collective-permute-start | bytes 1032200 | tf_op jit(solution)/shard_map/ppermute | solution.py:565
  29.9 7.9 %collective-permute-start.3 = (f32[7,32,384]{2,1,0:T(8,128)S(1)}, f32[7,32,384]{2,1,0:T(8,128)S(1)}, u32[]{:S(2)}, u32[]{:S(2)}) collective-permute-start(f32[7,32,384]{2,1,0:T(8,128)S(1)} %get-tuple-element.82), channel_id=1, source_target_pairs={{1,0},{2,1},{3,2},{4,3},{5,4},{6,5},{7,6},{0,7},{9,8},{10,9},{11,1... | collective-permute-start | bytes 1032200 | tf_op jit(solution)/shard_map/ppermute | solution.py:566
  39.3 7.9 %collective-permute-start.4 = (f32[7,32,384]{2,1,0:T(8,128)S(1)}, f32[7,32,384]{2,1,0:T(8,128)S(1)}, u32[]{:S(2)}, u32[]{:S(2)}) collective-permute-start(f32[7,32,384]{2,1,0:T(8,128)S(1)} %get-tuple-element.87), channel_id=1, source_target_pairs={{0,1},{1,2},{2,3},{3,4},{4,5},{5,6},{6,7},{7,0},{8,9},{9,10},{10,1... | collective-permute-start | bytes 1032200 | tf_op jit(solution)/shard_map/ppermute | solution.py:565
  39.3 7.9 %collective-permute-start.5 = (f32[7,32,384]{2,1,0:T(8,128)S(1)}, f32[7,32,384]{2,1,0:T(8,128)S(1)}, u32[]{:S(2)}, u32[]{:S(2)}) collective-permute-start(f32[7,32,384]{2,1,0:T(8,128)S(1)} %get-tuple-element.89), channel_id=1, source_target_pairs={{1,0},{2,1},{3,2},{4,3},{5,4},{6,5},{7,6},{0,7},{9,8},{10,9},{11,1... | collective-permute-start | bytes 1032200 | tf_op jit(solution)/shard_map/ppermute | solution.py:566
  48.9 7.9 %collective-permute-start.6 = (f32[7,32,384]{2,1,0:T(8,128)S(1)}, f32[7,32,384]{2,1,0:T(8,128)S(1)}, u32[]{:S(2)}, u32[]{:S(2)}) collective-permute-start(f32[7,32,384]{2,1,0:T(8,128)S(1)} %get-tuple-element.97), channel_id=1, source_target_pairs={{0,1},{1,2},{2,3},{3,4},{4,5},{5,6},{6,7},{7,0},{8,9},{9,10},{10,1... | collective-permute-start | bytes 1032200 | tf_op jit(solution)/shard_map/ppermute | solution.py:565
  48.9 7.9 %collective-permute-start.7 = (f32[7,32,384]{2,1,0:T(8,128)S(1)}, f32[7,32,384]{2,1,0:T(8,128)S(1)}, u32[]{:S(2)}, u32[]{:S(2)}) collective-permute-start(f32[7,32,384]{2,1,0:T(8,128)S(1)} %get-tuple-element.99), channel_id=1, source_target_pairs={{1,0},{2,1},{3,2},{4,3},{5,4},{6,5},{7,6},{0,7},{9,8},{10,9},{11,1... | collective-permute-start | bytes 1032200 | tf_op jit(solution)/shard_map/ppermute | solution.py:566
  58.3 7.9 %collective-permute-start.8 = (f32[7,32,384]{2,1,0:T(8,128)S(1)}, f32[7,32,384]{2,1,0:T(8,128)S(1)}, u32[]{:S(2)}, u32[]{:S(2)}) collective-permute-start(f32[7,32,384]{2,1,0:T(8,128)S(1)} %get-tuple-element.104), channel_id=1, source_target_pairs={{0,1},{1,2},{2,3},{3,4},{4,5},{5,6},{6,7},{7,0},{8,9},{9,10},{10,1... | collective-permute-start | bytes 1032200 | tf_op jit(solution)/shard_map/ppermute | solution.py:565
  58.3 7.9 %collective-permute-start.9 = (f32[7,32,384]{2,1,0:T(8,128)S(1)}, f32[7,32,384]{2,1,0:T(8,128)S(1)}, u32[]{:S(2)}, u32[]{:S(2)}) collective-permute-start(f32[7,32,384]{2,1,0:T(8,128)S(1)} %get-tuple-element.106), channel_id=1, source_target_pairs={{1,0},{2,1},{3,2},{4,3},{5,4},{6,5},{7,6},{0,7},{9,8},{10,9},{11,1... | collective-permute-start | bytes 1032200 | tf_op jit(solution)/shard_map/ppermute | solution.py:566
  67.7 7.9 %collective-permute-start.10 = (f32[7,32,384]{2,1,0:T(8,128)S(1)}, f32[7,32,384]{2,1,0:T(8,128)S(1)}, u32[]{:S(2)}, u32[]{:S(2)}) collective-permute-start(f32[7,32,384]{2,1,0:T(8,128)S(1)} %get-tuple-element.111), channel_id=1, source_target_pairs={{0,1},{1,2},{2,3},{3,4},{4,5},{5,6},{6,7},{7,0},{8,9},{9,10},{10,1... | collective-permute-start | bytes 1032200 | tf_op jit(solution)/shard_map/ppermute | solution.py:565
  67.7 7.9 %collective-permute-start.11 = (f32[7,32,384]{2,1,0:T(8,128)S(1)}, f32[7,32,384]{2,1,0:T(8,128)S(1)}, u32[]{:S(2)}, u32[]{:S(2)}) collective-permute-start(f32[7,32,384]{2,1,0:T(8,128)S(1)} %get-tuple-element.113), channel_id=1, source_target_pairs={{1,0},{2,1},{3,2},{4,3},{5,4},{6,5},{7,6},{0,7},{9,8},{10,9},{11,1... | collective-permute-start | bytes 1032200 | tf_op jit(solution)/shard_map/ppermute | solution.py:566
  77.1 7.9 %collective-permute-start.12 = (f32[7,32,384]{2,1,0:T(8,128)S(1)}, f32[7,32,384]{2,1,0:T(8,128)S(1)}, u32[]{:S(2)}, u32[]{:S(2)}) collective-permute-start(f32[7,32,384]{2,1,0:T(8,128)S(1)} %get-tuple-element.118), channel_id=1, source_target_pairs={{0,1},{1,2},{2,3},{3,4},{4,5},{5,6},{6,7},{7,0},{8,9},{9,10},{10,1... | collective-permute-start | bytes 1032200 | tf_op jit(solution)/shard_map/ppermute | solution.py:565
  77.1 7.9 %collective-permute-start.13 = (f32[7,32,384]{2,1,0:T(8,128)S(1)}, f32[7,32,384]{2,1,0:T(8,128)S(1)}, u32[]{:S(2)}, u32[]{:S(2)}) collective-permute-start(f32[7,32,384]{2,1,0:T(8,128)S(1)} %get-tuple-element.120), channel_id=1, source_target_pairs={{1,0},{2,1},{3,2},{4,3},{5,4},{6,5},{7,6},{0,7},{9,8},{10,9},{11,1... | collective-permute-start | bytes 1032200 | tf_op jit(solution)/shard_map/ppermute | solution.py:566
  86.7 7.9 %collective-permute-start.14 = (f32[7,32,384]{2,1,0:T(8,128)S(1)}, f32[7,32,384]{2,1,0:T(8,128)S(1)}, u32[]{:S(2)}, u32[]{:S(2)}) collective-permute-start(f32[7,32,384]{2,1,0:T(8,128)S(1)} %get-tuple-element.125), channel_id=1, source_target_pairs={{0,1},{1,2},{2,3},{3,4},{4,5},{5,6},{6,7},{7,0},{8,9},{9,10},{10,1... | collective-permute-start | bytes 1032200 | tf_op jit(solution)/shard_map/ppermute | solution.py:565
  86.7 7.9 %collective-permute-start.15 = (f32[7,32,384]{2,1,0:T(8,128)S(1)}, f32[7,32,384]{2,1,0:T(8,128)S(1)}, u32[]{:S(2)}, u32[]{:S(2)}) collective-permute-start(f32[7,32,384]{2,1,0:T(8,128)S(1)} %get-tuple-element.127), channel_id=1, source_target_pairs={{1,0},{2,1},{3,2},{4,3},{5,4},{6,5},{7,6},{0,7},{9,8},{10,9},{11,1... | collective-permute-start | bytes 1032200 | tf_op jit(solution)/shard_map/ppermute | solution.py:566
